TPU v7x, 32 devices: a whole 2x2x4 slice. The times are simulated.
32 devices in a mesh: sample: 2 (over y), wire: 4 (over z), xsec: 2 (over x), cols: 2 (over core).
Axes of the slice: x: 2, y: 2, z: 4, core: 2. Of those that a mesh axis runs over, the one named last changes fastest.
Arguments:
- blocks: bfloat16 [32, 2, 64, 1728], P(('sample', 'wire'), 'xsec'), parts along dimension 0, may hold values from -0.109375 to 0.109375
- pattern: int32 [32, 2, 27], P(('sample', 'wire'), 'xsec'), parts along dimension 0, may hold values 0 or 1
- current: bfloat16 [32, 2, 64, 2, 512], P(('sample', 'wire'), 'xsec', None, None, 'cols'), parts along dimension 0, may hold values from -6 to 6
- previous: bfloat16 [32, 2, 64, 2, 512], P(('sample', 'wire'), 'xsec', None, None, 'cols'), parts along dimension 0, may hold values from -6 to 6
- accum: float32 [32, 2, 64, 2, 512], P(('sample', 'wire'), 'xsec', None, None, 'cols'), parts along dimension 0, may hold values from -6 to 6
- coefs: float32 [4], replicated, may hold values from 0.3 to 1
- sketch: bfloat16 [32, 2, 64, 512], P(('sample', 'wire'), 'xsec'), parts along dimension 0, may hold values from -6 to 6
- signs: int32 [32, 2, 64, 512], P(('sample', 'wire'), 'xsec', None, 'cols'), parts along dimension 0, may hold values from 0 to 1
Outputs:
- newest: bfloat16 [32, 2, 64, 2, 512], P(('sample', 'wire'), 'xsec', None, None, 'cols'), parts along dimension 0
- before: bfloat16 [32, 2, 64, 2, 512], P(('sample', 'wire'), 'xsec', None, None, 'cols'), parts along dimension 0
- summed: float32 [32, 2, 64, 2, 512], P(('sample', 'wire'), 'xsec', None, None, 'cols'), parts along dimension 0
- gram: float32 [1024, 512], P(('sample', 'wire', 'xsec'), 'cols'), parts along dimension 0
- quadratic: float32 [1024], P(('sample', 'cols')), parts along dimension 0
There are 2 independent parts, one for each index of `sample`. A program takes and returns all parts, laid end to end along the dimension named above; an argument that names none is the same for every part. Nothing has to cross between parts.
All inputs are finite; a program needn't handle non-finite values. No bound on the sum of `pattern` on one device may be relied on, other than what follows from the above.
Results may differ from a plain program's by a relative error of at most 0.0065.
Values may be sent and summed in bfloat16 or wider, within the bound.
No kernel may reach another device: no remote copies, remote signals or barrier semaphores. Data moves between devices by JAX's collectives and lax.ppermute only.
A program may use at most 64 MiB of HBM per device.

v0:
```python
import jax
import jax.numpy as jnp
from jax import lax
from jax.sharding import PartitionSpec as P

REACH = 4
STEPS = 4


def padded(x, sides, width, wrap):
    for axis, dim in sides:
        size, length = (lax.axis_size(axis), x.shape[dim])
        up = [(i, (i + 1) % size) for i in range(size if wrap else size - 1)]
        down = [(j, i) for i, j in up]
        last = lax.slice_in_dim(x, length - width, length, axis=dim)
        initial = lax.slice_in_dim(x, 0, width, axis=dim)
        before = lax.ppermute(last, axis, up)
        after = lax.ppermute(initial, axis, down)
        x = jnp.concatenate([before, x, after], axis=dim)
    return x


def apply_operator(field, masked):
    cells, tiles, orbs, halves, local_cols = field.shape
    reach = REACH
    lengthened = padded(field, (("wire", 0),), reach, True)
    extended = padded(lengthened, (("xsec", 1),), 1, False)
    flat_ext = extended.reshape(cells + 2 * reach, tiles + 2, orbs, halves * local_cols)
    total = jnp.zeros((cells, tiles, orbs, halves * local_cols), jnp.float32)
    for shift_d in range(2 * reach + 1):
        for shift_e in range(3):
            column = shift_d * 3 + shift_e
            piece = flat_ext[shift_d : shift_d + cells, shift_e : shift_e + tiles]
            part = masked[:, :, :, column * orbs : (column + 1) * orbs]
            total = total + jnp.einsum(
                "ctik,ctkn->ctin", part, piece, preferred_element_type=jnp.float32
            )
    return total.reshape(cells, tiles, orbs, halves, local_cols)


def body(blocks, pattern, current, previous, accum, coefs, sketch, signs):
    cells, tiles, orbs, wide = blocks.shape
    count = wide // orbs
    masked = (
        blocks.reshape(cells, tiles, orbs, count, orbs)
        * pattern.astype(jnp.bfloat16)[:, :, None, :, None]
    ).reshape(cells, tiles, orbs, wide)
    for step in range(STEPS):
        image = apply_operator(current, masked)
        nxt = (2.0 * image - previous.astype(jnp.float32)).astype(jnp.bfloat16)
        accum = accum + coefs[step] * nxt.astype(jnp.float32)
        previous = current
        current = nxt
    cells, tiles, orbs, halves, local_cols = accum.shape
    all_rows = cells * lax.axis_size("wire") * tiles * lax.axis_size("xsec") * orbs
    scale = jnp.float32(1.0) / jnp.sqrt(jnp.float32(all_rows))
    sketched = accum[:, :, :, 0, :].astype(jnp.bfloat16).reshape(cells * tiles * orbs, local_cols)
    omega = sketch.reshape(cells * tiles * orbs, sketch.shape[3])
    partial_gram = lax.dot_general(
        omega, sketched, (((0,), (0,)), ((), ())), preferred_element_type=jnp.float32
    )
    gram = lax.psum_scatter(partial_gram, ("wire", "xsec"), scatter_dimension=0, tiled=True) * scale
    plus_minus = (2 * signs - 1).astype(jnp.float32)
    local_quad = jnp.sum(plus_minus * accum[:, :, :, 1, :], axis=(0, 1, 2))
    quadratic = lax.psum(local_quad, ("wire", "xsec")) * scale
    return (current, previous, accum, gram, quadratic)


def solution(mesh):
    return jax.shard_map(
        body,
        mesh=mesh,
        in_specs=(
            P(("sample", "wire"), "xsec", None, None),
            P(("sample", "wire"), "xsec", None),
            P(("sample", "wire"), "xsec", None, None, "cols"),
            P(("sample", "wire"), "xsec", None, None, "cols"),
            P(("sample", "wire"), "xsec", None, None, "cols"),
            P(),
            P(("sample", "wire"), "xsec", None, None),
            P(("sample", "wire"), "xsec", None, "cols"),
        ),
        out_specs=(
            P(("sample", "wire"), "xsec", None, None, "cols"),
            P(("sample", "wire"), "xsec", None, None, "cols"),
            P(("sample", "wire"), "xsec", None, None, "cols"),
            P(("sample", "wire", "xsec"), "cols"),
            P(("sample", "cols")),
        ),
        check_vma=False,
    )
```

profile of v0, /device:TPU:0, one launch (start us, length us, event | category | flops | bytes accessed | tf_op | source)
XLA Modules:
  0.0 268.2 jit_solution(3019702308393329979)
XLA Ops:
  7.2 3.1 %collective-permute-start = (bf16[4,1,64,2,256]{4,3,2,1,0:T(2,128)(2,1)}, bf16[4,1,64,2,256]{4,3,2,1,0:T(2,128)(2,1)S(1)}, u32[]{:S(2)}, u32[]{:S(2)}) collective-permute-start(bf16[4,1,64,2,256]{4,3,2,1,0:T(2,128)(2,1)} %param.10), channel_id=1, source_target_pairs={{0,4},{4,8},{8,12},{12,0},{1,5},{5,9},{9,13},{13,1},{2,6},{6,10},{... | collective-permute-start | bytes 786440 | tf_op jit(solution)/shard_map/ppermute | solution.py:17
  12.4 7.3 %collective-permute-done = bf16[4,1,64,2,256]{4,3,2,1,0:T(2,128)(2,1)S(1)} collective-permute-done((bf16[4,1,64,2,256]{4,3,2,1,0:T(2,128)(2,1)}, bf16[4,1,64,2,256]{4,3,2,1,0:T(2,128)(2,1)S(1)}, u32[]{:S(2)}, u32[]{:S(2)}) %collective-permute-start) | collective-permute-done | bytes 262176 | tf_op jit(solution)/shard_map/ppermute | solution.py:17
  21.1 2.8 %collective-permute-done.1 = bf16[4,1,64,2,256]{4,3,2,1,0:T(2,128)(2,1)S(1)} collective-permute-done((bf16[4,1,64,2,256]{4,3,2,1,0:T(2,128)(2,1)}, bf16[4,1,64,2,256]{4,3,2,1,0:T(2,128)(2,1)S(1)}, u32[]{:S(2)}, u32[]{:S(2)}) %collective-permute-start.1) | collective-permute-done | bytes 262176 | tf_op jit(solution)/shard_map/ppermute | solution.py:18
  24.1 3.4 %collective-permute-start.2 = (bf16[12,1,64,2,256]{4,3,2,1,0:T(2,128)(2,1)S(1)}, bf16[12,1,64,2,256]{4,3,2,1,0:T(2,128)(2,1)S(1)}, u32[]{:S(2)}, u32[]{:S(2)}) collective-permute-start(bf16[12,1,64,2,256]{4,3,2,1,0:T(2,128)(2,1)S(1)} %constant_dynamic-update-slice_fusion), channel_id=1, source_target_pairs={{0,2},{1,3},{4,6},{5,7},{8,10},{9,11},{12,14},{13,15},{16,18},{17,... | collective-permute-start | bytes 2359304 | tf_op jit(solution)/shard_map/ppermute | solution.py:17
  31.0 12.9 %collective-permute-done.2 = bf16[12,1,64,2,256]{4,3,2,1,0:T(2,128)(2,1)S(1)} collective-permute-done((bf16[12,1,64,2,256]{4,3,2,1,0:T(2,128)(2,1)S(1)}, bf16[12,1,64,2,256]{4,3,2,1,0:T(2,128)(2,1)S(1)}, u32[]{:S(2)}, u32[]{:S(2)}) %collective-permute-start.2) | collective-permute-done | bytes 786464 | tf_op jit(solution)/shard_map/ppermute | solution.py:17
  43.9 4.2 %collective-permute-done.3 = bf16[12,1,64,2,256]{4,3,2,1,0:T(2,128)(2,1)S(1)} collective-permute-done((bf16[12,1,64,2,256]{4,3,2,1,0:T(2,128)(2,1)S(1)}, bf16[12,1,64,2,256]{4,3,2,1,0:T(2,128)(2,1)S(1)}, u32[]{:S(2)}, u32[]{:S(2)}) %collective-permute-start.3) | collective-permute-done | bytes 786464 | tf_op jit(solution)/shard_map/ppermute | solution.py:18
  48.1 4.6 %pad_maximum_fusion = bf16[12,3,64,2,256]{4,3,2,1,0:T(2,128)(2,1)} fusion(bf16[12,1,64,2,256]{4,3,2,1,0:T(2,128)(2,1)S(1)} %collective-permute-done.3, bf16[12,1,64,2,256]{4,3,2,1,0:T(2,128)(2,1)S(1)} %constant_dynamic-update-slice_fusion, bf16[12,1,64,2,256]{4,3,2,1,0:T(2,128)(2,1)S(1)} %collective-permute-done.2), kind=kLoop, calls=%fused_computation | loop fusion | flops 2359296 | bytes 4718592 | tf_op jit(solution)/shard_map/concatenate | solution.py:19
  52.7 5.3 %reshape.948 = bf16[12,3,64,512]{3,2,1,0:T(8,128)(2,1)S(1)} reshape(bf16[12,3,64,2,256]{4,3,2,1,0:T(2,128)(2,1)} %pad_maximum_fusion) | data formatting | bytes 4718592 | tf_op jit(solution)/shard_map/reshape | solution.py:28
  71.6 7.2 %collective-permute-done.4 = bf16[4,1,64,2,256]{4,2,0,3,1:T(8,128)(2,1)S(1)} collective-permute-done((bf16[4,1,64,2,256]{4,2,0,3,1:T(8,128)(2,1)S(1)}, bf16[4,1,64,2,256]{4,2,0,3,1:T(8,128)(2,1)S(1)}, u32[]{:S(2)}, u32[]{:S(2)}) %collective-permute-start.4) | collective-permute-done | bytes 262176 | tf_op jit(solution)/shard_map/ppermute | solution.py:17
  78.8 3.0 %collective-permute-done.5 = bf16[4,1,64,2,256]{4,2,0,3,1:T(8,128)(2,1)S(1)} collective-permute-done((bf16[4,1,64,2,256]{4,2,0,3,1:T(8,128)(2,1)S(1)}, bf16[4,1,64,2,256]{4,2,0,3,1:T(8,128)(2,1)S(1)}, u32[]{:S(2)}, u32[]{:S(2)}) %collective-permute-start.5) | collective-permute-done | bytes 262176 | tf_op jit(solution)/shard_map/ppermute | solution.py:18
  84.7 15.7 %collective-permute-done.6 = bf16[12,1,64,2,256]{4,2,0,3,1:T(8,128)(2,1)S(1)} collective-permute-done((bf16[12,1,64,2,256]{4,2,0,3,1:T(8,128)(2,1)S(1)}, bf16[12,1,64,2,256]{4,2,0,3,1:T(8,128)(2,1)S(1)}, u32[]{:S(2)}, u32[]{:S(2)}) %collective-permute-start.6) | collective-permute-done | bytes 786464 | tf_op jit(solution)/shard_map/ppermute | solution.py:17
  100.4 4.2 %collective-permute-done.7 = bf16[12,1,64,2,256]{4,2,0,3,1:T(8,128)(2,1)S(1)} collective-permute-done((bf16[12,1,64,2,256]{4,2,0,3,1:T(8,128)(2,1)S(1)}, bf16[12,1,64,2,256]{4,2,0,3,1:T(8,128)(2,1)S(1)}, u32[]{:S(2)}, u32[]{:S(2)}) %collective-permute-start.7) | collective-permute-done | bytes 786464 | tf_op jit(solution)/shard_map/ppermute | solution.py:18
  112.5 3.5 %collective-permute-start.9 = (bf16[4,1,64,2,256]{4,2,0,3,1:T(8,128)(2,1)S(1)}, bf16[4,1,64,2,256]{4,2,0,3,1:T(8,128)(2,1)S(1)}, u32[]{:S(2)}, u32[]{:S(2)}) collective-permute-start(bf16[4,1,64,2,256]{4,2,0,3,1:T(8,128)(2,1)S(1)} %fusion.10), channel_id=1, source_target_pairs={{4,0},{8,4},{12,8},{0,12},{5,1},{9,5},{13,9},{1,13},{6,2},{10,6},{... | collective-permute-start | bytes 786440 | tf_op jit(solution)/shard_map/ppermute | solution.py:18
  116.0 7.2 %collective-permute-done.8 = bf16[4,1,64,2,256]{4,2,0,3,1:T(8,128)(2,1)S(1)} collective-permute-done((bf16[4,1,64,2,256]{4,2,0,3,1:T(8,128)(2,1)S(1)}, bf16[4,1,64,2,256]{4,2,0,3,1:T(8,128)(2,1)S(1)}, u32[]{:S(2)}, u32[]{:S(2)}) %collective-permute-start.8) | collective-permute-done | bytes 262176 | tf_op jit(solution)/shard_map/ppermute | solution.py:17
  123.1 2.1 collective-permute-done.9
  128.1 14.2 %collective-permute-done.10 = bf16[12,1,64,2,256]{4,2,0,3,1:T(8,128)(2,1)S(1)} collective-permute-done((bf16[12,1,64,2,256]{4,2,0,3,1:T(8,128)(2,1)S(1)}, bf16[12,1,64,2,256]{4,2,0,3,1:T(8,128)(2,1)S(1)}, u32[]{:S(2)}, u32[]{:S(2)}) %collective-permute-start.10) | collective-permute-done | bytes 786464 | tf_op jit(solution)/shard_map/ppermute | solution.py:17
  142.3 4.2 %collective-permute-done.11 = bf16[12,1,64,2,256]{4,2,0,3,1:T(8,128)(2,1)S(1)} collective-permute-done((bf16[12,1,64,2,256]{4,2,0,3,1:T(8,128)(2,1)S(1)}, bf16[12,1,64,2,256]{4,2,0,3,1:T(8,128)(2,1)S(1)}, u32[]{:S(2)}, u32[]{:S(2)}) %collective-permute-start.11) | collective-permute-done | bytes 786464 | tf_op jit(solution)/shard_map/ppermute | solution.py:18
  154.1 3.8 %collective-permute-start.13 = (bf16[4,1,64,2,256]{4,2,0,3,1:T(8,128)(2,1)S(1)}, bf16[4,1,64,2,256]{4,2,0,3,1:T(8,128)(2,1)S(1)}, u32[]{:S(2)}, u32[]{:S(2)}) collective-permute-start(bf16[4,1,64,2,256]{4,2,0,3,1:T(8,128)(2,1)S(1)} %fusion.4), channel_id=1, source_target_pairs={{4,0},{8,4},{12,8},{0,12},{5,1},{9,5},{13,9},{1,13},{6,2},{10,6},{... | collective-permute-start | bytes 786440 | tf_op jit(solution)/shard_map/ppermute | solution.py:18
  157.9 6.6 %collective-permute-done.12 = bf16[4,1,64,2,256]{4,2,0,3,1:T(8,128)(2,1)S(1)} collective-permute-done((bf16[4,1,64,2,256]{4,2,0,3,1:T(8,128)(2,1)S(1)}, bf16[4,1,64,2,256]{4,2,0,3,1:T(8,128)(2,1)S(1)}, u32[]{:S(2)}, u32[]{:S(2)}) %collective-permute-start.12) | collective-permute-done | bytes 262176 | tf_op jit(solution)/shard_map/ppermute | solution.py:17
  169.0 12.4 %collective-permute-done.14 = bf16[12,1,64,2,256]{4,2,0,3,1:T(8,128)(2,1)S(1)} collective-permute-done((bf16[12,1,64,2,256]{4,2,0,3,1:T(8,128)(2,1)S(1)}, bf16[12,1,64,2,256]{4,2,0,3,1:T(8,128)(2,1)S(1)}, u32[]{:S(2)}, u32[]{:S(2)}) %collective-permute-start.14) | collective-permute-done | bytes 786464 | tf_op jit(solution)/shard_map/ppermute | solution.py:17
  181.4 4.2 %collective-permute-done.15 = bf16[12,1,64,2,256]{4,2,0,3,1:T(8,128)(2,1)S(1)} collective-permute-done((bf16[12,1,64,2,256]{4,2,0,3,1:T(8,128)(2,1)S(1)}, bf16[12,1,64,2,256]{4,2,0,3,1:T(8,128)(2,1)S(1)}, u32[]{:S(2)}, u32[]{:S(2)}) %collective-permute-start.15) | collective-permute-done | bytes 786464 | tf_op jit(solution)/shard_map/ppermute | solution.py:18
  193.0 2.8 %fusion.8 = (f32[4,1,64,2,256]{4,2,0,3,1:T(8,128)S(1)}, bf16[4,1,64,2,256]{4,2,0,3,1:T(8,128)(2,1)S(1)}) fusion(bf16[4,1,64,2,256]{4,2,0,3,1:T(8,128)(2,1)S(1)} %fusion.11, bf16[4,1,64,2,256]{4,2,0,3,1:T(8,128)(2,1)S(1)} %fusion.10, f32[4,1,64,2,256]{4,3,2,1,0:T(2,128)S(1)} %copy-done.2, bf16[4,1,64,2,256]{4,2,0,3,1:T(8,128)(2,1)S(1)} %fusion.4, ...), kind=kLoop, calls=%fused_computation.125 | loop fusion | flops 1835008 | bytes 2621456 | tf_op jit(solution)/shard_map/add | solution.py:51
  200.3 18.4 %psum.7 = f32[256]{0:T(256)S(1)} all-reduce(f32[256]{0:T(256)S(1)} %fusion.13), channel_id=1, replica_groups=mesh['sample'=2,'wire'=4,'xsec'=2,'cols'=2] {'wire','xsec'}, use_global_device_ids=true, to_apply=%region_2.0 | all-reduce | flops 256 | bytes 2048 | tf_op jit(solution)/shard_map/psum | solution.py:65
  219.2 40.5 %reduce-scatter.4.cloned.1.call-done = f32[64,256]{1,0:T(8,128)} async-done(((f32[512,256]{1,0:T(8,128)}), f32[64,256]{1,0:T(8,128)}) %reduce-scatter.4.cloned.1.call-update) | async-done | bytes 65552
  (168 shorter events, 59.7 us)
Async XLA Ops:
  7.2 188.6 %copy-start = (bf16[4,1,64,512]{3,2,1,0:T(8,128)(2,1)S(1)}, bf16[4,1,64,512]{3,2,1,0:T(8,128)(2,1)}, u32[]{:S(2)}) copy-start(bf16[4,1,64,512]{3,2,1,0:T(8,128)(2,1)} %param.14) | copy-start | bytes 786436
  7.2 252.5 %reduce-scatter.4.cloned.1.call-start = ((), (), s32[]{:S(2)}) async-start(), calls=%async_computation.1 | async-start | bytes 589824
  7.2 12.5 %collective-permute-start = (bf16[4,1,64,2,256]{4,3,2,1,0:T(2,128)(2,1)}, bf16[4,1,64,2,256]{4,3,2,1,0:T(2,128)(2,1)S(1)}, u32[]{:S(2)}, u32[]{:S(2)}) collective-permute-start(bf16[4,1,64,2,256]{4,3,2,1,0:T(2,128)(2,1)} %param.10), channel_id=1, source_target_pairs={{0,4},{4,8},{8,12},{12,0},{1,5},{5,9},{9,13},{13,1},{2,6},{6,10},{... | collective-permute-start | bytes 786440 | tf_op jit(solution)/shard_map/ppermute | solution.py:17
  10.3 13.6 %collective-permute-start.1 = (bf16[4,1,64,2,256]{4,3,2,1,0:T(2,128)(2,1)}, bf16[4,1,64,2,256]{4,3,2,1,0:T(2,128)(2,1)S(1)}, u32[]{:S(2)}, u32[]{:S(2)}) collective-permute-start(bf16[4,1,64,2,256]{4,3,2,1,0:T(2,128)(2,1)} %param.10), channel_id=1, source_target_pairs={{4,0},{8,4},{12,8},{0,12},{5,1},{9,5},{13,9},{1,13},{6,2},{10,6},{... | collective-permute-start | bytes 786440 | tf_op jit(solution)/shard_map/ppermute | solution.py:18
  24.1 19.8 %collective-permute-start.2 = (bf16[12,1,64,2,256]{4,3,2,1,0:T(2,128)(2,1)S(1)}, bf16[12,1,64,2,256]{4,3,2,1,0:T(2,128)(2,1)S(1)}, u32[]{:S(2)}, u32[]{:S(2)}) collective-permute-start(bf16[12,1,64,2,256]{4,3,2,1,0:T(2,128)(2,1)S(1)} %constant_dynamic-update-slice_fusion), channel_id=1, source_target_pairs={{0,2},{1,3},{4,6},{5,7},{8,10},{9,11},{12,14},{13,15},{16,18},{17,... | collective-permute-start | bytes 2359304 | tf_op jit(solution)/shard_map/ppermute | solution.py:17
  27.6 20.5 %collective-permute-start.3 = (bf16[12,1,64,2,256]{4,3,2,1,0:T(2,128)(2,1)S(1)}, bf16[12,1,64,2,256]{4,3,2,1,0:T(2,128)(2,1)S(1)}, u32[]{:S(2)}, u32[]{:S(2)}) collective-permute-start(bf16[12,1,64,2,256]{4,3,2,1,0:T(2,128)(2,1)S(1)} %constant_dynamic-update-slice_fusion), channel_id=1, source_target_pairs={{2,0},{3,1},{6,4},{7,5},{10,8},{11,9},{14,12},{15,13},{18,16},{19,... | collective-permute-start | bytes 2359304 | tf_op jit(solution)/shard_map/ppermute | solution.py:18
  67.7 11.1 %collective-permute-start.4 = (bf16[4,1,64,2,256]{4,2,0,3,1:T(8,128)(2,1)S(1)}, bf16[4,1,64,2,256]{4,2,0,3,1:T(8,128)(2,1)S(1)}, u32[]{:S(2)}, u32[]{:S(2)}) collective-permute-start(bf16[4,1,64,2,256]{4,2,0,3,1:T(8,128)(2,1)S(1)} %fusion.11), channel_id=1, source_target_pairs={{0,4},{4,8},{8,12},{12,0},{1,5},{5,9},{9,13},{13,1},{2,6},{6,10},{... | collective-permute-start | bytes 786440 | tf_op jit(solution)/shard_map/ppermute | solution.py:17
  69.5 12.3 %collective-permute-start.5 = (bf16[4,1,64,2,256]{4,2,0,3,1:T(8,128)(2,1)S(1)}, bf16[4,1,64,2,256]{4,2,0,3,1:T(8,128)(2,1)S(1)}, u32[]{:S(2)}, u32[]{:S(2)}) collective-permute-start(bf16[4,1,64,2,256]{4,2,0,3,1:T(8,128)(2,1)S(1)} %fusion.11), channel_id=1, source_target_pairs={{4,0},{8,4},{12,8},{0,12},{5,1},{9,5},{13,9},{1,13},{6,2},{10,6},{... | collective-permute-start | bytes 786440 | tf_op jit(solution)/shard_map/ppermute | solution.py:18
  81.9 18.5 %collective-permute-start.6 = (bf16[12,1,64,2,256]{4,2,0,3,1:T(8,128)(2,1)S(1)}, bf16[12,1,64,2,256]{4,2,0,3,1:T(8,128)(2,1)S(1)}, u32[]{:S(2)}, u32[]{:S(2)}) collective-permute-start(bf16[12,1,64,2,256]{4,2,0,3,1:T(8,128)(2,1)S(1)} %pad_maximum_fusion.1), channel_id=1, source_target_pairs={{0,2},{1,3},{4,6},{5,7},{8,10},{9,11},{12,14},{13,15},{16,18},{17,... | collective-permute-start | bytes 2359304 | tf_op jit(solution)/shard_map/ppermute | solution.py:17
  83.4 21.2 %collective-permute-start.7 = (bf16[12,1,64,2,256]{4,2,0,3,1:T(8,128)(2,1)S(1)}, bf16[12,1,64,2,256]{4,2,0,3,1:T(8,128)(2,1)S(1)}, u32[]{:S(2)}, u32[]{:S(2)}) collective-permute-start(bf16[12,1,64,2,256]{4,2,0,3,1:T(8,128)(2,1)S(1)} %pad_maximum_fusion.1), channel_id=1, source_target_pairs={{2,0},{3,1},{6,4},{7,5},{10,8},{11,9},{14,12},{15,13},{18,16},{19,... | collective-permute-start | bytes 2359304 | tf_op jit(solution)/shard_map/ppermute | solution.py:18
  111.0 1.1 copy-start.1
  112.1 11.0 %collective-permute-start.8 = (bf16[4,1,64,2,256]{4,2,0,3,1:T(8,128)(2,1)S(1)}, bf16[4,1,64,2,256]{4,2,0,3,1:T(8,128)(2,1)S(1)}, u32[]{:S(2)}, u32[]{:S(2)}) collective-permute-start(bf16[4,1,64,2,256]{4,2,0,3,1:T(8,128)(2,1)S(1)} %fusion.10), channel_id=1, source_target_pairs={{0,4},{4,8},{8,12},{12,0},{1,5},{5,9},{9,13},{13,1},{2,6},{6,10},{... | collective-permute-start | bytes 786440 | tf_op jit(solution)/shard_map/ppermute | solution.py:17
  112.5 12.7 %collective-permute-start.9 = (bf16[4,1,64,2,256]{4,2,0,3,1:T(8,128)(2,1)S(1)}, bf16[4,1,64,2,256]{4,2,0,3,1:T(8,128)(2,1)S(1)}, u32[]{:S(2)}, u32[]{:S(2)}) collective-permute-start(bf16[4,1,64,2,256]{4,2,0,3,1:T(8,128)(2,1)S(1)} %fusion.10), channel_id=1, source_target_pairs={{4,0},{8,4},{12,8},{0,12},{5,1},{9,5},{13,9},{1,13},{6,2},{10,6},{... | collective-permute-start | bytes 786440 | tf_op jit(solution)/shard_map/ppermute | solution.py:18
  125.3 17.0 %collective-permute-start.10 = (bf16[12,1,64,2,256]{4,2,0,3,1:T(8,128)(2,1)S(1)}, bf16[12,1,64,2,256]{4,2,0,3,1:T(8,128)(2,1)S(1)}, u32[]{:S(2)}, u32[]{:S(2)}) collective-permute-start(bf16[12,1,64,2,256]{4,2,0,3,1:T(8,128)(2,1)S(1)} %pad_maximum_fusion.2), channel_id=1, source_target_pairs={{0,2},{1,3},{4,6},{5,7},{8,10},{9,11},{12,14},{13,15},{16,18},{17,... | collective-permute-start | bytes 2359304 | tf_op jit(solution)/shard_map/ppermute | solution.py:17
  126.8 19.7 %collective-permute-start.11 = (bf16[12,1,64,2,256]{4,2,0,3,1:T(8,128)(2,1)S(1)}, bf16[12,1,64,2,256]{4,2,0,3,1:T(8,128)(2,1)S(1)}, u32[]{:S(2)}, u32[]{:S(2)}) collective-permute-start(bf16[12,1,64,2,256]{4,2,0,3,1:T(8,128)(2,1)S(1)} %pad_maximum_fusion.2), channel_id=1, source_target_pairs={{2,0},{3,1},{6,4},{7,5},{10,8},{11,9},{14,12},{15,13},{18,16},{19,... | collective-permute-start | bytes 2359304 | tf_op jit(solution)/shard_map/ppermute | solution.py:18
  153.4 15.1 %copy-start.4 = (f32[4]{0:T(128)S(1)}, f32[4]{0:T(128)}, u32[]{:S(2)}) copy-start(f32[4]{0:T(128)} %param.13) | copy-start | bytes 52
  154.0 10.5 %collective-permute-start.12 = (bf16[4,1,64,2,256]{4,2,0,3,1:T(8,128)(2,1)S(1)}, bf16[4,1,64,2,256]{4,2,0,3,1:T(8,128)(2,1)S(1)}, u32[]{:S(2)}, u32[]{:S(2)}) collective-permute-start(bf16[4,1,64,2,256]{4,2,0,3,1:T(8,128)(2,1)S(1)} %fusion.4), channel_id=1, source_target_pairs={{0,4},{4,8},{8,12},{12,0},{1,5},{5,9},{9,13},{13,1},{2,6},{6,10},{... | collective-permute-start | bytes 786440 | tf_op jit(solution)/shard_map/ppermute | solution.py:17
  154.1 11.5 %collective-permute-start.13 = (bf16[4,1,64,2,256]{4,2,0,3,1:T(8,128)(2,1)S(1)}, bf16[4,1,64,2,256]{4,2,0,3,1:T(8,128)(2,1)S(1)}, u32[]{:S(2)}, u32[]{:S(2)}) collective-permute-start(bf16[4,1,64,2,256]{4,2,0,3,1:T(8,128)(2,1)S(1)} %fusion.4), channel_id=1, source_target_pairs={{4,0},{8,4},{12,8},{0,12},{5,1},{9,5},{13,9},{1,13},{6,2},{10,6},{... | collective-permute-start | bytes 786440 | tf_op jit(solution)/shard_map/ppermute | solution.py:18
  165.6 15.8 %collective-permute-start.14 = (bf16[12,1,64,2,256]{4,2,0,3,1:T(8,128)(2,1)S(1)}, bf16[12,1,64,2,256]{4,2,0,3,1:T(8,128)(2,1)S(1)}, u32[]{:S(2)}, u32[]{:S(2)}) collective-permute-start(bf16[12,1,64,2,256]{4,2,0,3,1:T(8,128)(2,1)S(1)} %pad_maximum_fusion.3), channel_id=1, source_target_pairs={{0,2},{1,3},{4,6},{5,7},{8,10},{9,11},{12,14},{13,15},{16,18},{17,... | collective-permute-start | bytes 2359304 | tf_op jit(solution)/shard_map/ppermute | solution.py:17
  167.1 18.4 %collective-permute-start.15 = (bf16[12,1,64,2,256]{4,2,0,3,1:T(8,128)(2,1)S(1)}, bf16[12,1,64,2,256]{4,2,0,3,1:T(8,128)(2,1)S(1)}, u32[]{:S(2)}, u32[]{:S(2)}) collective-permute-start(bf16[12,1,64,2,256]{4,2,0,3,1:T(8,128)(2,1)S(1)} %pad_maximum_fusion.3), channel_id=1, source_target_pairs={{2,0},{3,1},{6,4},{7,5},{10,8},{11,9},{14,12},{15,13},{18,16},{19,... | collective-permute-start | bytes 2359304 | tf_op jit(solution)/shard_map/ppermute | solution.py:18
  191.9 1.1 copy-start.2
  195.8 4.4 %copy-start.3 = (s32[4,1,64,256]{3,2,1,0:T(8,128)S(1)}, s32[4,1,64,256]{3,2,1,0:T(8,128)}, u32[]{:S(2)}) copy-start(s32[4,1,64,256]{3,2,1,0:T(8,128)} %param.15) | copy-start | bytes 786436
Sparse Core Ops, SparseCore 0:
  197.2 62.4 reduce-scatter.3
where the time goes:
time: 269 us; the launch traced here: 268 us
  waiting for transfers between devices  150 us (56%)
  starting transfers between devices  29.9 us (11%)
  matrix products  26.5 us (10%)
  blocking collectives  18.4 us (7%)
  local copies, waits for them, and re-layouts  16.5 us (6%)
  between operations  15 us (6%)
  other arithmetic  12.3 us (5%)
    ppermute x8, waiting for transfers between devices, padded(): before = lax.ppermute(last, axis, up)  83.5 us
    unnamed x2, waiting for transfers between devices  40.5 us
    dot_general x108, matrix products, apply_operator(): jnp.einsum('ctik,ctkn->ctin', part, piece, preferred_element_type=jnp.flo...  26.3 us
    ppermute x8, waiting for transfers between devices, padded(): after = lax.ppermute(initial, axis, down)  25.7 us
    psum x1, blocking collectives, body(): quadratic = lax.psum(local_quad, ('wire', 'xsec')) * scale  18.4 us
    ppermute x8, starting transfers between devices, padded(): after = lax.ppermute(initial, axis, down)  16.7 us
    ppermute x8, starting transfers between devices, padded(): before = lax.ppermute(last, axis, up)  13.2 us
    unnamed x19, local copies, waits for them, and re-layouts  7.16 us
  transfers between devices with their start and end apart: 17, of which 17 were waited for; matrix products, arithmetic and copies ran while one was open for 3% of the time, Pallas kernels for 0%

commit v1 on v0

v1 whole, which is shorter than its diff:
```python
import jax
import jax.numpy as jnp
from jax import lax
from jax.sharding import PartitionSpec as P

STEPS = 4


def from_tile(x, offset):
    size = lax.axis_size("xsec")
    return lax.ppermute(x, "xsec", [((i + offset) % size, i) for i in range(size)])


def to_tile(x, offset):
    size = lax.axis_size("xsec")
    return lax.ppermute(x, "xsec", [(i, (i + offset) % size) for i in range(size)])


def around(x, reach):
    size, cells = (lax.axis_size("wire"), x.shape[1])
    up = [(i, (i + 1) % size) for i in range(size)]
    down = [(j, i) for i, j in up]
    before = lax.ppermute(x[:, cells - reach :], "wire", up)
    after = lax.ppermute(x[:, :reach], "wire", down)
    return before, after


def column_block(x, index, width):
    return lax.dynamic_slice_in_dim(x, index * width, width, axis=x.ndim - 1)


def tiles_in(x, width):
    size, me = (lax.axis_size("xsec"), lax.axis_index("xsec"))
    parts = [column_block(x, me, width)]
    for offset in range(1, size):
        parts.append(from_tile(column_block(x, (me - offset) % size, width), offset))
    return parts


def columns_out(parts):
    size, me = (lax.axis_size("xsec"), lax.axis_index("xsec"))
    got = [parts[0]] + [to_tile(parts[offset], offset) for offset in range(1, size)]
    blocks = []
    for j in range(size):
        block = got[0]
        for offset in range(1, size):
            block = jnp.where((me - offset) % size == j, got[offset], block)
        blocks.append(block)
    return jnp.concatenate(blocks, axis=-1)


def band_of(masked, pairs, reach):
    size, me = (lax.axis_size("xsec"), lax.axis_index("xsec"))
    rows = []
    for i in range(size):
        cells = masked[i].shape[0]
        columns = []
        for u in range(size):
            gap = (me + u) % size - (me + i) % size + 1
            picked = lax.dynamic_index_in_dim(masked[i], jnp.clip(gap, 0, 2), 3, keepdims=False)
            if size > 2 and i != u:
                picked = jnp.where((gap >= 0) & (gap <= 2), picked, jnp.zeros_like(picked))
            band = jnp.stack(
                [jnp.pad(picked[c], ((0, 0), (c, cells - 1 - c), (0, 0))) for c in range(cells)]
            )
            columns.append(band)
        rows.append(columns)
    ext = cells + 2 * reach
    orbs = masked[0].shape[1]

    def part(low, high):
        return jnp.concatenate(
            [
                jnp.concatenate(
                    [b[:, :, low:high].reshape(cells * orbs, (high - low) * orbs) for b in columns],
                    axis=1,
                )
                for columns in rows
            ],
            axis=0,
        )

    return part(0, reach), part(reach, reach + cells), part(reach + cells, ext)


def body(blocks, pattern, current, previous, accum, coefs, sketch, signs):
    cells, tiles, orbs, wide = blocks.shape
    halves, local_cols = current.shape[3:]
    count = wide // orbs
    span = count // 3
    reach = span // 2
    xs, me = (lax.axis_size("xsec"), lax.axis_index("xsec"))
    wires = lax.axis_size("wire")
    width = local_cols // xs
    rows = cells * orbs

    field_parts = tiles_in(current[:, 0], width)
    halo_parts = [around(f[None].reshape(1, cells, orbs, halves * width), reach) for f in field_parts]

    masked = (
        blocks[:, 0].reshape(cells, orbs, count, orbs)
        * pattern[:, 0].astype(jnp.bfloat16)[:, None, :, None]
    ).reshape(cells, orbs, span, 3, orbs)
    everyone = [masked] + [from_tile(masked, offset) for offset in range(1, xs)]
    left, own, right = band_of(everyone, None, reach)

    field = [jnp.stack([f[:, :, h] for f in field_parts]) for h in range(halves)]
    before_parts = tiles_in(previous[:, 0], width)
    older = [jnp.stack([f[:, :, h] for f in before_parts]) for h in range(halves)]
    accum_parts = tiles_in(accum[:, 0], width)
    total = [jnp.stack([f[:, :, h] for f in accum_parts]) for h in range(halves)]
    omega_parts = [sketch[:, 0]] + [from_tile(sketch[:, 0], offset) for offset in range(1, xs)]
    omega = jnp.stack(omega_parts).reshape(xs * rows, sketch.shape[3])
    sign_parts = tiles_in((2 * signs[:, 0] - 1).astype(jnp.bfloat16), width)
    plus_minus = jnp.stack(sign_parts)

    halo = [
        [
            jnp.concatenate(
                [p[side].reshape(1, reach, orbs, halves, width)[:, :, :, h] for p in halo_parts]
            )
            for side in range(2)
        ]
        for h in range(halves)
    ]

    def dot(matrix, value):
        return lax.dot(
            matrix, value.reshape(matrix.shape[1], width), preferred_element_type=jnp.float32
        )

    partial_sum = [None] * halves
    for step in range(STEPS):
        for h in range(halves):
            if step > 0:
                halo[h] = around(field[h], reach)
            image = dot(own, field[h]) + dot(left, halo[h][0]) + dot(right, halo[h][1])
            image = image.reshape(xs, cells, orbs, width)
            nxt = (2.0 * image - older[h].astype(jnp.float32)).astype(jnp.bfloat16)
            partial_sum[h] = total[h]
            total[h] = total[h] + coefs[step] * nxt.astype(jnp.float32)
            older[h] = field[h]
            field[h] = nxt

    newest = jnp.stack(
        [columns_out([field[h][i] for i in range(xs)]) for h in range(halves)], axis=2
    )
    before = jnp.stack(
        [columns_out([older[h][i] for i in range(xs)]) for h in range(halves)], axis=2
    )
    summed = jnp.stack(
        [columns_out([partial_sum[h][i] for i in range(xs)]) for h in range(halves)], axis=2
    )
    summed = summed + coefs[STEPS - 1] * newest.astype(jnp.float32)

    all_rows = cells * wires * tiles * xs * orbs
    scale = jnp.float32(1.0) / jnp.sqrt(jnp.float32(all_rows))

    sketched = total[0].astype(jnp.bfloat16).reshape(xs * rows, width)
    piece = lax.dot_general(
        omega, sketched, (((0,), (0,)), ((), ())), preferred_element_type=jnp.float32
    )
    place = lax.axis_index("wire")
    piece = piece.reshape((wires, piece.shape[0] // wires, width))
    hop = 1
    while hop < wires:
        split = piece.reshape((-1, 2) + piece.shape[1:])
        bit = (place // hop) % 2
        keep = lax.dynamic_index_in_dim(split, bit, 1, keepdims=False)
        send = lax.dynamic_index_in_dim(split, 1 - bit, 1, keepdims=False)
        got = lax.ppermute(
            send.astype(jnp.bfloat16), "wire", [(i, i ^ hop) for i in range(wires)]
        )
        piece = keep + got.astype(jnp.float32)
        hop *= 2
    piece = piece[0] * scale
    piece = piece.reshape((xs, piece.shape[0] // xs, width))
    gram = columns_out(
        [lax.dynamic_index_in_dim(piece, (me + i) % xs, 0, keepdims=False) for i in range(xs)]
    )

    quad = jnp.sum(plus_minus.astype(jnp.float32) * total[1], axis=(0, 1, 2))[None]
    hop = 1
    while hop < wires:
        quad = quad + lax.ppermute(quad, "wire", [(i, i ^ hop) for i in range(wires)])
        hop *= 2
    quad = quad * scale
    quadratic = columns_out([quad] * xs)[0]

    return (newest[:, None], before[:, None], summed[:, None], gram, quadratic)


def solution(mesh):
    return jax.shard_map(
        body,
        mesh=mesh,
        in_specs=(
            P(("sample", "wire"), "xsec", None, None),
            P(("sample", "wire"), "xsec", None),
            P(("sample", "wire"), "xsec", None, None, "cols"),
            P(("sample", "wire"), "xsec", None, None, "cols"),
            P(("sample", "wire"), "xsec", None, None, "cols"),
            P(),
            P(("sample", "wire"), "xsec", None, None),
            P(("sample", "wire"), "xsec", None, "cols"),
        ),
        out_specs=(
            P(("sample", "wire"), "xsec", None, None, "cols"),
            P(("sample", "wire"), "xsec", None, None, "cols"),
            P(("sample", "wire"), "xsec", None, None, "cols"),
            P(("sample", "wire", "xsec"), "cols"),
            P(("sample", "cols")),
        ),
        check_vma=False,
    )
```

time: 269 us -> 165 us (0.61)
  waiting for transfers between devices: 150 us -> 52 us
  starting transfers between devices: 29.9 us -> 48.4 us
  blocking collectives: 18.4 us -> 0 us
  local copies, waits for them, and re-layouts: 16.5 us -> 34 us
  matrix products: 26.5 us -> 13.3 us
  between operations: 15 us -> 2.09 us
    ppermute x16 -> x34, waiting for transfers between devices: 109 us -> 52 us  [the longest x6 29.8 us: from_tile(): lax.ppermute(x, 'xsec', [((i + offset) % size, i) for i in range(size)])]
    unnamed x2 -> x0, waiting for transfers between devices: 40.5 us -> none
    ppermute x16 -> x34, starting transfers between devices: 29.9 us -> 48.4 us  [the longest x8 26.2 us: around(): after = lax.ppermute(x[:, :reach], 'wire', down)]
    psum x1 -> x0, blocking collectives: 18.4 us -> none  [body(): quadratic = lax.psum(local_quad, ('wire', 'xsec')) * scale]
    dot_general x108 -> x24, matrix products: 26.3 us -> 13 us  [dot(): lax.dot(matrix, value.reshape(matrix.shape[1], width), preferred_element_...]
    another operation x0 -> x22, local copies, waits for them, and re-layouts: none -> 7.47 us  [the longest x1 5.27 us: body(): blocks[:, 0].reshape(cells, orbs, count, orbs)]
    slice x1 -> x22, local copies, waits for them, and re-layouts: 0.59 us -> 6.66 us  [the longest x16 2.77 us: part(): b[:, :, low:high].reshape(cells * orbs, (high - low) * orbs)]
    reshape x4 -> x17, local copies, waits for them, and re-layouts: 5.95 us -> 9.74 us  [the longest x12 8.47 us: part(): b[:, :, low:high].reshape(cells * orbs, (high - low) * orbs)]
  transfers between devices with their start and end apart: 17 -> 34, of which waited for: 17 -> 12; matrix products, arithmetic and copies ran while one was open for 3% -> 31% of each run, Pallas kernels for 0% -> 0%
where the time goes in v1:
time: 165 us
  waiting for transfers between devices  52 us (32%)
  starting transfers between devices  48.4 us (29%)
  local copies, waits for them, and re-layouts  34 us (21%)
  other arithmetic  14.8 us (9%)
  matrix products  13.3 us (8%)
  between operations  2.09 us (1%)
    ppermute x6, waiting for transfers between devices, from_tile(): lax.ppermute(x, 'xsec', [((i + offset) % size, i) for i in range(size)])  29.8 us
    ppermute x8, starting transfers between devices, around(): after = lax.ppermute(x[:, :reach], 'wire', down)  26.2 us
    dot_general x24, matrix products, dot(): lax.dot(matrix, value.reshape(matrix.shape[1], width), preferred_element_...  13 us
    ppermute x8, waiting for transfers between devices, to_tile(): lax.ppermute(x, 'xsec', [(i, (i + offset) % size) for i in range(size)])  11.9 us
    reshape x12, local copies, waits for them, and re-layouts, part(): b[:, :, low:high].reshape(cells * orbs, (high - low) * orbs)  8.47 us
    ppermute x6, starting transfers between devices, from_tile(): lax.ppermute(x, 'xsec', [((i + offset) % size, i) for i in range(size)])  7.25 us
    ppermute x8, starting transfers between devices, to_tile(): lax.ppermute(x, 'xsec', [(i, (i + offset) % size) for i in range(size)])  6.66 us
    ppermute x8, starting transfers between devices, around(): before = lax.ppermute(x[:, cells - reach:], 'wire', up)  5.94 us
  transfers between devices with their start and end apart: 34, of which 12 were waited for; matrix products, arithmetic and copies ran while one was open for 31% of the time, Pallas kernels for 0%

profile of v1, /device:TPU:0, one launch (start us, length us, event | category | flops | bytes accessed | tf_op | source)
XLA Modules:
  0.0 164.6 jit_solution(404033563464379268)
XLA Ops:
  2.3 3.1 %collective-permute-start.2 = (bf16[1,4,64,256]{3,2,1,0:T(8,128)(2,1)S(1)}, bf16[1,4,64,256]{3,2,1,0:T(8,128)(2,1)}, u32[]{:S(2)}, u32[]{:S(2)}) collective-permute-start(bf16[1,4,64,256]{3,2,1,0:T(8,128)(2,1)S(1)} %reshape_broadcast_in_dim.6), channel_id=1, source_target_pairs={{0,4},{4,8},{8,12},{12,0},{1,5},{5,9},{9,13},{13,1},{2,6},{6,10},{... | collective-permute-start | bytes 393224 | tf_op jit(solution)/shard_map/ppermute | solution.py:23
  5.4 2.1 %collective-permute-start.4 = (bf16[1,4,64,256]{3,2,1,0:T(8,128)(2,1)S(1)}, bf16[1,4,64,256]{3,2,1,0:T(8,128)(2,1)S(1)}, u32[]{:S(2)}, u32[]{:S(2)}) collective-permute-start(bf16[1,4,64,256]{3,2,1,0:T(8,128)(2,1)S(1)} %reshape_broadcast_in_dim.6), channel_id=1, source_target_pairs={{4,0},{8,4},{12,8},{0,12},{5,1},{9,5},{13,9},{1,13},{6,2},{10,6},{... | collective-permute-start | bytes 393224 | tf_op jit(solution)/shard_map/ppermute | solution.py:24
  7.5 5.3 %reshape_squeeze.3 = bf16[4,64,9,3,64]{4,3,2,1,0:T(4,128)(2,1)} reshape(bf16[4,1,64,1728]{3,2,1,0:T(8,128)(2,1)} %param.8) | data formatting | bytes 1769472 | tf_op jit(solution)/shard_map/reshape;squeeze | solution.py:101
  12.9 2.7 %broadcast_multiply_fusion = bf16[4,64,9,3,64]{4,3,2,1,0:T(4,128)(2,1)S(1)} fusion(bf16[4,64,9,3,64]{4,3,2,1,0:T(4,128)(2,1)} %reshape_squeeze.3, bf16[4,9,3]{2,1,0:T(8,128)(2,1)S(1)} %convert_element_type.215), kind=kLoop, calls=%fused_computation | loop fusion | flops 442368 | bytes 1769688 | tf_op jit(solution)/shard_map/mul | solution.py:101
  22.4 2.5 %fusion.52 = (bf16[1,64,9,1,64]{4,3,2,1,0:T(2,128)(2,1)S(1)}, bf16[1,64,9,1,64]{4,3,2,1,0:T(2,128)(2,1)S(1)}, bf16[1,64,9,1,64]{4,3,2,1,0:T(2,128)(2,1)S(1)}, bf...) fusion(bf16[4,64,9,3,64]{4,3,2,1,0:T(4,128)(2,1)S(1)} %broadcas, ...), kind=kLoop, calls=%fused_computation.222 | loop fusion | bytes 1179664 | tf_op jit(solution)/shard_map/slice | solution.py:64
  34.3 27.5 %collective-permute-done.30 = bf16[4,64,128]{2,1,0:T(8,128)(2,1)S(1)} collective-permute-done((bf16[4,64,128]{2,1,0:T(8,128)(2,1)}, bf16[4,64,128]{2,1,0:T(8,128)(2,1)S(1)}, u32[]{:S(2)}, u32[]{:S(2)}) %collective-permute-start.30) | collective-permute-done | bytes 65568 | tf_op jit(solution)/shard_map/ppermute | solution.py:11
  68.2 3.7 %collective-permute-start.5 = (bf16[1,4,64,256]{3,2,1,0:T(8,128)(2,1)S(1)}, bf16[1,4,64,256]{3,2,1,0:T(8,128)(2,1)S(1)}, u32[]{:S(2)}, u32[]{:S(2)}) collective-permute-start(bf16[1,4,64,256]{3,2,1,0:T(8,128)(2,1)S(1)} %reshape_broadcast_in_dim.7), channel_id=1, source_target_pairs={{4,0},{8,4},{12,8},{0,12},{5,1},{9,5},{13,9},{1,13},{6,2},{10,6},{... | collective-permute-start | bytes 393224 | tf_op jit(solution)/shard_map/ppermute | solution.py:24
  75.6 1.9 %collective-permute-done.26 = bf16[4,64,512]{2,1,0:T(8,128)(2,1)S(1)} collective-permute-done((bf16[4,64,512]{2,1,0:T(8,128)(2,1)S(1)}, bf16[4,64,512]{2,1,0:T(8,128)(2,1)S(1)}, u32[]{:S(2)}, u32[]{:S(2)}) %collective-permute-start.26) | collective-permute-done | bytes 262176 | tf_op jit(solution)/shard_map/ppermute | solution.py:11
  89.7 3.8 %collective-permute-start.15 = (bf16[2,4,64,128]{3,2,1,0:T(8,128)(2,1)S(1)}, bf16[2,4,64,128]{3,2,1,0:T(8,128)(2,1)S(1)}, u32[]{:S(2)}, u32[]{:S(2)}) collective-permute-start(bf16[2,4,64,128]{3,2,1,0:T(8,128)(2,1)S(1)} %subtract_convert_fusion.2), channel_id=1, source_target_pairs={{4,0},{8,4},{12,8},{0,12},{5,1},{9,5},{13,9},{1,13},{6,2},{10,6},{... | collective-permute-start | bytes 393224 | tf_op jit(solution)/shard_map/ppermute | solution.py:24
  94.6 3.8 %collective-permute-start.8 = (bf16[2,4,64,128]{3,2,1,0:T(8,128)(2,1)S(1)}, bf16[2,4,64,128]{3,2,1,0:T(8,128)(2,1)S(1)}, u32[]{:S(2)}, u32[]{:S(2)}) collective-permute-start(bf16[2,4,64,128]{3,2,1,0:T(8,128)(2,1)S(1)} %subtract_convert_fusion.5), channel_id=1, source_target_pairs={{4,0},{8,4},{12,8},{0,12},{5,1},{9,5},{13,9},{1,13},{6,2},{10,6},{... | collective-permute-start | bytes 393224 | tf_op jit(solution)/shard_map/ppermute | solution.py:24
  100.1 3.4 %collective-permute-start.17 = (bf16[2,4,64,128]{3,2,1,0:T(8,128)(2,1)S(1)}, bf16[2,4,64,128]{3,2,1,0:T(8,128)(2,1)S(1)}, u32[]{:S(2)}, u32[]{:S(2)}) collective-permute-start(bf16[2,4,64,128]{3,2,1,0:T(8,128)(2,1)S(1)} %subtract_convert_fusion), channel_id=1, source_target_pairs={{4,0},{8,4},{12,8},{0,12},{5,1},{9,5},{13,9},{1,13},{6,2},{10,6},{... | collective-permute-start | bytes 393224 | tf_op jit(solution)/shard_map/ppermute | solution.py:24
  105.8 2.8 %collective-permute-start.10 = (bf16[2,4,64,128]{3,2,1,0:T(8,128)(2,1)S(1)}, bf16[2,4,64,128]{3,2,1,0:T(8,128)(2,1)S(1)}, u32[]{:S(2)}, u32[]{:S(2)}) collective-permute-start(bf16[2,4,64,128]{3,2,1,0:T(8,128)(2,1)S(1)} %subtract_convert_fusion.3), channel_id=1, source_target_pairs={{4,0},{8,4},{12,8},{0,12},{5,1},{9,5},{13,9},{1,13},{6,2},{10,6},{... | collective-permute-start | bytes 393224 | tf_op jit(solution)/shard_map/ppermute | solution.py:24
  110.3 1.9 %fusion.29 = (f32[2,4,64,128]{3,2,1,0:T(8,128)S(1)}, bf16[2,4,64,128]{3,2,1,0:T(8,128)(2,1)S(1)}, f32[2,4,64,128]{3,2,1,0:T(8,128)S(1)}) fusion(f32[]{:T(128)} %bitcast.95, f32[]{:T(128)} %bitcast.94, f32[]{:T(128)} %bitcast.93, f32[1,4,64,128]{3,2,1,0:T(8,128)S(1)} %copy-done.2, f32[1,4,64,128]{3,2,1,0:T(8,128)S(1)} %get-tuple-element.76, ...), kind=kLoop, calls=%fused_computation.71 | loop fusion | flops 1310720 | bytes 1966092 | tf_op jit(solution)/shard_map/add | solution.py:141
  113.3 2.8 %collective-permute-start.19 = (bf16[2,4,64,128]{3,2,1,0:T(8,128)(2,1)S(1)}, bf16[2,4,64,128]{3,2,1,0:T(8,128)(2,1)S(1)}, u32[]{:S(2)}, u32[]{:S(2)}) collective-permute-start(bf16[2,4,64,128]{3,2,1,0:T(8,128)(2,1)S(1)} %get-tuple-element.38), channel_id=1, source_target_pairs={{4,0},{8,4},{12,8},{0,12},{5,1},{9,5},{13,9},{1,13},{6,2},{10,6},{... | collective-permute-start | bytes 393224 | tf_op jit(solution)/shard_map/ppermute | solution.py:24
  117.3 1.9 %fusion.17 = (f32[2,4,64,128]{3,2,1,0:T(8,128)S(1)}, bf16[2,4,64,128]{3,2,1,0:T(8,128)(2,1)S(1)}, f32[2,4,64,128]{3,2,1,0:T(8,128)S(1)}) fusion(f32[]{:T(128)} %bitcast.95, f32[]{:T(128)} %bitcast.94, f32[]{:T(128)} %bitcast.93, f32[1,4,64,128]{3,2,1,0:T(8,128)S(1)} %copy-done.1, f32[1,4,64,128]{3,2,1,0:T(8,128)S(1)} %get-tuple-element.75, ...), kind=kLoop, calls=%fused_computation.59 | loop fusion | flops 1310720 | bytes 1966092 | tf_op jit(solution)/shard_map/add | solution.py:141
  119.4 3.8 %collective-permute-start.12 = (bf16[2,4,64,128]{3,2,1,0:T(8,128)(2,1)S(1)}, bf16[2,4,64,128]{3,2,1,0:T(8,128)(2,1)S(1)}, u32[]{:S(2)}, u32[]{:S(2)}) collective-permute-start(bf16[2,4,64,128]{3,2,1,0:T(8,128)(2,1)S(1)} %get-tuple-element.36), channel_id=1, source_target_pairs={{4,0},{8,4},{12,8},{0,12},{5,1},{9,5},{13,9},{1,13},{6,2},{10,6},{... | collective-permute-start | bytes 393224 | tf_op jit(solution)/shard_map/ppermute | solution.py:24
  123.9 4.1 %collective-permute-done.21 = bf16[4,64,128]{2,1,0:T(8,128)(2,1)S(1)} collective-permute-done((bf16[4,64,128]{2,1,0:T(8,128)(2,1)S(1)}, bf16[4,64,128]{2,1,0:T(8,128)(2,1)S(1)}, u32[]{:S(2)}, u32[]{:S(2)}) %collective-permute-start.21) | collective-permute-done | bytes 65568 | tf_op jit(solution)/shard_map/ppermute | solution.py:16
  128.6 3.6 %collective-permute-done.22 = bf16[4,64,128]{2,1,0:T(8,128)(2,1)S(1)} collective-permute-done((bf16[4,64,128]{2,1,0:T(8,128)(2,1)S(1)}, bf16[4,64,128]{2,1,0:T(8,128)(2,1)S(1)}, u32[]{:S(2)}, u32[]{:S(2)}) %collective-permute-start.22) | collective-permute-done | bytes 65568 | tf_op jit(solution)/shard_map/ppermute | solution.py:16
  135.7 2.8 %fusion.25 = (f32[128]{0:T(128)S(1)}, f32[512,128]{1,0:T(8,128)S(1)}) fusion(bf16[512,128]{1,0:T(8,128)(2,1)S(1)} %get-tuple-element.121, bf16[512,128]{1,0:T(8,128)(2,1)S(1)} %get-tuple-element.123, f32[2,4,64,128]{3,2,1,0:T(8,128)S(1)} %get-tuple-element.73, bf16[2,4,64,128]{3,2,1,0:T(8,128)(2,1)S(1)} %copy-done.17, f32[]{:T(128)} %bitcast.104, ...), kind=kOutput, calls=%fused_computation.67 | convolution fusion | flops 70582144 | bytes 2097680 | tf_op jit(solution)/shard_map/dot_general | solution.py:128
  138.8 2.7 %fusion.13 = (bf16[512,128]{1,0:T(8,128)(2,1)S(1)}, f32[512,128]{1,0:T(8,128)S(1)}) fusion(bf16[512,128]{1,0:T(8,128)(2,1)S(1)} %get-tuple-element.125, bf16[512,128]{1,0:T(8,128)(2,1)S(1)} %get-tuple-element.127, f32[2,4,64,128]{3,2,1,0:T(8,128)S(1)} %get-tuple-element.74, f32[]{:T(128)} %bitcast.104, f32[]{:T(128)} %bitcast.95, f32[]{:T(128)} %bitcast.94, ...), kind=kOutput, calls=%fused_computation.55 | convolution fusion | flops 70451200 | bytes 2097168 | tf_op jit(solution)/shard_map/dot_general | solution.py:128
  141.9 2.1 %collective-permute-start.27 = (bf16[2,128,128]{2,1,0:T(8,128)(2,1)S(1)}, bf16[2,128,128]{2,1,0:T(8,128)(2,1)S(1)}, u32[]{:S(2)}, u32[]{:S(2)}) collective-permute-start(bf16[2,128,128]{2,1,0:T(8,128)(2,1)S(1)} %fusion.45), channel_id=1, source_target_pairs={{0,4},{4,0},{8,12},{12,8},{1,5},{5,1},{9,13},{13,9},{2,6},{6,2},{1... | collective-permute-start | bytes 196616 | tf_op jit(solution)/shard_map/ppermute | solution.py:171
  146.4 4.4 %collective-permute-done.32 = f32[1,128]{1,0:T(1,128)S(1)} collective-permute-done((f32[1,128]{1,0:T(1,128)S(1)}, f32[1,128]{1,0:T(1,128)S(1)}, u32[]{:S(2)}, u32[]{:S(2)}) %collective-permute-start.32) | collective-permute-done | bytes 544 | tf_op jit(solution)/shard_map/ppermute | solution.py:185
  151.5 3.0 %collective-permute-done.33 = f32[1,128]{1,0:T(1,128)S(1)} collective-permute-done((f32[1,128]{1,0:T(1,128)S(1)}, f32[1,128]{1,0:T(1,128)S(1)}, u32[]{:S(2)}, u32[]{:S(2)}) %collective-permute-start.33) | collective-permute-done | bytes 544 | tf_op jit(solution)/shard_map/ppermute | solution.py:16
  156.0 4.0 %collective-permute-done.28 = bf16[1,128,128]{2,1,0:T(8,128)(2,1)S(1)} collective-permute-done((bf16[1,128,128]{2,1,0:T(8,128)(2,1)S(1)}, bf16[1,128,128]{2,1,0:T(8,128)(2,1)S(1)}, u32[]{:S(2)}, u32[]{:S(2)}) %collective-permute-start.28) | collective-permute-done | bytes 32800 | tf_op jit(solution)/shard_map/ppermute | solution.py:171
  (261 shorter events, 62.7 us)
Async XLA Ops:
  2.3 62.5 %collective-permute-start.2 = (bf16[1,4,64,256]{3,2,1,0:T(8,128)(2,1)S(1)}, bf16[1,4,64,256]{3,2,1,0:T(8,128)(2,1)}, u32[]{:S(2)}, u32[]{:S(2)}) collective-permute-start(bf16[1,4,64,256]{3,2,1,0:T(8,128)(2,1)S(1)} %reshape_broadcast_in_dim.6), channel_id=1, source_target_pairs={{0,4},{4,8},{8,12},{12,0},{1,5},{5,9},{9,13},{13,1},{2,6},{6,10},{... | collective-permute-start | bytes 393224 | tf_op jit(solution)/shard_map/ppermute | solution.py:23
  5.4 62.1 %collective-permute-start.4 = (bf16[1,4,64,256]{3,2,1,0:T(8,128)(2,1)S(1)}, bf16[1,4,64,256]{3,2,1,0:T(8,128)(2,1)S(1)}, u32[]{:S(2)}, u32[]{:S(2)}) collective-permute-start(bf16[1,4,64,256]{3,2,1,0:T(8,128)(2,1)S(1)} %reshape_broadcast_in_dim.6), channel_id=1, source_target_pairs={{4,0},{8,4},{12,8},{0,12},{5,1},{9,5},{13,9},{1,13},{6,2},{10,6},{... | collective-permute-start | bytes 393224 | tf_op jit(solution)/shard_map/ppermute | solution.py:24
  17.3 63.2 %collective-permute-start = (bf16[4,64,9,3,64]{4,1,3,2,0:T(8,128)(2,1)}, bf16[4,64,9,3,64]{4,1,3,2,0:T(8,128)(2,1)}, u32[]{:S(2)}, u32[]{:S(2)}) collective-permute-start(bf16[4,64,9,3,64]{4,1,3,2,0:T(8,128)(2,1)} %copy.225), channel_id=1, source_target_pairs={{2,0},{0,2},{3,1},{1,3},{6,4},{4,6},{7,5},{5,7},{10,8},{8,10},{11,... | collective-permute-start | bytes 2654216 | tf_op jit(solution)/shard_map/ppermute | solution.py:11
  19.6 44.3 %collective-permute-start.1 = (bf16[4,64,2,128]{3,1,0,2:T(8,128)(2,1)}, bf16[4,64,2,128]{3,1,0,2:T(8,128)(2,1)S(1)}, u32[]{:S(2)}, u32[]{:S(2)}) collective-permute-start(bf16[4,64,2,128]{3,1,0,2:T(8,128)(2,1)} %bitcast.308), channel_id=1, source_target_pairs={{2,0},{0,2},{3,1},{1,3},{6,4},{4,6},{7,5},{5,7},{10,8},{8,10},{11,... | collective-permute-start | bytes 393224 | tf_op jit(solution)/shard_map/ppermute | solution.py:11
  20.7 41.1 %collective-permute-start.30 = (bf16[4,64,128]{2,1,0:T(8,128)(2,1)}, bf16[4,64,128]{2,1,0:T(8,128)(2,1)S(1)}, u32[]{:S(2)}, u32[]{:S(2)}) collective-permute-start(bf16[4,64,128]{2,1,0:T(8,128)(2,1)} %get-tuple-element.92), channel_id=1, source_target_pairs={{2,0},{0,2},{3,1},{1,3},{6,4},{4,6},{7,5},{5,7},{10,8},{8,10},{11,... | collective-permute-start | bytes 196616 | tf_op jit(solution)/shard_map/ppermute | solution.py:11
  64.0 15.8 %collective-permute-start.23 = (f32[4,64,2,128]{3,1,0,2:T(8,128)S(1)}, f32[4,64,2,128]{3,1,0,2:T(8,128)S(1)}, u32[]{:S(2)}, u32[]{:S(2)}) collective-permute-start(f32[4,64,2,128]{3,1,0,2:T(8,128)S(1)} %bitcast.339), channel_id=1, source_target_pairs={{2,0},{0,2},{3,1},{1,3},{6,4},{4,6},{7,5},{5,7},{10,8},{8,10},{11,... | collective-permute-start | bytes 786440 | tf_op jit(solution)/shard_map/ppermute | solution.py:11
  64.7 12.7 %collective-permute-start.26 = (bf16[4,64,512]{2,1,0:T(8,128)(2,1)S(1)}, bf16[4,64,512]{2,1,0:T(8,128)(2,1)S(1)}, u32[]{:S(2)}, u32[]{:S(2)}) collective-permute-start(bf16[4,64,512]{2,1,0:T(8,128)(2,1)S(1)} %bitcast.350), channel_id=1, source_target_pairs={{2,0},{0,2},{3,1},{1,3},{6,4},{4,6},{7,5},{5,7},{10,8},{8,10},{11,... | collective-permute-start | bytes 786440 | tf_op jit(solution)/shard_map/ppermute | solution.py:11
  89.6 9.3 %collective-permute-start.14 = (bf16[2,4,64,128]{3,2,1,0:T(8,128)(2,1)S(1)}, bf16[2,4,64,128]{3,2,1,0:T(8,128)(2,1)S(1)}, u32[]{:S(2)}, u32[]{:S(2)}) collective-permute-start(bf16[2,4,64,128]{3,2,1,0:T(8,128)(2,1)S(1)} %subtract_convert_fusion.2), channel_id=1, source_target_pairs={{0,4},{4,8},{8,12},{12,0},{1,5},{5,9},{9,13},{13,1},{2,6},{6,10},{... | collective-permute-start | bytes 393224 | tf_op jit(solution)/shard_map/ppermute | solution.py:23
  89.7 9.6 %collective-permute-start.15 = (bf16[2,4,64,128]{3,2,1,0:T(8,128)(2,1)S(1)}, bf16[2,4,64,128]{3,2,1,0:T(8,128)(2,1)S(1)}, u32[]{:S(2)}, u32[]{:S(2)}) collective-permute-start(bf16[2,4,64,128]{3,2,1,0:T(8,128)(2,1)S(1)} %subtract_convert_fusion.2), channel_id=1, source_target_pairs={{4,0},{8,4},{12,8},{0,12},{5,1},{9,5},{13,9},{1,13},{6,2},{10,6},{... | collective-permute-start | bytes 393224 | tf_op jit(solution)/shard_map/ppermute | solution.py:24
  94.5 9.0 %collective-permute-start.7 = (bf16[2,4,64,128]{3,2,1,0:T(8,128)(2,1)S(1)}, bf16[2,4,64,128]{3,2,1,0:T(8,128)(2,1)S(1)}, u32[]{:S(2)}, u32[]{:S(2)}) collective-permute-start(bf16[2,4,64,128]{3,2,1,0:T(8,128)(2,1)S(1)} %subtract_convert_fusion.5), channel_id=1, source_target_pairs={{0,4},{4,8},{8,12},{12,0},{1,5},{5,9},{9,13},{13,1},{2,6},{6,10},{... | collective-permute-start | bytes 393224 | tf_op jit(solution)/shard_map/ppermute | solution.py:23
  94.6 9.8 %collective-permute-start.8 = (bf16[2,4,64,128]{3,2,1,0:T(8,128)(2,1)S(1)}, bf16[2,4,64,128]{3,2,1,0:T(8,128)(2,1)S(1)}, u32[]{:S(2)}, u32[]{:S(2)}) collective-permute-start(bf16[2,4,64,128]{3,2,1,0:T(8,128)(2,1)S(1)} %subtract_convert_fusion.5), channel_id=1, source_target_pairs={{4,0},{8,4},{12,8},{0,12},{5,1},{9,5},{13,9},{1,13},{6,2},{10,6},{... | collective-permute-start | bytes 393224 | tf_op jit(solution)/shard_map/ppermute | solution.py:24
  99.6 9.5 %collective-permute-start.16 = (bf16[2,4,64,128]{3,2,1,0:T(8,128)(2,1)S(1)}, bf16[2,4,64,128]{3,2,1,0:T(8,128)(2,1)S(1)}, u32[]{:S(2)}, u32[]{:S(2)}) collective-permute-start(bf16[2,4,64,128]{3,2,1,0:T(8,128)(2,1)S(1)} %subtract_convert_fusion), channel_id=1, source_target_pairs={{0,4},{4,8},{8,12},{12,0},{1,5},{5,9},{9,13},{13,1},{2,6},{6,10},{... | collective-permute-start | bytes 393224 | tf_op jit(solution)/shard_map/ppermute | solution.py:23
  100.1 9.8 %collective-permute-start.17 = (bf16[2,4,64,128]{3,2,1,0:T(8,128)(2,1)S(1)}, bf16[2,4,64,128]{3,2,1,0:T(8,128)(2,1)S(1)}, u32[]{:S(2)}, u32[]{:S(2)}) collective-permute-start(bf16[2,4,64,128]{3,2,1,0:T(8,128)(2,1)S(1)} %subtract_convert_fusion), channel_id=1, source_target_pairs={{4,0},{8,4},{12,8},{0,12},{5,1},{9,5},{13,9},{1,13},{6,2},{10,6},{... | collective-permute-start | bytes 393224 | tf_op jit(solution)/shard_map/ppermute | solution.py:24
  104.7 11.7 %collective-permute-start.9 = (bf16[2,4,64,128]{3,2,1,0:T(8,128)(2,1)S(1)}, bf16[2,4,64,128]{3,2,1,0:T(8,128)(2,1)S(1)}, u32[]{:S(2)}, u32[]{:S(2)}) collective-permute-start(bf16[2,4,64,128]{3,2,1,0:T(8,128)(2,1)S(1)} %subtract_convert_fusion.3), channel_id=1, source_target_pairs={{0,4},{4,8},{8,12},{12,0},{1,5},{5,9},{9,13},{13,1},{2,6},{6,10},{... | collective-permute-start | bytes 393224 | tf_op jit(solution)/shard_map/ppermute | solution.py:23
  105.8 11.0 %collective-permute-start.10 = (bf16[2,4,64,128]{3,2,1,0:T(8,128)(2,1)S(1)}, bf16[2,4,64,128]{3,2,1,0:T(8,128)(2,1)S(1)}, u32[]{:S(2)}, u32[]{:S(2)}) collective-permute-start(bf16[2,4,64,128]{3,2,1,0:T(8,128)(2,1)S(1)} %subtract_convert_fusion.3), channel_id=1, source_target_pairs={{4,0},{8,4},{12,8},{0,12},{5,1},{9,5},{13,9},{1,13},{6,2},{10,6},{... | collective-permute-start | bytes 393224 | tf_op jit(solution)/shard_map/ppermute | solution.py:24
  112.2 21.7 %collective-permute-start.18 = (bf16[2,4,64,128]{3,2,1,0:T(8,128)(2,1)S(1)}, bf16[2,4,64,128]{3,2,1,0:T(8,128)(2,1)S(1)}, u32[]{:S(2)}, u32[]{:S(2)}) collective-permute-start(bf16[2,4,64,128]{3,2,1,0:T(8,128)(2,1)S(1)} %get-tuple-element.38), channel_id=1, source_target_pairs={{0,4},{4,8},{8,12},{12,0},{1,5},{5,9},{9,13},{13,1},{2,6},{6,10},{... | collective-permute-start | bytes 393224 | tf_op jit(solution)/shard_map/ppermute | solution.py:23
  113.3 22.3 %collective-permute-start.19 = (bf16[2,4,64,128]{3,2,1,0:T(8,128)(2,1)S(1)}, bf16[2,4,64,128]{3,2,1,0:T(8,128)(2,1)S(1)}, u32[]{:S(2)}, u32[]{:S(2)}) collective-permute-start(bf16[2,4,64,128]{3,2,1,0:T(8,128)(2,1)S(1)} %get-tuple-element.38), channel_id=1, source_target_pairs={{4,0},{8,4},{12,8},{0,12},{5,1},{9,5},{13,9},{1,13},{6,2},{10,6},{... | collective-permute-start | bytes 393224 | tf_op jit(solution)/shard_map/ppermute | solution.py:24
  119.3 19.2 %collective-permute-start.11 = (bf16[2,4,64,128]{3,2,1,0:T(8,128)(2,1)S(1)}, bf16[2,4,64,128]{3,2,1,0:T(8,128)(2,1)S(1)}, u32[]{:S(2)}, u32[]{:S(2)}) collective-permute-start(bf16[2,4,64,128]{3,2,1,0:T(8,128)(2,1)S(1)} %get-tuple-element.36), channel_id=1, source_target_pairs={{0,4},{4,8},{8,12},{12,0},{1,5},{5,9},{9,13},{13,1},{2,6},{6,10},{... | collective-permute-start | bytes 393224 | tf_op jit(solution)/shard_map/ppermute | solution.py:23
  119.4 19.5 %collective-permute-start.12 = (bf16[2,4,64,128]{3,2,1,0:T(8,128)(2,1)S(1)}, bf16[2,4,64,128]{3,2,1,0:T(8,128)(2,1)S(1)}, u32[]{:S(2)}, u32[]{:S(2)}) collective-permute-start(bf16[2,4,64,128]{3,2,1,0:T(8,128)(2,1)S(1)} %get-tuple-element.36), channel_id=1, source_target_pairs={{4,0},{8,4},{12,8},{0,12},{5,1},{9,5},{13,9},{1,13},{6,2},{10,6},{... | collective-permute-start | bytes 393224 | tf_op jit(solution)/shard_map/ppermute | solution.py:24
  132.3 12.5 %collective-permute-start.24 = (f32[4,64,128]{2,1,0:T(8,128)S(1)}, f32[4,64,128]{2,1,0:T(8,128)S(1)}, u32[]{:S(2)}, u32[]{:S(2)}) collective-permute-start(f32[4,64,128]{2,1,0:T(8,128)S(1)} %slice_bitcast_fusion.9), channel_id=1, source_target_pairs={{0,2},{2,0},{1,3},{3,1},{4,6},{6,4},{5,7},{7,5},{8,10},{10,8},{9,1... | collective-permute-start | bytes 393224 | tf_op jit(solution)/shard_map/ppermute | solution.py:16
  133.9 12.4 %collective-permute-start.25 = (f32[4,64,128]{2,1,0:T(8,128)S(1)}, f32[4,64,128]{2,1,0:T(8,128)S(1)}, u32[]{:S(2)}, u32[]{:S(2)}) collective-permute-start(f32[4,64,128]{2,1,0:T(8,128)S(1)} %slice_bitcast_fusion.5), channel_id=1, source_target_pairs={{0,2},{2,0},{1,3},{3,1},{4,6},{6,4},{5,7},{7,5},{8,10},{10,8},{9,1... | collective-permute-start | bytes 393224 | tf_op jit(solution)/shard_map/ppermute | solution.py:16
  141.9 13.1 %collective-permute-start.27 = (bf16[2,128,128]{2,1,0:T(8,128)(2,1)S(1)}, bf16[2,128,128]{2,1,0:T(8,128)(2,1)S(1)}, u32[]{:S(2)}, u32[]{:S(2)}) collective-permute-start(bf16[2,128,128]{2,1,0:T(8,128)(2,1)S(1)} %fusion.45), channel_id=1, source_target_pairs={{0,4},{4,0},{8,12},{12,8},{1,5},{5,1},{9,13},{13,9},{2,6},{6,2},{1... | collective-permute-start | bytes 196616 | tf_op jit(solution)/shard_map/ppermute | solution.py:171
  144.0 11.1 %collective-permute-start.13 = (bf16[4,64,128]{2,1,0:T(8,128)(2,1)S(1)}, bf16[4,64,128]{2,1,0:T(8,128)(2,1)S(1)}, u32[]{:S(2)}, u32[]{:S(2)}) collective-permute-start(bf16[4,64,128]{2,1,0:T(8,128)(2,1)S(1)} %slice_bitcast_fusion.23), channel_id=1, source_target_pairs={{0,2},{2,0},{1,3},{3,1},{4,6},{6,4},{5,7},{7,5},{8,10},{10,8},{9,1... | collective-permute-start | bytes 196616 | tf_op jit(solution)/shard_map/ppermute | solution.py:16
  144.7 10.5 %collective-permute-start.20 = (bf16[4,64,128]{2,1,0:T(8,128)(2,1)S(1)}, bf16[4,64,128]{2,1,0:T(8,128)(2,1)S(1)}, u32[]{:S(2)}, u32[]{:S(2)}) collective-permute-start(bf16[4,64,128]{2,1,0:T(8,128)(2,1)S(1)} %slice_bitcast_fusion.17), channel_id=1, source_target_pairs={{0,2},{2,0},{1,3},{3,1},{4,6},{6,4},{5,7},{7,5},{8,10},{10,8},{9,1... | collective-permute-start | bytes 196616 | tf_op jit(solution)/shard_map/ppermute | solution.py:16
  (33 other events, 177.0 us)

commit v2 on v0

v2 whole, which is shorter than its diff:
```python
import functools

import jax
import jax.numpy as jnp
from jax import lax
from jax.experimental import pallas as pl
from jax.experimental.pallas import tpu as pltpu
from jax.sharding import PartitionSpec as P

STEPS = 4
VMEM = 12 << 20
SCALAR = pl.BlockSpec(memory_space=pltpu.SMEM)
WHOLE = pl.BlockSpec(memory_space=pltpu.VMEM)
PARAMS = pltpu.CompilerParams(vmem_limit_bytes=VMEM)


def bf16(*shape):
    return jax.ShapeDtypeStruct(shape, jnp.bfloat16)


def f32(*shape):
    return jax.ShapeDtypeStruct(shape, jnp.float32)


def cost(moved, flops=0):
    return pl.CostEstimate(flops=flops, transcendentals=0, bytes_accessed=moved)


def from_tile(x, offset, axis="xsec"):
    size = lax.axis_size(axis)
    return lax.ppermute(x, axis, [((i + offset) % size, i) for i in range(size)])


def to_tile(x, offset):
    return from_tile(x, lax.axis_size("xsec") - offset)


def around(x):
    size = lax.axis_size("wire")
    first, second = ([], [])
    for i in range(0, size, 2):
        j, k = (i + 1, (i + 2) % size)
        first += [(i, j), (j, i)]
        second += [(j, k), (k, j)]
    one = lax.ppermute(x, "wire", first)
    two = lax.ppermute(x, "wire", second)
    return one, two


def swap_bits(x, hop):
    return lax.ppermute(x, "wire", [(i, i ^ hop) for i in range(lax.axis_size("wire"))])


def deal_kernel(me, x, *outs):
    cells, _, orbs, halves, columns = x.shape
    count = len(outs)
    width = columns // count
    wide = x[...].astype(jnp.float32)
    for h in range(halves):
        value = wide[:, 0, :, h, :].reshape(cells * orbs, columns)
        for i in range(count):
            picked = value[:, :width]
            for b in range(1, count):
                block = value[:, b * width : (b + 1) * width]
                picked = jnp.where((me[0] - i + count) % count == b, block, picked)
            outs[i][:, h * width : (h + 1) * width] = picked.astype(x.dtype)


def deal(x, me):
    count = lax.axis_size("xsec")
    cells, _, orbs, halves, columns = x.shape
    shape = (cells * orbs, halves * columns // count)
    return pl.pallas_call(
        deal_kernel,
        out_shape=[jax.ShapeDtypeStruct(shape, x.dtype)] * count,
        in_specs=[SCALAR, WHOLE],
        out_specs=[WHOLE] * count,
        compiler_params=PARAMS,
        cost_estimate=cost(2 * x.size * x.dtype.itemsize),
    )(me, x)


def before_kernel(count, me, *refs):
    out = refs[-1]
    cells, _, orbs, halves, columns = out.shape
    width = columns // count
    rows = cells * orbs
    for h in range(halves):
        own, got = (refs[h * count], refs[h * count + 1 : (h + 1) * count])
        for b in range(count):
            value = own[:rows].astype(jnp.float32)
            for i in range(1, count):
                other = got[i - 1][...].astype(jnp.float32)
                value = jnp.where((me[0] - i + count) % count == b, other, value)
            value = value.astype(out.dtype).reshape(cells, orbs, width)
            out[:, 0, :, h, b * width : (b + 1) * width] = value


def last_kernel(count, me, coef, *refs):
    newest, summed = refs[-2:]
    cells, _, orbs, halves, columns = newest.shape
    width = columns // count
    rows = cells * orbs
    for h in range(halves):
        at = h * 3 * count

        def value(kind, i):
            return refs[at + kind * count + i][:rows].astype(jnp.float32)

        for b in range(count):
            late, mid, sums = [value(kind, 0) for kind in range(3)]
            for i in range(1, count):
                here = (me[0] - i + count) % count == b
                late = jnp.where(here, value(0, i), late)
                mid = jnp.where(here, value(1, i), mid)
                sums = jnp.where(here, value(2, i), sums)
            columns_at = slice(b * width, (b + 1) * width)
            shape = (cells, orbs, width)
            newest[:, 0, :, h, columns_at] = late.astype(newest.dtype).reshape(shape)
            sums = sums + coef[STEPS - 2] * mid
            sums = sums + coef[STEPS - 1] * late
            summed[:, 0, :, h, columns_at] = sums.reshape(shape)


def band_kernel(tile, sizes, gap, even, slot, pattern, *refs):
    cells, orbs, reach, tiles, pieces = sizes
    first, own, second = refs[-3:]
    share = cells // pieces
    span = 2 * reach + 1
    zero = jnp.zeros((orbs, orbs), jnp.bfloat16)

    def write(parts):
        def block(c, u, x):
            d = x - c
            if d < 0 or d >= span:
                return zero
            ref = parts[c // share]

            def at(e):
                column = 3 * d + e
                value = ref[c % share, :, column * orbs : (column + 1) * orbs]
                wanted = pattern[c, column] != 0
                if u != tile:
                    wanted = wanted & (gap[u] == e)
                return value, wanted

            if u == tile:
                value, wanted = at(1)
                return jnp.where(wanted, value, zero)
            low, want_low = at(0)
            high, want_high = at(2)
            return jnp.where(want_low, low, jnp.where(want_high, high, zero))

        turn = even[0] != 0
        for c in range(cells):
            rows = slice(c * orbs, (c + 1) * orbs)
            for u in range(tiles):
                for j in range(cells):
                    at = (u * cells + j) * orbs
                    own[rows, at : at + orbs] = block(c, u, reach + j)
                for j in range(reach):
                    at = (u * reach + j) * orbs
                    left, right = (block(c, u, j), block(c, u, reach + cells + j))
                    first[rows, at : at + orbs] = jnp.where(turn, right, left)
                    second[rows, at : at + orbs] = jnp.where(turn, left, right)

    for k in range(pieces):

        @pl.when(slot[0] == k)
        def _():
            write([refs[(piece - k) % pieces] for piece in range(pieces)])


def band_rows(tile, parts, pattern, gap, even, slot, sizes, held):
    cells, orbs, reach, tiles, _ = sizes
    rows = cells * orbs
    shapes = [(tiles * rows, tiles * n * orbs) for n in (reach, cells, reach)]
    n_in = 4 + len(parts)
    return pl.pallas_call(
        functools.partial(band_kernel, tile, sizes),
        out_shape=[bf16(*s) for s in shapes],
        grid=(1,),
        in_specs=[SCALAR] * 4
        + [pl.BlockSpec(p.shape, lambda i: (0, 0, 0)) for p in parts]
        + [pl.BlockSpec(memory_space=pl.ANY)] * len(held),
        out_specs=[pl.BlockSpec((rows, s[1]), lambda i: (tile, 0)) for s in shapes],
        input_output_aliases={n_in + i: i for i in range(len(held))},
        compiler_params=PARAMS,
        cost_estimate=cost(4 * rows * tiles * 3 * cells * orbs),
    )(gap, even, slot, pattern, *parts, *held)


def step_kernel(step, width, counts, lanes, kind, info, coef, *refs):
    refs = list(refs)

    def take(n):
        taken = refs[:n]
        del refs[:n]
        return taken

    own, first, second = take(3)
    field, near, far, older, sums, extra = [take(n) for n in counts]

    def parts(group, lane):
        return [ref[:, lane : lane + width] for ref in group]

    image = None
    for band, group, lane in zip((own, first, second), (field, near, far), lanes):
        at = 0
        for value in parts(group, lane[0]):
            depth = value.shape[0]
            term = jnp.dot(
                band[:, at : at + depth], value, preferred_element_type=jnp.float32
            )
            image = term if image is None else image + term
            at += depth

    old = jnp.concatenate(parts(older, lanes[3][0]))
    value = (2.0 * image - old.astype(jnp.float32)).astype(jnp.bfloat16)
    outs = refs
    size = value.shape[0]

    if kind in ("plain", "sum", "before"):
        outs.pop(0)[...] = value
    if kind in ("sum", "sketch", "probe"):
        now = jnp.concatenate(parts(field, lanes[0][0])).astype(jnp.float32)
        total = jnp.concatenate(parts(sums, lanes[4][0]))
        total = total + coef[step - 1] * now
        total = total + coef[step] * value.astype(jnp.float32)
    if kind == "sum":
        tiles = len(outs)
        for i in range(tiles):
            outs[i][...] = total[i * (size // tiles) : (i + 1) * (size // tiles)]
    if kind == "before":
        tiles = len(outs) + 1
        for i in range(1, tiles):
            outs[i - 1][...] = value[i * (size // tiles) : (i + 1) * (size // tiles)]
    if kind in ("sketch", "probe"):
        tiles = len(extra)
        for i in range(tiles):
            outs.pop(0)[...] = value[i * (size // tiles) : (i + 1) * (size // tiles)]
    if kind == "sketch":
        sketched = total.astype(jnp.bfloat16)
        piece = None
        for i, omega in enumerate(extra):
            term = jnp.dot(
                omega[...],
                sketched[i * (size // tiles) : (i + 1) * (size // tiles)],
                preferred_element_type=jnp.float32,
            )
            piece = term if piece is None else piece + term
        keep, send = outs
        high = keep.shape[1]
        for q in range(keep.shape[0]):
            low = piece[2 * q * high : (2 * q + 1) * high]
            top = piece[(2 * q + 1) * high : (2 * q + 2) * high]
            odd = info[0] % 2 == 1
            keep[q] = jnp.where(odd, top, low)
            send[q] = jnp.where(odd, low, top).astype(jnp.bfloat16)
    if kind == "probe":
        signs = jnp.concatenate([ref[...] for ref in extra]).astype(jnp.float32)
        outs[0][...] = jnp.sum(signs * total, axis=0, keepdims=True)


def advance(step, width, kind, info, coef, band, groups, lanes, outs):
    flat = [x for group in groups for x in group]
    rows, depth = band[1].shape
    return pl.pallas_call(
        functools.partial(step_kernel, step, width, [len(group) for group in groups], lanes, kind),
        out_shape=outs,
        in_specs=[SCALAR] * 2 + [WHOLE] * (3 + len(flat)),
        out_specs=[WHOLE] * len(outs),
        compiler_params=PARAMS,
        cost_estimate=cost(6 * rows * depth, 6 * rows * depth * width),
    )(info, coef, band[1], band[0], band[2], *flat)


def program(blocks, pattern, current, previous, accum, coefs, sketch, signs):
    cells, tiles, orbs, wide = blocks.shape
    halves, local_cols = current.shape[3:]
    reach = wide // orbs // 6
    xs, me = (lax.axis_size("xsec"), lax.axis_index("xsec").astype(jnp.int32))
    wires, place = (lax.axis_size("wire"), lax.axis_index("wire").astype(jnp.int32))
    cores, core = (lax.axis_size("cols"), lax.axis_index("cols").astype(jnp.int32))
    width = local_cols // xs
    rows = cells * orbs
    others = range(1, xs)
    assert tiles == 1 and cells == reach and wires % 2 == 0 and cells % cores == 0
    assert halves == 2 and STEPS == 4

    def column_block(x, i):
        return lax.dynamic_slice_in_dim(x, (me - i) % xs * width, width, axis=x.ndim - 1)

    blocks = blocks[:, 0]
    pattern = pattern[:, 0]
    share = cells // cores
    mine = lax.dynamic_slice_in_dim(blocks, core * share, share, axis=0)
    shares = [from_tile(mine, i) for i in others]
    patterns = [pattern] + [from_tile(pattern, i) for i in others]

    by_half = [current[:, 0, :, h].reshape(rows, local_cols) for h in range(halves)]
    dealt = [
        jnp.concatenate([column_block(v, i) for v in by_half], axis=1) for i in range(xs)
    ]
    field = [dealt[0]] + [from_tile(dealt[i], i) for i in others]
    halo = [around(field[0])]
    halo += [around(field[i]) for i in others]

    even = (1 - place % 2)[None]
    band = ()
    for i in range(xs):
        parts, slot, pieces = ([blocks], jnp.zeros((1,), jnp.int32), 1)
        if i > 0:
            parts = [shares[i - 1]]
            parts += [from_tile(shares[i - 1], k, "cols") for k in range(1, cores)]
            slot, pieces = (core[None], cores)
        gap = (me + lax.iota(jnp.int32, xs)) % xs - (me + i) % xs + 1
        sizes = (cells, orbs, reach, xs, pieces)
        band = band_rows(i, parts, patterns[i], gap, even, slot, sizes, band)

    dealt = deal(previous, me[None])
    older = [dealt[0]] + [from_tile(dealt[i], i) for i in others]
    dealt = deal(accum, me[None])
    sums = [dealt[0]] + [from_tile(dealt[i], i) for i in others]
    omega = sketch[:, 0].reshape(rows, sketch.shape[3]).T
    omega = [omega] + [from_tile(omega, i) for i in others]
    signed = (2 * signs[:, 0] - 1).astype(jnp.bfloat16).reshape(rows, local_cols)
    signed = [column_block(signed, 0)] + [from_tile(column_block(signed, i), i) for i in others]

    ranks = sketch.shape[3]
    full = bf16(xs * rows, width)
    piece = bf16(rows, width)
    info = place[None]

    def run(step, kind, field, near, far, older, sums, extra, lanes, outs):
        return advance(
            step, width, kind, info, coefs, band,
            (field, near, far, older, sums, extra), lanes, outs,
        )

    fields, olders, totals = ([None] * halves, [None] * halves, [None] * halves)
    for h in range(halves):
        lane = h * width
        (fields[h],) = run(
            0, "plain", field, [p[0] for p in halo], [p[1] for p in halo], older, [], [],
            ((lane,), (lane,), (lane,), (lane,), ()), [full],
        )
    zero = (0,)
    for h in range(halves):
        lane = (h * width,)
        near, far = around(fields[h])
        nxt, *totals[h] = run(
            1, "sum", [fields[h]], [near], [far], field, sums, [],
            (zero, zero, zero, lane, lane), [full] + [f32(rows, width)] * xs,
        )
        olders[h], fields[h] = (fields[h], nxt)
    befores = [None] * halves
    for h in range(halves):
        near, far = around(fields[h])
        nxt, *befores[h] = run(
            2, "before", [fields[h]], [near], [far], [olders[h]], [], [],
            (zero, zero, zero, zero, ()), [full] + [piece] * (xs - 1),
        )
        olders[h], fields[h] = (fields[h], nxt)
    newest, extras = ([None] * halves, [None] * halves)
    part = (wires // 2, ranks // wires, width)
    ends = [("sketch", omega, [f32(*part), bf16(*part)]), ("probe", signed, [f32(1, width)])]
    for h in range(halves):
        near, far = around(fields[h])
        kind, extra, outs = ends[h]
        results = run(
            3, kind, [fields[h]], [near], [far], [olders[h]], totals[h], extra,
            (zero, zero, zero, zero, zero), [piece] * xs + outs,
        )
        newest[h], extras[h] = (results[:xs], results[xs:])
    (keep, send), (quad,) = extras

    scale = jnp.float32(1.0) / jnp.sqrt(jnp.float32(rows * wires * tiles * xs))
    hop = 1
    while True:
        summed = keep + swap_bits(send, hop).astype(jnp.float32)
        hop *= 2
        if hop == wires:
            break
        split = summed.reshape((-1, 2) + summed.shape[1:])
        bit = (place // hop) % 2
        keep = lax.dynamic_index_in_dim(split, bit, 1, keepdims=False)
        send = lax.dynamic_index_in_dim(split, 1 - bit, 1, keepdims=False).astype(jnp.bfloat16)
    summed = summed[0] * scale
    summed = summed.reshape((xs, summed.shape[0] // xs, width))

    def placed(parts):
        got = [parts[0]] + [to_tile(parts[i], i) for i in others]
        blocks = []
        for b in range(xs):
            block = got[0]
            for i in others:
                block = jnp.where((me - i) % xs == b, got[i], block)
            blocks.append(block)
        return jnp.concatenate(blocks, axis=-1)

    gram = placed(
        [lax.dynamic_index_in_dim(summed, (me + i) % xs, 0, keepdims=False) for i in range(xs)],
    )

    hop = 1
    while hop < wires:
        quad = quad + sum(swap_bits(quad, hop * k) for k in range(1, min(4, wires // hop)))
        hop *= 4
    quadratic = placed([quad * scale] * xs)[0]

    sums_back = [[totals[h][0]] + [to_tile(totals[h][i], i) for i in others] for h in range(halves)]
    before_back = [
        [fields[h]] + [to_tile(befores[h][i - 1], i) for i in others]
        for h in range(halves)
    ]
    newest_back = [
        [newest[h][0]] + [to_tile(newest[h][i], i) for i in others]
        for h in range(halves)
    ]
    shape = current.shape
    before = pl.pallas_call(
        functools.partial(before_kernel, xs),
        out_shape=bf16(*shape),
        in_specs=[SCALAR] + [WHOLE] * (halves * xs),
        out_specs=WHOLE,
        compiler_params=PARAMS,
        cost_estimate=cost(4 * current.size),
    )(me[None], *before_back[0], *before_back[1])
    flat = [x for h in range(halves) for x in newest_back[h] + before_back[h] + sums_back[h]]
    last, total = pl.pallas_call(
        functools.partial(last_kernel, xs),
        out_shape=[bf16(*shape), f32(*shape)],
        in_specs=[SCALAR, SCALAR] + [WHOLE] * len(flat),
        out_specs=[WHOLE, WHOLE],
        compiler_params=PARAMS,
        cost_estimate=cost(16 * current.size),
    )(me[None], coefs, *flat)
    return (last, before, total, gram, quadratic)


def solution(mesh):
    return jax.shard_map(
        program,
        mesh=mesh,
        in_specs=(
            P(("sample", "wire"), "xsec", None, None),
            P(("sample", "wire"), "xsec", None),
            P(("sample", "wire"), "xsec", None, None, "cols"),
            P(("sample", "wire"), "xsec", None, None, "cols"),
            P(("sample", "wire"), "xsec", None, None, "cols"),
            P(),
            P(("sample", "wire"), "xsec", None, None),
            P(("sample", "wire"), "xsec", None, "cols"),
        ),
        out_specs=(
            P(("sample", "wire"), "xsec", None, None, "cols"),
            P(("sample", "wire"), "xsec", None, None, "cols"),
            P(("sample", "wire"), "xsec", None, None, "cols"),
            P(("sample", "wire", "xsec"), "cols"),
            P(("sample", "cols")),
        ),
        check_vma=False,
    )
```

time: 269 us -> 104 us (0.39)
  waiting for transfers between devices: 150 us -> 24.4 us
  matrix products: 26.5 us -> 0 us
  Pallas kernels: 0 us -> 20.3 us
  blocking collectives: 18.4 us -> 0 us
  starting transfers between devices: 29.9 us -> 47.4 us
  between operations: 15 us -> 1 us
  other arithmetic: 12.3 us -> 1.99 us
  local copies, waits for them, and re-layouts: 16.5 us -> 8.44 us
    ppermute x16 -> x37, waiting for transfers between devices: 109 us -> 24.4 us  [the longest x16 13.3 us: from_tile(): lax.ppermute(x, axis, [((i + offset) % size, i) for i in range(size)])]
    unnamed x2 -> x0, waiting for transfers between devices: 40.5 us -> none
    dot_general x109 -> x0, matrix products: 26.5 us -> none  [the longest x108 26.3 us: apply_operator(): jnp.einsum('ctik,ctkn->ctin', part, piece, preferred_element_type=jnp.flo...]
    pallas_call x0 -> x14, Pallas kernels: none -> 20.3 us  [the longest x8 11.1 us: advance(): pl.pallas_call(functools.partial(step_kernel, step, width, [len(group) fo...]
    psum x1 -> x0, blocking collectives: 18.4 us -> none  [body(): quadratic = lax.psum(local_quad, ('wire', 'xsec')) * scale]
    ppermute x16 -> x37, starting transfers between devices: 29.9 us -> 47.4 us  [the longest x16 18.4 us: from_tile(): lax.ppermute(x, axis, [((i + offset) % size, i) for i in range(size)])]
    reshape x4 -> x0, local copies, waits for them, and re-layouts: 5.95 us -> none  [apply_operator(): extended.reshape(cells + 2 * reach, tiles + 2, orbs, halves * local_cols)]
    concatenate x4, other arithmetic: 4.84 us -> 1.23 us  [the longest x2 1.2 us: placed(): return jnp.concatenate(blocks, axis=-1)]
  transfers between devices with their start and end apart: 17 -> 37, of which waited for: 17 -> 9; matrix products, arithmetic and copies ran while one was open for 3% -> 3% of each run, Pallas kernels for 0% -> 20%
where the time goes in v2:
time: 104 us; the launch traced here: 103 us
  starting transfers between devices  47.4 us (46%)
  waiting for transfers between devices  24.4 us (23%)
  Pallas kernels  20.3 us (20%)
  local copies, waits for them, and re-layouts  8.44 us (8%)
  other arithmetic  1.99 us (2%)
    ppermute x16, starting transfers between devices, from_tile(): lax.ppermute(x, axis, [((i + offset) % size, i) for i in range(size)])  18.4 us
    ppermute x8, starting transfers between devices, around(): two = lax.ppermute(x, 'wire', second)  15.6 us
    ppermute x16, waiting for transfers between devices, from_tile(): lax.ppermute(x, axis, [((i + offset) % size, i) for i in range(size)])  13.3 us
    pallas_call x8, Pallas kernels, advance(): pl.pallas_call(functools.partial(step_kernel, step, width, [len(group) fo...  11.1 us
    ppermute x8, starting transfers between devices, around(): one = lax.ppermute(x, 'wire', first)  8.33 us
    ppermute x5, waiting for transfers between devices, swap_bits(): lax.ppermute(x, 'wire', [(i, i ^ hop) for i in range(lax.axis_size('wire'...  6.42 us
    unnamed x42, local copies, waits for them, and re-layouts  5.81 us
    ppermute x5, starting transfers between devices, swap_bits(): lax.ppermute(x, 'wire', [(i, i ^ hop) for i in range(lax.axis_size('wire'...  4.98 us
  transfers between devices with their start and end apart: 37, of which 9 were waited for; matrix products, arithmetic and copies ran while one was open for 3% of the time, Pallas kernels for 20%

profile of v2, /device:TPU:0, one launch (start us, length us, event | category | flops | bytes accessed | tf_op | source)
XLA Modules:
  0.0 103.4 jit_solution(2850707383448349432)
XLA Ops:
  1.7 3.0 %collective-permute-start.1 = (bf16[2,64,1728]{2,1,0:T(8,128)(2,1)S(1)}, bf16[2,64,1728]{2,1,0:T(8,128)(2,1)S(1)}, u32[]{:S(2)}, u32[]{:S(2)}) collective-permute-start(bf16[2,64,1728]{2,1,0:T(8,128)(2,1)S(1)} %dynamic-slice_bitcast_fusion), channel_id=1, source_target_pairs={{2,0},{0,2},{3,1},{1,3},{6,4},{4,6},{7,5},{5,7},{10,8},{8,10},{11,... | collective-permute-start | bytes 1327112 | tf_op jit(solution)/shard_map/ppermute | solution.py:31
  4.8 10.5 %collective-permute-done.1.refs_0_ = bf16[2,64,1728]{2,1,0:T(8,128)(2,1)S(1)} collective-permute-done((bf16[2,64,1728]{2,1,0:T(8,128)(2,1)S(1)}, bf16[2,64,1728]{2,1,0:T(8,128)(2,1)S(1)}, u32[]{:S(2)}, u32[]{:S(2)}) %collective-permute-start.1) | collective-permute-done | bytes 442400 | tf_op jit(solution)/shard_map/ppermute | solution.py:31
  16.3 1.8 %collective-permute-start.3 = (bf16[256,256]{1,0:T(8,128)(2,1)S(1)}, bf16[256,256]{1,0:T(8,128)(2,1)S(1)}, u32[]{:S(2)}, u32[]{:S(2)}) collective-permute-start(bf16[256,256]{1,0:T(8,128)(2,1)S(1)} %pad_maximum_fusion.1), channel_id=1, source_target_pairs={{2,0},{0,2},{3,1},{1,3},{6,4},{4,6},{7,5},{5,7},{10,8},{8,10},{11,... | collective-permute-start | bytes 393224 | tf_op jit(solution)/shard_map/ppermute | solution.py:31
  18.5 1.7 %collective-permute-start.4 = (bf16[256,256]{1,0:T(8,128)(2,1)S(1)}, bf16[256,256]{1,0:T(8,128)(2,1)S(1)}, u32[]{:S(2)}, u32[]{:S(2)}) collective-permute-start(bf16[256,256]{1,0:T(8,128)(2,1)S(1)} %pad_maximum_fusion.refs_3_.refs_6_), channel_id=1, source_target_pairs={{0,4},{4,0},{8,12},{12,8},{1,5},{5,1},{9,13},{13,9},{2,6},{6,2},{1... | collective-permute-start | bytes 393224 | tf_op jit(solution)/shard_map/ppermute | solution.py:45
  20.3 2.5 %collective-permute-start.6 = (bf16[256,256]{1,0:T(8,128)(2,1)S(1)}, bf16[256,256]{1,0:T(8,128)(2,1)S(1)}, u32[]{:S(2)}, u32[]{:S(2)}) collective-permute-start(bf16[256,256]{1,0:T(8,128)(2,1)S(1)} %pad_maximum_fusion.refs_3_.refs_6_), channel_id=1, source_target_pairs={{4,8},{8,4},{12,0},{0,12},{5,9},{9,5},{13,1},{1,13},{6,10},{10,6},... | collective-permute-start | bytes 393224 | tf_op jit(solution)/shard_map/ppermute | solution.py:46
  25.9 1.9 %collective-permute-start.7 = (bf16[256,256]{1,0:T(8,128)(2,1)S(1)}, bf16[256,256]{1,0:T(8,128)(2,1)}, u32[]{:S(2)}, u32[]{:S(2)}) collective-permute-start(bf16[256,256]{1,0:T(8,128)(2,1)S(1)} %collective-permute-done.3.refs_4_.refs_7_), channel_id=1, source_target_pairs={{4,8},{8,4},{12,0},{0,12},{5,9},{9,5},{13,1},{1,13},{6,10},{10,6},... | collective-permute-start | bytes 393224 | tf_op jit(solution)/shard_map/ppermute | solution.py:46
  32.3 2.3 %collective-permute-done.7.refs_8_ = bf16[256,256]{1,0:T(8,128)(2,1)} collective-permute-done((bf16[256,256]{1,0:T(8,128)(2,1)S(1)}, bf16[256,256]{1,0:T(8,128)(2,1)}, u32[]{:S(2)}, u32[]{:S(2)}) %collective-permute-start.7) | collective-permute-done | bytes 131104 | tf_op jit(solution)/shard_map/ppermute | solution.py:46
  35.2 1.5 %shard_map.127.refs_3_.refs_6_ = bf16[512,128]{1,0:T(8,128)(2,1)S(1)} custom-call(s32[1]{0:T(128)} %bitcast.1.info, f32[4]{0:T(128)S(1)} %copy-done.15, bf16[512,512]{1,0:T(8,128)(2,1)S(1)} %get-tuple-element.37.refs_0_, bf16[512,512]{1,0:T(8,128)(2,1)S(1)} %get-tuple-element.38.refs_1_, bf16[512,512]{1,0:T(8,128)(2,1)S(1)} %get-tuple-element.39.refs_2_, ...), custom_call_target="tpu_custom_call" | custom-call | flops 201326592 | bytes 1572864 | tf_op jit(solution)/shard_map/pallas_call | solution.py:268
  37.4 2.6 %collective-permute-start.21 = (bf16[512,128]{1,0:T(8,128)(2,1)S(1)}, bf16[512,128]{1,0:T(8,128)(2,1)}, u32[]{:S(2)}, u32[]{:S(2)}) collective-permute-start(bf16[512,128]{1,0:T(8,128)(2,1)S(1)} %shard_map.127.refs_3_.refs_6_), channel_id=1, source_target_pairs={{4,8},{8,4},{12,0},{0,12},{5,9},{9,5},{13,1},{1,13},{6,10},{10,6},... | collective-permute-start | bytes 393224 | tf_op jit(solution)/shard_map/ppermute | solution.py:46
  40.0 1.5 %shard_map.122.refs_3_.refs_6_ = bf16[512,128]{1,0:T(8,128)(2,1)S(1)} custom-call(s32[1]{0:T(128)} %bitcast.1.info, f32[4]{0:T(128)S(1)} %copy-done.15, bf16[512,512]{1,0:T(8,128)(2,1)S(1)} %get-tuple-element.37.refs_0_, bf16[512,512]{1,0:T(8,128)(2,1)S(1)} %get-tuple-element.38.refs_1_, bf16[512,512]{1,0:T(8,128)(2,1)S(1)} %get-tuple-element.39.refs_2_, ...), custom_call_target="tpu_custom_call" | custom-call | flops 201326592 | bytes 1572864 | tf_op jit(solution)/shard_map/pallas_call | solution.py:268
  47.6 1.5 %shard_map.128 = (bf16[512,128]{1,0:T(8,128)(2,1)S(1)}, f32[256,128]{1,0:T(8,128)S(1)}, f32[256,128]{1,0:T(8,128)S(1)}) custom-call(s32[1]{0:T(128)} %bitcast.1.info, f32[4]{0:T(128)S(1)} %copy-done.15, bf16[512,512]{1,0:T(8,128)(2,1)S(1)} %get-tuple-element.37.refs_0_, bf16[512,512]{1,0:T(8,128)(2,1)S(1)} %get-tuple-element.38.refs_1_, ...), custom_call_target="tpu_custom_call" | custom-call | flops 201326592 | bytes 1572864 | tf_op jit(solution)/shard_map/pallas_call | solution.py:268
  49.1 3.7 %collective-permute-start.22 = (bf16[512,128]{1,0:T(8,128)(2,1)S(1)}, bf16[512,128]{1,0:T(8,128)(2,1)S(1)}, u32[]{:S(2)}, u32[]{:S(2)}) collective-permute-start(bf16[512,128]{1,0:T(8,128)(2,1)S(1)} %get-tuple-element.51.refs_3_.refs_6_), channel_id=1, source_target_pairs={{0,4},{4,0},{8,12},{12,8},{1,5},{5,1},{9,13},{13,9},{2,6},{6,2},{1... | collective-permute-start | bytes 393224 | tf_op jit(solution)/shard_map/ppermute | solution.py:45
  52.9 1.9 %collective-permute-start.23 = (bf16[512,128]{1,0:T(8,128)(2,1)S(1)}, bf16[512,128]{1,0:T(8,128)(2,1)S(1)}, u32[]{:S(2)}, u32[]{:S(2)}) collective-permute-start(bf16[512,128]{1,0:T(8,128)(2,1)S(1)} %get-tuple-element.51.refs_3_.refs_6_), channel_id=1, source_target_pairs={{4,8},{8,4},{12,0},{0,12},{5,9},{9,5},{13,1},{1,13},{6,10},{10,6},... | collective-permute-start | bytes 393224 | tf_op jit(solution)/shard_map/ppermute | solution.py:46
  59.1 2.0 %collective-permute-start.13 = (bf16[512,128]{1,0:T(8,128)(2,1)S(1)}, bf16[512,128]{1,0:T(8,128)(2,1)S(1)}, u32[]{:S(2)}, u32[]{:S(2)}) collective-permute-start(bf16[512,128]{1,0:T(8,128)(2,1)S(1)} %get-tuple-element.44.refs_3_.refs_6_), channel_id=1, source_target_pairs={{4,8},{8,4},{12,0},{0,12},{5,9},{9,5},{13,1},{1,13},{6,10},{10,6},... | collective-permute-start | bytes 393224 | tf_op jit(solution)/shard_map/ppermute | solution.py:46
  62.8 1.6 %collective-permute-start.28 = (bf16[256,128]{1,0:T(8,128)(2,1)S(1)}, bf16[256,128]{1,0:T(8,128)(2,1)S(1)}, u32[]{:S(2)}, u32[]{:S(2)}) collective-permute-start(bf16[256,128]{1,0:T(8,128)(2,1)S(1)} %get-tuple-element.57), channel_id=1, source_target_pairs={{2,0},{0,2},{3,1},{1,3},{6,4},{4,6},{7,5},{5,7},{10,8},{8,10},{11,... | collective-permute-start | bytes 196616 | tf_op jit(solution)/shard_map/ppermute | solution.py:31
  64.4 1.6 %collective-permute-done.13.refs_5_ = bf16[512,128]{1,0:T(8,128)(2,1)S(1)} collective-permute-done((bf16[512,128]{1,0:T(8,128)(2,1)S(1)}, bf16[512,128]{1,0:T(8,128)(2,1)S(1)}, u32[]{:S(2)}, u32[]{:S(2)}) %collective-permute-start.13) | collective-permute-done | bytes 131104 | tf_op jit(solution)/shard_map/ppermute | solution.py:46
  71.5 2.4 %collective-permute-start.15 = (bf16[512,128]{1,0:T(8,128)(2,1)S(1)}, bf16[512,128]{1,0:T(8,128)(2,1)S(1)}, u32[]{:S(2)}, u32[]{:S(2)}) collective-permute-start(bf16[512,128]{1,0:T(8,128)(2,1)S(1)} %get-tuple-element.45.refs_3_.refs_2_.refs_0_), channel_id=1, source_target_pairs={{4,8},{8,4},{12,0},{0,12},{5,9},{9,5},{13,1},{1,13},{6,10},{10,6},... | collective-permute-start | bytes 393224 | tf_op jit(solution)/shard_map/ppermute | solution.py:46
  73.8 1.7 %shard_map.132 = bf16[4,1,64,2,256]{4,3,2,1,0:T(2,128)(2,1)} custom-call(s32[1]{0:T(128)} %bitcast.me, bf16[512,128]{1,0:T(8,128)(2,1)S(1)} %get-tuple-element.45.refs_3_.refs_2_.refs_0_, bf16[256,128]{1,0:T(8,128)(2,1)S(1)} %collective-permute-done.18.refs_3_.refs_1_, bf16[512,128]{1,0:T(8,128)(2,1)S(1)} %get-tuple-element.52.refs_3_.refs_8_.refs_2_, ...), custom_call_target="tpu_custom_call" | custom-call | bytes 524288 | tf_op jit(solution)/shard_map/pallas_call | solution.py:422
  81.3 2.0 %collective-permute-start.35 = (f32[1,128]{1,0:T(1,128)S(1)}, f32[1,128]{1,0:T(1,128)S(1)}, u32[]{:S(2)}, u32[]{:S(2)}) collective-permute-start(f32[1,128]{1,0:T(1,128)S(1)} %get-tuple-element.62), channel_id=1, source_target_pairs={{0,12},{4,8},{8,4},{12,0},{1,13},{5,9},{9,5},{13,1},{2,14},{6,10},... | collective-permute-start | bytes 1544 | tf_op jit(solution)/shard_map/ppermute | solution.py:51
  83.3 2.1 %shard_map.126 = (bf16[256,128]{1,0:T(8,128)(2,1)S(1)}, bf16[256,128]{1,0:T(8,128)(2,1)S(1)}, f32[2,128,128]{2,1,0:T(8,128)S(1)}, bf16[2,128,128]{2,1,0:T(8,128)(2,1)S(1)}) custom-call(s32[1]{0:T(128)} %bitcast.1.info, f32[4]{0:T(128)S(1)} %copy-done.15, bf16[512,512]{1,0:T(8,128)(2,1)S(1)} %get-tuple-element.37.refs_0_, ...), custom_call_target="tpu_custom_call" | custom-call | flops 201326592 | bytes 1572864 | tf_op jit(solution)/shard_map/pallas_call | solution.py:268
  87.7 2.0 %collective-permute-done.30 = bf16[2,128,128]{2,1,0:T(8,128)(2,1)S(1)} collective-permute-done((bf16[2,128,128]{2,1,0:T(8,128)(2,1)S(1)}, bf16[2,128,128]{2,1,0:T(8,128)(2,1)S(1)}, u32[]{:S(2)}, u32[]{:S(2)}) %collective-permute-start.30) | collective-permute-done | bytes 65568 | tf_op jit(solution)/shard_map/ppermute | solution.py:51
  90.9 2.4 %collective-permute-done.36 = f32[1,128]{1,0:T(1,128)S(1)} collective-permute-done((f32[1,128]{1,0:T(1,128)S(1)}, f32[1,128]{1,0:T(1,128)S(1)}, u32[]{:S(2)}, u32[]{:S(2)}) %collective-permute-start.36) | collective-permute-done | bytes 544 | tf_op jit(solution)/shard_map/ppermute | solution.py:31
  93.6 4.4 %collective-permute-done.31 = bf16[1,128,128]{2,1,0:T(8,128)(2,1)S(1)} collective-permute-done((bf16[1,128,128]{2,1,0:T(8,128)(2,1)S(1)}, bf16[1,128,128]{2,1,0:T(8,128)(2,1)S(1)}, u32[]{:S(2)}, u32[]{:S(2)}) %collective-permute-start.31) | collective-permute-done | bytes 32800 | tf_op jit(solution)/shard_map/ppermute | solution.py:51
  99.9 2.9 %shard_map.131 = (bf16[4,1,64,2,256]{4,3,2,1,0:T(2,128)(2,1)}, f32[4,1,64,2,256]{4,3,2,1,0:T(2,128)}) custom-call(s32[1]{0:T(128)} %bitcast.me, f32[4]{0:T(128)S(1)} %copy-done.15, bf16[256,128]{1,0:T(8,128)(2,1)S(1)} %get-tuple-element.48.refs_0_, bf16[256,128]{1,0:T(8,128)(2,1)S(1)} %collective-permute-done.17.refs_1_, ...), custom_call_target="tpu_custom_call" | custom-call | bytes 2097152 | tf_op jit(solution)/shard_map/pallas_call | solution.py:431
  (125 shorter events, 40.8 us)
Async XLA Ops:
  1.7 13.6 %collective-permute-start.1 = (bf16[2,64,1728]{2,1,0:T(8,128)(2,1)S(1)}, bf16[2,64,1728]{2,1,0:T(8,128)(2,1)S(1)}, u32[]{:S(2)}, u32[]{:S(2)}) collective-permute-start(bf16[2,64,1728]{2,1,0:T(8,128)(2,1)S(1)} %dynamic-slice_bitcast_fusion), channel_id=1, source_target_pairs={{2,0},{0,2},{3,1},{1,3},{6,4},{4,6},{7,5},{5,7},{10,8},{8,10},{11,... | collective-permute-start | bytes 1327112 | tf_op jit(solution)/shard_map/ppermute | solution.py:31
  15.3 10.6 %collective-permute-start.2 = (bf16[2,64,1728]{2,1,0:T(8,128)(2,1)S(1)}, bf16[2,64,1728]{2,1,0:T(8,128)(2,1)S(1)}, u32[]{:S(2)}, u32[]{:S(2)}) collective-permute-start(bf16[2,64,1728]{2,1,0:T(8,128)(2,1)S(1)} %collective-permute-done.1.refs_0_), channel_id=1, source_target_pairs={{1,0},{0,1},{3,2},{2,3},{5,4},{4,5},{7,6},{6,7},{9,8},{8,9},{11,10... | collective-permute-start | bytes 1327112 | tf_op jit(solution)/shard_map/ppermute | solution.py:31
  16.3 8.9 %collective-permute-start.3 = (bf16[256,256]{1,0:T(8,128)(2,1)S(1)}, bf16[256,256]{1,0:T(8,128)(2,1)S(1)}, u32[]{:S(2)}, u32[]{:S(2)}) collective-permute-start(bf16[256,256]{1,0:T(8,128)(2,1)S(1)} %pad_maximum_fusion.1), channel_id=1, source_target_pairs={{2,0},{0,2},{3,1},{1,3},{6,4},{4,6},{7,5},{5,7},{10,8},{8,10},{11,... | collective-permute-start | bytes 393224 | tf_op jit(solution)/shard_map/ppermute | solution.py:31
  18.5 12.9 %collective-permute-start.4 = (bf16[256,256]{1,0:T(8,128)(2,1)S(1)}, bf16[256,256]{1,0:T(8,128)(2,1)S(1)}, u32[]{:S(2)}, u32[]{:S(2)}) collective-permute-start(bf16[256,256]{1,0:T(8,128)(2,1)S(1)} %pad_maximum_fusion.refs_3_.refs_6_), channel_id=1, source_target_pairs={{0,4},{4,0},{8,12},{12,8},{1,5},{5,1},{9,13},{13,9},{2,6},{6,2},{1... | collective-permute-start | bytes 393224 | tf_op jit(solution)/shard_map/ppermute | solution.py:45
  20.3 11.8 %collective-permute-start.6 = (bf16[256,256]{1,0:T(8,128)(2,1)S(1)}, bf16[256,256]{1,0:T(8,128)(2,1)S(1)}, u32[]{:S(2)}, u32[]{:S(2)}) collective-permute-start(bf16[256,256]{1,0:T(8,128)(2,1)S(1)} %pad_maximum_fusion.refs_3_.refs_6_), channel_id=1, source_target_pairs={{4,8},{8,4},{12,0},{0,12},{5,9},{9,5},{13,1},{1,13},{6,10},{10,6},... | collective-permute-start | bytes 393224 | tf_op jit(solution)/shard_map/ppermute | solution.py:46
  23.7 8.3 %collective-permute-start.8 = (bf16[256,256]{1,0:T(8,128)(2,1)}, bf16[256,256]{1,0:T(8,128)(2,1)S(1)}, u32[]{:S(2)}, u32[]{:S(2)}) collective-permute-start(bf16[256,256]{1,0:T(8,128)(2,1)} %get-tuple-element.41), channel_id=1, source_target_pairs={{2,0},{0,2},{3,1},{1,3},{6,4},{4,6},{7,5},{5,7},{10,8},{8,10},{11,... | collective-permute-start | bytes 393224 | tf_op jit(solution)/shard_map/ppermute | solution.py:31
  25.9 8.7 %collective-permute-start.7 = (bf16[256,256]{1,0:T(8,128)(2,1)S(1)}, bf16[256,256]{1,0:T(8,128)(2,1)}, u32[]{:S(2)}, u32[]{:S(2)}) collective-permute-start(bf16[256,256]{1,0:T(8,128)(2,1)S(1)} %collective-permute-done.3.refs_4_.refs_7_), channel_id=1, source_target_pairs={{4,8},{8,4},{12,0},{0,12},{5,9},{9,5},{13,1},{1,13},{6,10},{10,6},... | collective-permute-start | bytes 393224 | tf_op jit(solution)/shard_map/ppermute | solution.py:46
  31.4 13.2 %collective-permute-start.11 = (f32[256,256]{1,0:T(8,128)}, f32[256,256]{1,0:T(8,128)S(1)}, u32[]{:S(2)}, u32[]{:S(2)}) collective-permute-start(f32[256,256]{1,0:T(8,128)} %get-tuple-element.43), channel_id=1, source_target_pairs={{2,0},{0,2},{3,1},{1,3},{6,4},{4,6},{7,5},{5,7},{10,8},{8,10},{11,... | collective-permute-start | bytes 786440 | tf_op jit(solution)/shard_map/ppermute | solution.py:31
  36.8 9.3 %collective-permute-start.20 = (bf16[512,128]{1,0:T(8,128)(2,1)S(1)}, bf16[512,128]{1,0:T(8,128)(2,1)S(1)}, u32[]{:S(2)}, u32[]{:S(2)}) collective-permute-start(bf16[512,128]{1,0:T(8,128)(2,1)S(1)} %shard_map.127.refs_3_.refs_6_), channel_id=1, source_target_pairs={{0,4},{4,0},{8,12},{12,8},{1,5},{5,1},{9,13},{13,9},{2,6},{6,2},{1... | collective-permute-start | bytes 393224 | tf_op jit(solution)/shard_map/ppermute | solution.py:45
  37.4 9.3 %collective-permute-start.21 = (bf16[512,128]{1,0:T(8,128)(2,1)S(1)}, bf16[512,128]{1,0:T(8,128)(2,1)}, u32[]{:S(2)}, u32[]{:S(2)}) collective-permute-start(bf16[512,128]{1,0:T(8,128)(2,1)S(1)} %shard_map.127.refs_3_.refs_6_), channel_id=1, source_target_pairs={{4,8},{8,4},{12,0},{0,12},{5,9},{9,5},{13,1},{1,13},{6,10},{10,6},... | collective-permute-start | bytes 393224 | tf_op jit(solution)/shard_map/ppermute | solution.py:46
  41.6 13.1 %collective-permute-start.10 = (bf16[512,128]{1,0:T(8,128)(2,1)S(1)}, bf16[512,128]{1,0:T(8,128)(2,1)S(1)}, u32[]{:S(2)}, u32[]{:S(2)}) collective-permute-start(bf16[512,128]{1,0:T(8,128)(2,1)S(1)} %shard_map.122.refs_3_.refs_6_), channel_id=1, source_target_pairs={{4,8},{8,4},{12,0},{0,12},{5,9},{9,5},{13,1},{1,13},{6,10},{10,6},... | collective-permute-start | bytes 393224 | tf_op jit(solution)/shard_map/ppermute | solution.py:46
  42.8 12.5 %collective-permute-start.9 = (bf16[512,128]{1,0:T(8,128)(2,1)S(1)}, bf16[512,128]{1,0:T(8,128)(2,1)S(1)}, u32[]{:S(2)}, u32[]{:S(2)}) collective-permute-start(bf16[512,128]{1,0:T(8,128)(2,1)S(1)} %shard_map.122.refs_3_.refs_6_), channel_id=1, source_target_pairs={{0,4},{4,0},{8,12},{12,8},{1,5},{5,1},{9,13},{13,9},{2,6},{6,2},{1... | collective-permute-start | bytes 393224 | tf_op jit(solution)/shard_map/ppermute | solution.py:45
  44.6 34.1 %collective-permute-start.16 = (bf16[512,256]{1,0:T(8,128)(2,1)S(1)}, bf16[512,256]{1,0:T(8,128)(2,1)}, u32[]{:S(2)}, u32[]{:S(2)}) collective-permute-start(bf16[512,256]{1,0:T(8,128)(2,1)S(1)} %bitcast.21), channel_id=1, source_target_pairs={{2,0},{0,2},{3,1},{1,3},{6,4},{4,6},{7,5},{5,7},{10,8},{8,10},{11,... | collective-permute-start | bytes 786440 | tf_op jit(solution)/shard_map/ppermute | solution.py:31
  49.1 12.0 %collective-permute-start.22 = (bf16[512,128]{1,0:T(8,128)(2,1)S(1)}, bf16[512,128]{1,0:T(8,128)(2,1)S(1)}, u32[]{:S(2)}, u32[]{:S(2)}) collective-permute-start(bf16[512,128]{1,0:T(8,128)(2,1)S(1)} %get-tuple-element.51.refs_3_.refs_6_), channel_id=1, source_target_pairs={{0,4},{4,0},{8,12},{12,8},{1,5},{5,1},{9,13},{13,9},{2,6},{6,2},{1... | collective-permute-start | bytes 393224 | tf_op jit(solution)/shard_map/ppermute | solution.py:45
  52.9 8.8 %collective-permute-start.23 = (bf16[512,128]{1,0:T(8,128)(2,1)S(1)}, bf16[512,128]{1,0:T(8,128)(2,1)S(1)}, u32[]{:S(2)}, u32[]{:S(2)}) collective-permute-start(bf16[512,128]{1,0:T(8,128)(2,1)S(1)} %get-tuple-element.51.refs_3_.refs_6_), channel_id=1, source_target_pairs={{4,8},{8,4},{12,0},{0,12},{5,9},{9,5},{13,1},{1,13},{6,10},{10,6},... | collective-permute-start | bytes 393224 | tf_op jit(solution)/shard_map/ppermute | solution.py:46
  61.1 8.8 %collective-permute-start.26 = (bf16[256,128]{1,0:T(8,128)(2,1)S(1)}, bf16[256,128]{1,0:T(8,128)(2,1)S(1)}, u32[]{:S(2)}, u32[]{:S(2)}) collective-permute-start(bf16[256,128]{1,0:T(8,128)(2,1)S(1)} %get-tuple-element.65), channel_id=1, source_target_pairs={{2,0},{0,2},{3,1},{1,3},{6,4},{4,6},{7,5},{5,7},{10,8},{8,10},{11,... | collective-permute-start | bytes 196616 | tf_op jit(solution)/shard_map/ppermute | solution.py:31
  62.8 8.3 %collective-permute-start.28 = (bf16[256,128]{1,0:T(8,128)(2,1)S(1)}, bf16[256,128]{1,0:T(8,128)(2,1)S(1)}, u32[]{:S(2)}, u32[]{:S(2)}) collective-permute-start(bf16[256,128]{1,0:T(8,128)(2,1)S(1)} %get-tuple-element.57), channel_id=1, source_target_pairs={{2,0},{0,2},{3,1},{1,3},{6,4},{4,6},{7,5},{5,7},{10,8},{8,10},{11,... | collective-permute-start | bytes 196616 | tf_op jit(solution)/shard_map/ppermute | solution.py:31
  68.5 7.1 %collective-permute-start.24 = (bf16[512,128]{1,0:T(8,128)(2,1)S(1)}, bf16[512,128]{1,0:T(8,128)(2,1)S(1)}, u32[]{:S(2)}, u32[]{:S(2)}) collective-permute-start(bf16[512,128]{1,0:T(8,128)(2,1)S(1)} %get-tuple-element.52.refs_3_.refs_8_.refs_2_), channel_id=1, source_target_pairs={{0,4},{4,0},{8,12},{12,8},{1,5},{5,1},{9,13},{13,9},{2,6},{6,2},{1... | collective-permute-start | bytes 393224 | tf_op jit(solution)/shard_map/ppermute | solution.py:45
  71.1 8.8 %collective-permute-start.14 = (bf16[512,128]{1,0:T(8,128)(2,1)S(1)}, bf16[512,128]{1,0:T(8,128)(2,1)S(1)}, u32[]{:S(2)}, u32[]{:S(2)}) collective-permute-start(bf16[512,128]{1,0:T(8,128)(2,1)S(1)} %get-tuple-element.45.refs_3_.refs_2_.refs_0_), channel_id=1, source_target_pairs={{0,4},{4,0},{8,12},{12,8},{1,5},{5,1},{9,13},{13,9},{2,6},{6,2},{1... | collective-permute-start | bytes 393224 | tf_op jit(solution)/shard_map/ppermute | solution.py:45
  71.5 9.8 %collective-permute-start.15 = (bf16[512,128]{1,0:T(8,128)(2,1)S(1)}, bf16[512,128]{1,0:T(8,128)(2,1)S(1)}, u32[]{:S(2)}, u32[]{:S(2)}) collective-permute-start(bf16[512,128]{1,0:T(8,128)(2,1)S(1)} %get-tuple-element.45.refs_3_.refs_2_.refs_0_), channel_id=1, source_target_pairs={{4,8},{8,4},{12,0},{0,12},{5,9},{9,5},{13,1},{1,13},{6,10},{10,6},... | collective-permute-start | bytes 393224 | tf_op jit(solution)/shard_map/ppermute | solution.py:46
  75.6 24.3 %collective-permute-start.29 = (f32[256,128]{1,0:T(8,128)S(1)}, f32[256,128]{1,0:T(8,128)S(1)}, u32[]{:S(2)}, u32[]{:S(2)}) collective-permute-start(f32[256,128]{1,0:T(8,128)S(1)} %get-tuple-element.54.refs_8_), channel_id=1, source_target_pairs={{2,0},{0,2},{3,1},{1,3},{6,4},{4,6},{7,5},{5,7},{10,8},{8,10},{11,... | collective-permute-start | bytes 393224 | tf_op jit(solution)/shard_map/ppermute | solution.py:31
  76.8 23.1 %collective-permute-start.19 = (f32[256,128]{1,0:T(8,128)S(1)}, f32[256,128]{1,0:T(8,128)S(1)}, u32[]{:S(2)}, u32[]{:S(2)}) collective-permute-start(f32[256,128]{1,0:T(8,128)S(1)} %copy-done.14), channel_id=1, source_target_pairs={{2,0},{0,2},{3,1},{1,3},{6,4},{4,6},{7,5},{5,7},{10,8},{8,10},{11,... | collective-permute-start | bytes 393224 | tf_op jit(solution)/shard_map/ppermute | solution.py:31
  85.5 14.4 %collective-permute-start.27 = (bf16[256,128]{1,0:T(8,128)(2,1)S(1)}, bf16[256,128]{1,0:T(8,128)(2,1)S(1)}, u32[]{:S(2)}, u32[]{:S(2)}) collective-permute-start(bf16[256,128]{1,0:T(8,128)(2,1)S(1)} %get-tuple-element.56), channel_id=1, source_target_pairs={{2,0},{0,2},{3,1},{1,3},{6,4},{4,6},{7,5},{5,7},{10,8},{8,10},{11,... | collective-permute-start | bytes 196616 | tf_op jit(solution)/shard_map/ppermute | solution.py:31
  86.6 13.2 %collective-permute-start.17 = (bf16[256,128]{1,0:T(8,128)(2,1)S(1)}, bf16[256,128]{1,0:T(8,128)(2,1)S(1)}, u32[]{:S(2)}, u32[]{:S(2)}) collective-permute-start(bf16[256,128]{1,0:T(8,128)(2,1)S(1)} %get-tuple-element.49), channel_id=1, source_target_pairs={{2,0},{0,2},{3,1},{1,3},{6,4},{4,6},{7,5},{5,7},{10,8},{8,10},{11,... | collective-permute-start | bytes 196616 | tf_op jit(solution)/shard_map/ppermute | solution.py:31
  (33 other events, 154.9 us)

commit v3 on v2

--- a/solution.py
+++ b/solution.py
@@ -78,6 +78,44 @@
         compiler_params=PARAMS,
         cost_estimate=cost(2 * x.size * x.dtype.itemsize),
     )(me, x)
+
+
+def stack_kernel(*refs):
+    count = refs[-1].shape[0] // refs[0].shape[0]
+    ins, outs = (refs[:count], refs[count:])
+    rows, width = (ins[0].shape[0], outs[0].shape[1])
+    for h, out in enumerate(outs):
+        for i, ref in enumerate(ins):
+            out[i * rows : (i + 1) * rows] = ref[:, h * width : (h + 1) * width]
+
+
+def stacked(parts, width):
+    rows, columns = parts[0].shape
+    shape = bf16(len(parts) * rows, width)
+    return pl.pallas_call(
+        stack_kernel,
+        out_shape=[shape] * (columns // width),
+        in_specs=[WHOLE] * len(parts),
+        out_specs=[WHOLE] * (columns // width),
+        compiler_params=PARAMS,
+        cost_estimate=cost(4 * len(parts) * rows * columns),
+    )(*parts)
+
+
+def rest_kernel(me, sketch, signs, turned, *outs):
+    cells, _, orbs, ranks = sketch.shape
+    count = len(outs)
+    columns = signs.shape[3]
+    width = columns // count
+    value = sketch[...].reshape(cells * orbs, ranks)
+    turned[...] = value.astype(jnp.float32).T.astype(jnp.bfloat16)
+    value = (2 * signs[...] - 1).astype(jnp.float32).reshape(cells * orbs, columns)
+    for i in range(count):
+        picked = value[:, :width]
+        for b in range(1, count):
+            block = value[:, b * width : (b + 1) * width]
+            picked = jnp.where((me[0] - i + count) % count == b, block, picked)
+        outs[i][...] = picked.astype(jnp.bfloat16)
 
 
 def before_kernel(count, me, *refs):
@@ -122,12 +160,54 @@
             summed[:, 0, :, h, columns_at] = sums.reshape(shape)
 
 
+def pack_kernel(core, me, pattern, blocks, out):
+    share, orbs, wide = blocks.shape
+    span = wide // orbs // 3
+    slots = out.shape[2] // orbs // span
+    zero = jnp.zeros((orbs, orbs), jnp.bfloat16)
+    for c in range(share):
+        cell = core[0] * share + c
+
+        def block(d, e):
+            column = 3 * d + e
+            value = blocks[c, :, column * orbs : (column + 1) * orbs]
+            return jnp.where(pattern[cell, column] != 0, value, zero)
+
+        for d in range(span):
+            values = [block(d, e) for e in range(3)]
+            if slots == 2:
+                values = [values[1], jnp.where(me[0] == 0, values[2], values[0])]
+            for n, value in enumerate(values):
+                at = (slots * d + n) * orbs
+                out[c, :, at : at + orbs] = value
+
+
+def packed(blocks, pattern, core, me, cores, slots):
+    cells, orbs, wide = blocks.shape
+    share = cells // cores
+    shape = (share, orbs, wide // 3 * slots)
+    return pl.pallas_call(
+        pack_kernel,
+        out_shape=bf16(*shape),
+        grid_spec=pltpu.PrefetchScalarGridSpec(
+            num_scalar_prefetch=3,
+            grid=(1,),
+            in_specs=[pl.BlockSpec((share, orbs, wide), lambda i, core, me, p: (core[0], 0, 0))],
+            out_specs=pl.BlockSpec(shape, lambda i, core, me, p: (0, 0, 0)),
+        ),
+        compiler_params=PARAMS,
+        cost_estimate=cost(4 * share * orbs * wide),
+    )(core, me, pattern, blocks)
+
+
 def band_kernel(tile, sizes, gap, even, slot, pattern, *refs):
     cells, orbs, reach, tiles, pieces = sizes
     first, own, second = refs[-3:]
     share = cells // pieces
     span = 2 * reach + 1
     zero = jnp.zeros((orbs, orbs), jnp.bfloat16)
+    slots = refs[0].shape[2] // orbs // span
+    masked = tile == 0
 
     def write(parts):
         def block(c, u, x):
@@ -137,19 +217,17 @@
             ref = parts[c // share]
 
             def at(e):
-                column = 3 * d + e
+                column = slots * d + e
                 value = ref[c % share, :, column * orbs : (column + 1) * orbs]
-                wanted = pattern[c, column] != 0
-                if u != tile:
-                    wanted = wanted & (gap[u] == e)
-                return value, wanted
-
+                if masked:
+                    value = jnp.where(pattern[c, column] != 0, value, zero)
+                return value
+
+            if slots == 2:
+                return at(0 if u == tile else 1)
             if u == tile:
-                value, wanted = at(1)
-                return jnp.where(wanted, value, zero)
-            low, want_low = at(0)
-            high, want_high = at(2)
-            return jnp.where(want_low, low, jnp.where(want_high, high, zero))
+                return at(1)
+            return jnp.where(gap[u] == 0, at(0), jnp.where(gap[u] == 2, at(2), zero))
 
         turn = even[0] != 0
         for c in range(cells):
@@ -275,6 +353,72 @@
     )(info, coef, band[1], band[0], band[2], *flat)
 
 
+def fold_kernel(hop, place, keep, got, kept, send):
+    odd = (place[0] // hop) % 2 == 1
+    for q in range(kept.shape[0]):
+        low = keep[2 * q] + got[2 * q].astype(jnp.float32)
+        top = keep[2 * q + 1] + got[2 * q + 1].astype(jnp.float32)
+        kept[q] = jnp.where(odd, top, low)
+        send[q] = jnp.where(odd, low, top).astype(jnp.bfloat16)
+
+
+def mix_kernel(send, *refs):
+    terms, (quad, out) = (refs[:-2], refs[-2:])
+    rows = send.shape[1]
+    total = terms[0][...]
+    for term in terms[1:]:
+        total = total + term[...]
+    quad[...] = total
+    high = total.astype(jnp.bfloat16)
+    low = (total - high.astype(jnp.float32)).astype(jnp.bfloat16)
+    spare = out.shape[0] - rows - 2
+    pad = jnp.zeros((spare, total.shape[1]), jnp.float32)
+    tail = jnp.concatenate([high.astype(jnp.float32), low.astype(jnp.float32), pad])
+    out[:rows] = send[0]
+    out[rows:] = tail.astype(jnp.bfloat16)
+
+
+def finish_kernel(scale, me, keep, got, quad, *outs):
+    rows = keep.shape[1]
+    count = len(outs)
+    share = rows // count
+    tail = got[rows:].astype(jnp.float32)
+    total = (quad[...] + tail[0:1] + tail[1:2]) * scale
+    spare = jnp.zeros((outs[0].shape[0] - share - 1, total.shape[1]), jnp.float32)
+    gram = (keep[0] + got[:rows].astype(jnp.float32)) * scale
+    for i in range(count):
+        picked = gram[:share]
+        for b in range(1, count):
+            here = (me[0] + i) % count == b
+            picked = jnp.where(here, gram[b * share : (b + 1) * share], picked)
+        outs[i][:share] = picked
+        outs[i][share:] = jnp.concatenate([total, spare])
+
+
+def place_kernel(me, *refs):
+    parts, (gram, quad) = (refs[:-2], refs[-2:])
+    count = len(parts)
+    share, columns = gram.shape
+    width = columns // count
+    for b in range(count):
+        value = parts[0][...]
+        for i in range(1, count):
+            value = jnp.where((me[0] - i + count) % count == b, parts[i][...], value)
+        gram[:, b * width : (b + 1) * width] = value[:share]
+        quad[:, b * width : (b + 1) * width] = value[share : share + 1]
+
+
+def small(kernel, scalars, arrays, outs):
+    return pl.pallas_call(
+        kernel,
+        out_shape=outs,
+        in_specs=[SCALAR] * len(scalars) + [WHOLE] * len(arrays),
+        out_specs=[WHOLE] * len(outs),
+        compiler_params=PARAMS,
+        cost_estimate=cost(sum(4 * x.size for x in arrays)),
+    )(*scalars, *arrays)
+
+
 def program(blocks, pattern, current, previous, accum, coefs, sketch, signs):
     cells, tiles, orbs, wide = blocks.shape
     halves, local_cols = current.shape[3:]
@@ -291,20 +435,16 @@
     def column_block(x, i):
         return lax.dynamic_slice_in_dim(x, (me - i) % xs * width, width, axis=x.ndim - 1)
 
-    blocks = blocks[:, 0]
-    pattern = pattern[:, 0]
-    share = cells // cores
-    mine = lax.dynamic_slice_in_dim(blocks, core * share, share, axis=0)
-    shares = [from_tile(mine, i) for i in others]
-    patterns = [pattern] + [from_tile(pattern, i) for i in others]
-
     by_half = [current[:, 0, :, h].reshape(rows, local_cols) for h in range(halves)]
     dealt = [
         jnp.concatenate([column_block(v, i) for v in by_half], axis=1) for i in range(xs)
     ]
-    field = [dealt[0]] + [from_tile(dealt[i], i) for i in others]
-    halo = [around(field[0])]
-    halo += [around(field[i]) for i in others]
+    fields = stacked([dealt[0]] + [from_tile(dealt[i], i) for i in others], width)
+
+    blocks = blocks[:, 0]
+    pattern = pattern[:, 0]
+    mine = packed(blocks, pattern, core[None], me[None], cores, min(xs, 3))
+    shares = [from_tile(mine, i) for i in others]
 
     even = (1 - place % 2)[None]
     band = ()
@@ -316,21 +456,25 @@
             slot, pieces = (core[None], cores)
         gap = (me + lax.iota(jnp.int32, xs)) % xs - (me + i) % xs + 1
         sizes = (cells, orbs, reach, xs, pieces)
-        band = band_rows(i, parts, patterns[i], gap, even, slot, sizes, band)
+        band = band_rows(i, parts, pattern, gap, even, slot, sizes, band)
 
     dealt = deal(previous, me[None])
     older = [dealt[0]] + [from_tile(dealt[i], i) for i in others]
     dealt = deal(accum, me[None])
     sums = [dealt[0]] + [from_tile(dealt[i], i) for i in others]
-    omega = sketch[:, 0].reshape(rows, sketch.shape[3]).T
-    omega = [omega] + [from_tile(omega, i) for i in others]
-    signed = (2 * signs[:, 0] - 1).astype(jnp.bfloat16).reshape(rows, local_cols)
-    signed = [column_block(signed, 0)] + [from_tile(column_block(signed, i), i) for i in others]
-
     ranks = sketch.shape[3]
+    turned, *signed = small(
+        rest_kernel, [me[None]], [sketch, signs],
+        [bf16(ranks, rows)] + [bf16(rows, width)] * xs,
+    )
+    omega = [turned] + [from_tile(turned, i) for i in others]
+    signed = [signed[0]] + [from_tile(signed[i], i) for i in others]
+
     full = bf16(xs * rows, width)
     piece = bf16(rows, width)
     info = place[None]
+
+    fields = list(fields)
 
     def run(step, kind, field, near, far, older, sums, extra, lanes, outs):
         return advance(
@@ -338,20 +482,22 @@
             (field, near, far, older, sums, extra), lanes, outs,
         )
 
-    fields, olders, totals = ([None] * halves, [None] * halves, [None] * halves)
-    for h in range(halves):
-        lane = h * width
-        (fields[h],) = run(
-            0, "plain", field, [p[0] for p in halo], [p[1] for p in halo], older, [], [],
-            ((lane,), (lane,), (lane,), (lane,), ()), [full],
-        )
+    olders, totals = ([None] * halves, [None] * halves)
     zero = (0,)
     for h in range(halves):
         lane = (h * width,)
         near, far = around(fields[h])
+        (nxt,) = run(
+            0, "plain", [fields[h]], [near], [far], older, [], [],
+            (zero, zero, zero, lane, ()), [full],
+        )
+        olders[h], fields[h] = (fields[h], nxt)
+    for h in range(halves):
+        lane = (h * width,)
+        near, far = around(fields[h])
         nxt, *totals[h] = run(
-            1, "sum", [fields[h]], [near], [far], field, sums, [],
-            (zero, zero, zero, lane, lane), [full] + [f32(rows, width)] * xs,
+            1, "sum", [fields[h]], [near], [far], [olders[h]], sums, [],
+            (zero, zero, zero, zero, lane), [full] + [f32(rows, width)] * xs,
         )
         olders[h], fields[h] = (fields[h], nxt)
     befores = [None] * halves
@@ -375,39 +521,31 @@
         newest[h], extras[h] = (results[:xs], results[xs:])
     (keep, send), (quad,) = extras
 
-    scale = jnp.float32(1.0) / jnp.sqrt(jnp.float32(rows * wires * tiles * xs))
     hop = 1
-    while True:
-        summed = keep + swap_bits(send, hop).astype(jnp.float32)
+    high = ranks // wires
+    terms = [quad]
+    while 2 * hop < wires:
+        got = swap_bits(send, hop)
+        terms = [sum(terms[1:], terms[0])]
+        terms.append(swap_bits(terms[0], hop))
         hop *= 2
-        if hop == wires:
-            break
-        split = summed.reshape((-1, 2) + summed.shape[1:])
-        bit = (place // hop) % 2
-        keep = lax.dynamic_index_in_dim(split, bit, 1, keepdims=False)
-        send = lax.dynamic_index_in_dim(split, 1 - bit, 1, keepdims=False).astype(jnp.bfloat16)
-    summed = summed[0] * scale
-    summed = summed.reshape((xs, summed.shape[0] // xs, width))
-
-    def placed(parts):
-        got = [parts[0]] + [to_tile(parts[i], i) for i in others]
-        blocks = []
-        for b in range(xs):
-            block = got[0]
-            for i in others:
-                block = jnp.where((me - i) % xs == b, got[i], block)
-            blocks.append(block)
-        return jnp.concatenate(blocks, axis=-1)
-
-    gram = placed(
-        [lax.dynamic_index_in_dim(summed, (me + i) % xs, 0, keepdims=False) for i in range(xs)],
+        part = (wires // hop // 2, high, width)
+        keep, send = small(
+            functools.partial(fold_kernel, hop), [info], [keep, got],
+            [f32(*part), bf16(*part)],
+        )
+    quad, mixed = small(mix_kernel, [], [send, *terms], [f32(1, width), bf16(high + 16, width)])
+    mixed = swap_bits(mixed, hop)
+    scale = 1.0 / float(rows * wires * tiles * xs) ** 0.5
+    finished = small(
+        functools.partial(finish_kernel, scale), [me[None]], [keep, mixed, quad],
+        [f32(high // xs + 8, width)] * xs,
     )
-
-    hop = 1
-    while hop < wires:
-        quad = quad + sum(swap_bits(quad, hop * k) for k in range(1, min(4, wires // hop)))
-        hop *= 4
-    quadratic = placed([quad * scale] * xs)[0]
+    finished = [finished[0]] + [to_tile(finished[i], i) for i in others]
+    gram, quadratic = small(
+        place_kernel, [me[None]], finished, [f32(high // xs, local_cols), f32(1, local_cols)]
+    )
+    quadratic = quadratic[0]
 
     sums_back = [[totals[h][0]] + [to_tile(totals[h][i], i) for i in others] for h in range(halves)]
     before_back = [

time: 104 us -> 89.7 us (0.86)
  local copies, waits for them, and re-layouts: 8.44 us -> 2.99 us
  waiting for transfers between devices: 24.4 us -> 20.3 us
  other arithmetic: 1.99 us -> 0.06 us
  starting transfers between devices: 47.4 us -> 45.9 us
    ppermute x16 -> x14, waiting for transfers between devices: 13.3 us -> 8.65 us  [from_tile(): lax.ppermute(x, axis, [((i + offset) % size, i) for i in range(size)])]
    ppermute x5 -> x3, waiting for transfers between devices: 6.42 us -> 2.16 us  [swap_bits(): lax.ppermute(x, 'wire', [(i, i ^ hop) for i in range(lax.axis_size('wire'...]
    ppermute x8, waiting for transfers between devices: 4.35 us -> 8.56 us  [around(): two = lax.ppermute(x, 'wire', second)]
    ppermute x8, starting transfers between devices: 15.6 us -> 19.1 us  [around(): two = lax.ppermute(x, 'wire', second)]
    unnamed x42 -> x20, local copies, waits for them, and re-layouts: 5.81 us -> 2.58 us
    ppermute x8, starting transfers between devices: 8.33 us -> 5.13 us  [around(): one = lax.ppermute(x, 'wire', first)]
    pallas_call x0 -> x7, Pallas kernels: none -> 1.71 us  [the longest x5 0.85 us: small(): pl.pallas_call(kernel, out_shape=outs, in_specs=[SCALAR] * len(scalars) +...]
    pallas_call x8, Pallas kernels: 11.1 us -> 9.46 us  [advance(): pl.pallas_call(functools.partial(step_kernel, step, width, [len(group) fo...]
  transfers between devices with their start and end apart: 37 -> 33, of which waited for: 9 -> 12; matrix products, arithmetic and copies ran while one was open for 3% -> 1% of each run, Pallas kernels for 20% -> 20%
where the time goes in v3:
time: 89.7 us; the launch traced here: 89.5 us
  starting transfers between devices  45.9 us (51%)
  waiting for transfers between devices  20.3 us (23%)
  Pallas kernels  19.4 us (22%)
  local copies, waits for them, and re-layouts  2.99 us (3%)
  between operations  0.92 us (1%)
    ppermute x8, starting transfers between devices, around(): two = lax.ppermute(x, 'wire', second)  19.1 us
    ppermute x14, starting transfers between devices, from_tile(): lax.ppermute(x, axis, [((i + offset) % size, i) for i in range(size)])  17.2 us
    pallas_call x8, Pallas kernels, advance(): pl.pallas_call(functools.partial(step_kernel, step, width, [len(group) fo...  9.46 us
    ppermute x14, waiting for transfers between devices, from_tile(): lax.ppermute(x, axis, [((i + offset) % size, i) for i in range(size)])  8.65 us
    ppermute x8, waiting for transfers between devices, around(): two = lax.ppermute(x, 'wire', second)  8.56 us
    ppermute x8, starting transfers between devices, around(): one = lax.ppermute(x, 'wire', first)  5.13 us
    ppermute x3, starting transfers between devices, swap_bits(): lax.ppermute(x, 'wire', [(i, i ^ hop) for i in range(lax.axis_size('wire'...  4.41 us
    pallas_call x1, Pallas kernels, program(): pl.pallas_call(functools.partial(last_kernel, xs), out_shape=[bf16(*shape...  2.9 us
  transfers between devices with their start and end apart: 33, of which 12 were waited for; matrix products, arithmetic and copies ran while one was open for 1% of the time, Pallas kernels for 20%

profile of v3, /device:TPU:0, one launch (start us, length us, event | category | flops | bytes accessed | tf_op | source)
XLA Modules:
  0.0 89.5 jit_solution(17546127861631103829)
XLA Ops:
  3.3 3.0 %collective-permute-start = (bf16[2,64,1152]{2,1,0:T(8,128)(2,1)S(1)}, bf16[2,64,1152]{2,1,0:T(8,128)(2,1)S(1)}, u32[]{:S(2)}, u32[]{:S(2)}) collective-permute-start(bf16[2,64,1152]{2,1,0:T(8,128)(2,1)S(1)} %shard_map.119), channel_id=1, source_target_pairs={{2,0},{0,2},{3,1},{1,3},{6,4},{4,6},{7,5},{5,7},{10,8},{8,10},{11,... | collective-permute-start | bytes 884744 | tf_op jit(solution)/shard_map/ppermute | solution.py:31
  6.9 6.5 %collective-permute-done.refs_0_ = bf16[2,64,1152]{2,1,0:T(8,128)(2,1)S(1)} collective-permute-done((bf16[2,64,1152]{2,1,0:T(8,128)(2,1)S(1)}, bf16[2,64,1152]{2,1,0:T(8,128)(2,1)S(1)}, u32[]{:S(2)}, u32[]{:S(2)}) %collective-permute-start) | collective-permute-done | bytes 294944 | tf_op jit(solution)/shard_map/ppermute | solution.py:31
  13.4 1.8 %collective-permute-start.2 = (bf16[256,256]{1,0:T(8,128)(2,1)S(1)}, bf16[256,256]{1,0:T(8,128)(2,1)S(1)}, u32[]{:S(2)}, u32[]{:S(2)}) collective-permute-start(bf16[256,256]{1,0:T(8,128)(2,1)S(1)} %pad_maximum_fusion.1), channel_id=1, source_target_pairs={{2,0},{0,2},{3,1},{1,3},{6,4},{4,6},{7,5},{5,7},{10,8},{8,10},{11,... | collective-permute-start | bytes 393224 | tf_op jit(solution)/shard_map/ppermute | solution.py:31
  16.7 1.8 %collective-permute-start.8 = (f32[256,256]{1,0:T(8,128)S(1)}, f32[256,256]{1,0:T(8,128)S(1)}, u32[]{:S(2)}, u32[]{:S(2)}) collective-permute-start(f32[256,256]{1,0:T(8,128)S(1)} %get-tuple-element.57), channel_id=1, source_target_pairs={{2,0},{0,2},{3,1},{1,3},{6,4},{4,6},{7,5},{5,7},{10,8},{8,10},{11,... | collective-permute-start | bytes 786440 | tf_op jit(solution)/shard_map/ppermute | solution.py:31
  19.9 1.9 %collective-permute-start.3 = (bf16[512,128]{1,0:T(8,128)(2,1)S(1)}, bf16[512,128]{1,0:T(8,128)(2,1)S(1)}, u32[]{:S(2)}, u32[]{:S(2)}) collective-permute-start(bf16[512,128]{1,0:T(8,128)(2,1)S(1)} %get-tuple-element.53.refs_3_.refs_6_), channel_id=1, source_target_pairs={{0,4},{4,0},{8,12},{12,8},{1,5},{5,1},{9,13},{13,9},{2,6},{6,2},{1... | collective-permute-start | bytes 393224 | tf_op jit(solution)/shard_map/ppermute | solution.py:45
  21.8 2.5 %collective-permute-start.4 = (bf16[512,128]{1,0:T(8,128)(2,1)S(1)}, bf16[512,128]{1,0:T(8,128)(2,1)S(1)}, u32[]{:S(2)}, u32[]{:S(2)}) collective-permute-start(bf16[512,128]{1,0:T(8,128)(2,1)S(1)} %get-tuple-element.53.refs_3_.refs_6_), channel_id=1, source_target_pairs={{4,8},{8,4},{12,0},{0,12},{5,9},{9,5},{13,1},{1,13},{6,10},{10,6},... | collective-permute-start | bytes 393224 | tf_op jit(solution)/shard_map/ppermute | solution.py:46
  28.4 3.1 %collective-permute-done.4.refs_5_ = bf16[512,128]{1,0:T(8,128)(2,1)S(1)} collective-permute-done((bf16[512,128]{1,0:T(8,128)(2,1)S(1)}, bf16[512,128]{1,0:T(8,128)(2,1)S(1)}, u32[]{:S(2)}, u32[]{:S(2)}) %collective-permute-start.4) | collective-permute-done | bytes 131104 | tf_op jit(solution)/shard_map/ppermute | solution.py:46
  33.3 2.9 %collective-permute-start.7 = (bf16[512,128]{1,0:T(8,128)(2,1)S(1)}, bf16[512,128]{1,0:T(8,128)(2,1)S(1)}, u32[]{:S(2)}, u32[]{:S(2)}) collective-permute-start(bf16[512,128]{1,0:T(8,128)(2,1)S(1)} %shard_map.124.refs_3_.refs_6_), channel_id=1, source_target_pairs={{4,8},{8,4},{12,0},{0,12},{5,9},{9,5},{13,1},{1,13},{6,10},{10,6},... | collective-permute-start | bytes 393224 | tf_op jit(solution)/shard_map/ppermute | solution.py:46
  38.3 3.3 %collective-permute-start.20 = (bf16[512,128]{1,0:T(8,128)(2,1)S(1)}, bf16[512,128]{1,0:T(8,128)(2,1)S(1)}, u32[]{:S(2)}, u32[]{:S(2)}) collective-permute-start(bf16[512,128]{1,0:T(8,128)(2,1)S(1)} %shard_map.130.refs_3_.refs_6_), channel_id=1, source_target_pairs={{4,8},{8,4},{12,0},{0,12},{5,9},{9,5},{13,1},{1,13},{6,10},{10,6},... | collective-permute-start | bytes 393224 | tf_op jit(solution)/shard_map/ppermute | solution.py:46
  41.6 1.9 %collective-permute-done.7.refs_5_ = bf16[512,128]{1,0:T(8,128)(2,1)S(1)} collective-permute-done((bf16[512,128]{1,0:T(8,128)(2,1)S(1)}, bf16[512,128]{1,0:T(8,128)(2,1)S(1)}, u32[]{:S(2)}, u32[]{:S(2)}) %collective-permute-start.7) | collective-permute-done | bytes 131104 | tf_op jit(solution)/shard_map/ppermute | solution.py:46
  46.7 1.6 %collective-permute-start.13 = (bf16[512,256]{1,0:T(8,128)(2,1)S(1)}, bf16[512,256]{1,0:T(8,128)(2,1)S(1)}, u32[]{:S(2)}, u32[]{:S(2)}) collective-permute-start(bf16[512,256]{1,0:T(8,128)(2,1)S(1)} %get-tuple-element.62.refs_9_), channel_id=1, source_target_pairs={{2,0},{0,2},{3,1},{1,3},{6,4},{4,6},{7,5},{5,7},{10,8},{8,10},{11,... | collective-permute-start | bytes 786440 | tf_op jit(solution)/shard_map/ppermute | solution.py:31
  51.3 2.5 %collective-permute-start.22 = (bf16[512,128]{1,0:T(8,128)(2,1)S(1)}, bf16[512,128]{1,0:T(8,128)(2,1)S(1)}, u32[]{:S(2)}, u32[]{:S(2)}) collective-permute-start(bf16[512,128]{1,0:T(8,128)(2,1)S(1)} %get-tuple-element.67.refs_3_.refs_6_), channel_id=1, source_target_pairs={{4,8},{8,4},{12,0},{0,12},{5,9},{9,5},{13,1},{1,13},{6,10},{10,6},... | collective-permute-start | bytes 393224 | tf_op jit(solution)/shard_map/ppermute | solution.py:46
  55.4 3.5 %collective-permute-start.12 = (bf16[512,128]{1,0:T(8,128)(2,1)S(1)}, bf16[512,128]{1,0:T(8,128)(2,1)S(1)}, u32[]{:S(2)}, u32[]{:S(2)}) collective-permute-start(bf16[512,128]{1,0:T(8,128)(2,1)S(1)} %get-tuple-element.59.refs_3_.refs_2_.refs_0_), channel_id=1, source_target_pairs={{4,8},{8,4},{12,0},{0,12},{5,9},{9,5},{13,1},{1,13},{6,10},{10,6},... | collective-permute-start | bytes 393224 | tf_op jit(solution)/shard_map/ppermute | solution.py:46
  59.0 2.1 %collective-permute-done.22.refs_5_ = bf16[512,128]{1,0:T(8,128)(2,1)S(1)} collective-permute-done((bf16[512,128]{1,0:T(8,128)(2,1)S(1)}, bf16[512,128]{1,0:T(8,128)(2,1)S(1)}, u32[]{:S(2)}, u32[]{:S(2)}) %collective-permute-start.22) | collective-permute-done | bytes 131104 | tf_op jit(solution)/shard_map/ppermute | solution.py:46
  62.2 2.3 %collective-permute-start.24 = (bf16[512,128]{1,0:T(8,128)(2,1)S(1)}, bf16[512,128]{1,0:T(8,128)(2,1)S(1)}, u32[]{:S(2)}, u32[]{:S(2)}) collective-permute-start(bf16[512,128]{1,0:T(8,128)(2,1)S(1)} %get-tuple-element.68.refs_3_.refs_8_.refs_2_), channel_id=1, source_target_pairs={{4,8},{8,4},{12,0},{0,12},{5,9},{9,5},{13,1},{1,13},{6,10},{10,6},... | collective-permute-start | bytes 393224 | tf_op jit(solution)/shard_map/ppermute | solution.py:46
  64.6 1.5 %collective-permute-start.25 = (bf16[256,128]{1,0:T(8,128)(2,1)S(1)}, bf16[256,128]{1,0:T(8,128)(2,1)S(1)}, u32[]{:S(2)}, u32[]{:S(2)}) collective-permute-start(bf16[256,128]{1,0:T(8,128)(2,1)S(1)} %get-tuple-element.72), channel_id=1, source_target_pairs={{2,0},{0,2},{3,1},{1,3},{6,4},{4,6},{7,5},{5,7},{10,8},{8,10},{11,... | collective-permute-start | bytes 196616 | tf_op jit(solution)/shard_map/ppermute | solution.py:31
  66.7 1.6 %shard_map.129 = (bf16[256,128]{1,0:T(8,128)(2,1)S(1)}, bf16[256,128]{1,0:T(8,128)(2,1)S(1)}, f32[2,128,128]{2,1,0:T(8,128)S(1)}, bf16[2,128,128]{2,1,0:T(8,128)(2,1)S(1)}) custom-call(s32[1]{0:T(128)} %bitcast.1.info.place, f32[4]{0:T(128)S(1)} %copy-done.6, bf16[512,512]{1,0:T(8,128)(2,1)S(1)} %get-tuple-element.50.refs_0_, ...), custom_call_target="tpu_custom_call" | custom-call | flops 201326592 | bytes 1572864 | tf_op jit(solution)/shard_map/pallas_call | solution.py:346
  68.4 1.6 %collective-permute-start.27 = (bf16[256,128]{1,0:T(8,128)(2,1)S(1)}, bf16[256,128]{1,0:T(8,128)(2,1)S(1)}, u32[]{:S(2)}, u32[]{:S(2)}) collective-permute-start(bf16[256,128]{1,0:T(8,128)(2,1)S(1)} %get-tuple-element.75), channel_id=1, source_target_pairs={{2,0},{0,2},{3,1},{1,3},{6,4},{4,6},{7,5},{5,7},{10,8},{8,10},{11,... | collective-permute-start | bytes 196616 | tf_op jit(solution)/shard_map/ppermute | solution.py:31
  73.1 2.0 %collective-permute-start.30 = (f32[1,128]{1,0:T(1,128)S(1)}, f32[1,128]{1,0:T(1,128)S(1)}, u32[]{:S(2)}, u32[]{:S(2)}) collective-permute-start(f32[1,128]{1,0:T(1,128)S(1)} %get-tuple-element.82.refs_0_), channel_id=1, source_target_pairs={{0,4},{4,0},{8,12},{12,8},{1,5},{5,1},{9,13},{13,9},{2,6},{6,2},{1... | collective-permute-start | bytes 1544 | tf_op jit(solution)/shard_map/ppermute | solution.py:51
  75.2 1.6 %collective-permute-done.30.refs_1_ = f32[1,128]{1,0:T(1,128)S(1)} collective-permute-done((f32[1,128]{1,0:T(1,128)S(1)}, f32[1,128]{1,0:T(1,128)S(1)}, u32[]{:S(2)}, u32[]{:S(2)}) %collective-permute-start.30) | collective-permute-done | bytes 544 | tf_op jit(solution)/shard_map/ppermute | solution.py:51
  76.8 2.3 %collective-permute-start.31 = (bf16[144,128]{1,0:T(8,128)(2,1)S(1)}, bf16[144,128]{1,0:T(8,128)(2,1)S(1)}, u32[]{:S(2)}, u32[]{:S(2)}) collective-permute-start(bf16[144,128]{1,0:T(8,128)(2,1)S(1)} %get-tuple-element.83), channel_id=1, source_target_pairs={{0,8},{4,12},{8,0},{12,4},{1,9},{5,13},{9,1},{13,5},{2,10},{6,14},... | collective-permute-start | bytes 110600 | tf_op jit(solution)/shard_map/ppermute | solution.py:51
  79.7 1.5 %collective-permute-start.26 = (bf16[256,128]{1,0:T(8,128)(2,1)S(1)}, bf16[256,128]{1,0:T(8,128)(2,1)S(1)}, u32[]{:S(2)}, u32[]{:S(2)}) collective-permute-start(bf16[256,128]{1,0:T(8,128)(2,1)S(1)} %get-tuple-element.74), channel_id=1, source_target_pairs={{2,0},{0,2},{3,1},{1,3},{6,4},{4,6},{7,5},{5,7},{10,8},{8,10},{11,... | collective-permute-start | bytes 196616 | tf_op jit(solution)/shard_map/ppermute | solution.py:31
  83.9 1.7 %shard_map.135 = bf16[4,1,64,2,256]{4,3,2,1,0:T(2,128)(2,1)} custom-call(s32[1]{0:T(128)} %bitcast.me, bf16[512,128]{1,0:T(8,128)(2,1)S(1)} %get-tuple-element.59.refs_3_.refs_2_.refs_0_, bf16[256,128]{1,0:T(8,128)(2,1)S(1)} %collective-permute-done.15.refs_3_.refs_1_, bf16[512,128]{1,0:T(8,128)(2,1)S(1)} %get-tuple-element.68.refs_3_.refs_8_.refs_2_, ...), custom_call_target="tpu_custom_call" | custom-call | bytes 524288 | tf_op jit(solution)/shard_map/pallas_call | solution.py:560
  86.0 2.9 %shard_map.134 = (bf16[4,1,64,2,256]{4,3,2,1,0:T(2,128)(2,1)}, f32[4,1,64,2,256]{4,3,2,1,0:T(2,128)}) custom-call(s32[1]{0:T(128)} %bitcast.me, f32[4]{0:T(128)S(1)} %copy-done.6, bf16[256,128]{1,0:T(8,128)(2,1)S(1)} %get-tuple-element.63.refs_0_, bf16[256,128]{1,0:T(8,128)(2,1)S(1)} %collective-permute-done.14.refs_1_, ...), custom_call_target="tpu_custom_call" | custom-call | bytes 2097152 | tf_op jit(solution)/shard_map/pallas_call | solution.py:569
  (89 shorter events, 31.1 us)
Async XLA Ops:
  3.3 10.0 %collective-permute-start = (bf16[2,64,1152]{2,1,0:T(8,128)(2,1)S(1)}, bf16[2,64,1152]{2,1,0:T(8,128)(2,1)S(1)}, u32[]{:S(2)}, u32[]{:S(2)}) collective-permute-start(bf16[2,64,1152]{2,1,0:T(8,128)(2,1)S(1)} %shard_map.119), channel_id=1, source_target_pairs={{2,0},{0,2},{3,1},{1,3},{6,4},{4,6},{7,5},{5,7},{10,8},{8,10},{11,... | collective-permute-start | bytes 884744 | tf_op jit(solution)/shard_map/ppermute | solution.py:31
  13.4 12.9 %collective-permute-start.1 = (bf16[2,64,1152]{2,1,0:T(8,128)(2,1)S(1)}, bf16[2,64,1152]{2,1,0:T(8,128)(2,1)S(1)}, u32[]{:S(2)}, u32[]{:S(2)}) collective-permute-start(bf16[2,64,1152]{2,1,0:T(8,128)(2,1)S(1)} %collective-permute-done.refs_0_), channel_id=1, source_target_pairs={{1,0},{0,1},{3,2},{2,3},{5,4},{4,5},{7,6},{6,7},{9,8},{8,9},{11,10... | collective-permute-start | bytes 884744 | tf_op jit(solution)/shard_map/ppermute | solution.py:31
  15.8 9.7 %collective-permute-start.5 = (bf16[256,256]{1,0:T(8,128)(2,1)S(1)}, bf16[256,256]{1,0:T(8,128)(2,1)S(1)}, u32[]{:S(2)}, u32[]{:S(2)}) collective-permute-start(bf16[256,256]{1,0:T(8,128)(2,1)S(1)} %get-tuple-element.55), channel_id=1, source_target_pairs={{2,0},{0,2},{3,1},{1,3},{6,4},{4,6},{7,5},{5,7},{10,8},{8,10},{11,... | collective-permute-start | bytes 393224 | tf_op jit(solution)/shard_map/ppermute | solution.py:31
  16.7 24.9 %collective-permute-start.8 = (f32[256,256]{1,0:T(8,128)S(1)}, f32[256,256]{1,0:T(8,128)S(1)}, u32[]{:S(2)}, u32[]{:S(2)}) collective-permute-start(f32[256,256]{1,0:T(8,128)S(1)} %get-tuple-element.57), channel_id=1, source_target_pairs={{2,0},{0,2},{3,1},{1,3},{6,4},{4,6},{7,5},{5,7},{10,8},{8,10},{11,... | collective-permute-start | bytes 786440 | tf_op jit(solution)/shard_map/ppermute | solution.py:31
  19.9 8.5 %collective-permute-start.3 = (bf16[512,128]{1,0:T(8,128)(2,1)S(1)}, bf16[512,128]{1,0:T(8,128)(2,1)S(1)}, u32[]{:S(2)}, u32[]{:S(2)}) collective-permute-start(bf16[512,128]{1,0:T(8,128)(2,1)S(1)} %get-tuple-element.53.refs_3_.refs_6_), channel_id=1, source_target_pairs={{0,4},{4,0},{8,12},{12,8},{1,5},{5,1},{9,13},{13,9},{2,6},{6,2},{1... | collective-permute-start | bytes 393224 | tf_op jit(solution)/shard_map/ppermute | solution.py:45
  21.8 9.7 %collective-permute-start.4 = (bf16[512,128]{1,0:T(8,128)(2,1)S(1)}, bf16[512,128]{1,0:T(8,128)(2,1)S(1)}, u32[]{:S(2)}, u32[]{:S(2)}) collective-permute-start(bf16[512,128]{1,0:T(8,128)(2,1)S(1)} %get-tuple-element.53.refs_3_.refs_6_), channel_id=1, source_target_pairs={{4,8},{8,4},{12,0},{0,12},{5,9},{9,5},{13,1},{1,13},{6,10},{10,6},... | collective-permute-start | bytes 393224 | tf_op jit(solution)/shard_map/ppermute | solution.py:46
  25.5 10.8 %collective-permute-start.17 = (bf16[512,128]{1,0:T(8,128)(2,1)S(1)}, bf16[512,128]{1,0:T(8,128)(2,1)S(1)}, u32[]{:S(2)}, u32[]{:S(2)}) collective-permute-start(bf16[512,128]{1,0:T(8,128)(2,1)S(1)} %get-tuple-element.66.refs_3_.refs_6_), channel_id=1, source_target_pairs={{0,4},{4,0},{8,12},{12,8},{1,5},{5,1},{9,13},{13,9},{2,6},{6,2},{1... | collective-permute-start | bytes 393224 | tf_op jit(solution)/shard_map/ppermute | solution.py:45
  26.2 10.9 %collective-permute-start.18 = (bf16[512,128]{1,0:T(8,128)(2,1)S(1)}, bf16[512,128]{1,0:T(8,128)(2,1)S(1)}, u32[]{:S(2)}, u32[]{:S(2)}) collective-permute-start(bf16[512,128]{1,0:T(8,128)(2,1)S(1)} %get-tuple-element.66.refs_3_.refs_6_), channel_id=1, source_target_pairs={{4,8},{8,4},{12,0},{0,12},{5,9},{9,5},{13,1},{1,13},{6,10},{10,6},... | collective-permute-start | bytes 393224 | tf_op jit(solution)/shard_map/ppermute | solution.py:46
  33.3 8.4 %collective-permute-start.6 = (bf16[512,128]{1,0:T(8,128)(2,1)S(1)}, bf16[512,128]{1,0:T(8,128)(2,1)S(1)}, u32[]{:S(2)}, u32[]{:S(2)}) collective-permute-start(bf16[512,128]{1,0:T(8,128)(2,1)S(1)} %shard_map.124.refs_3_.refs_6_), channel_id=1, source_target_pairs={{0,4},{4,0},{8,12},{12,8},{1,5},{5,1},{9,13},{13,9},{2,6},{6,2},{1... | collective-permute-start | bytes 393224 | tf_op jit(solution)/shard_map/ppermute | solution.py:45
  33.3 10.2 %collective-permute-start.7 = (bf16[512,128]{1,0:T(8,128)(2,1)S(1)}, bf16[512,128]{1,0:T(8,128)(2,1)S(1)}, u32[]{:S(2)}, u32[]{:S(2)}) collective-permute-start(bf16[512,128]{1,0:T(8,128)(2,1)S(1)} %shard_map.124.refs_3_.refs_6_), channel_id=1, source_target_pairs={{4,8},{8,4},{12,0},{0,12},{5,9},{9,5},{13,1},{1,13},{6,10},{10,6},... | collective-permute-start | bytes 393224 | tf_op jit(solution)/shard_map/ppermute | solution.py:46
  38.2 10.9 %collective-permute-start.19 = (bf16[512,128]{1,0:T(8,128)(2,1)S(1)}, bf16[512,128]{1,0:T(8,128)(2,1)S(1)}, u32[]{:S(2)}, u32[]{:S(2)}) collective-permute-start(bf16[512,128]{1,0:T(8,128)(2,1)S(1)} %shard_map.130.refs_3_.refs_6_), channel_id=1, source_target_pairs={{0,4},{4,0},{8,12},{12,8},{1,5},{5,1},{9,13},{13,9},{2,6},{6,2},{1... | collective-permute-start | bytes 393224 | tf_op jit(solution)/shard_map/ppermute | solution.py:45
  38.3 10.8 %collective-permute-start.20 = (bf16[512,128]{1,0:T(8,128)(2,1)S(1)}, bf16[512,128]{1,0:T(8,128)(2,1)S(1)}, u32[]{:S(2)}, u32[]{:S(2)}) collective-permute-start(bf16[512,128]{1,0:T(8,128)(2,1)S(1)} %shard_map.130.refs_3_.refs_6_), channel_id=1, source_target_pairs={{4,8},{8,4},{12,0},{0,12},{5,9},{9,5},{13,1},{1,13},{6,10},{10,6},... | collective-permute-start | bytes 393224 | tf_op jit(solution)/shard_map/ppermute | solution.py:46
  44.7 9.2 %collective-permute-start.10 = (bf16[512,128]{1,0:T(8,128)(2,1)S(1)}, bf16[512,128]{1,0:T(8,128)(2,1)S(1)}, u32[]{:S(2)}, u32[]{:S(2)}) collective-permute-start(bf16[512,128]{1,0:T(8,128)(2,1)S(1)} %get-tuple-element.58.refs_3_.refs_6_), channel_id=1, source_target_pairs={{4,8},{8,4},{12,0},{0,12},{5,9},{9,5},{13,1},{1,13},{6,10},{10,6},... | collective-permute-start | bytes 393224 | tf_op jit(solution)/shard_map/ppermute | solution.py:46
  45.7 8.1 %collective-permute-start.9 = (bf16[512,128]{1,0:T(8,128)(2,1)S(1)}, bf16[512,128]{1,0:T(8,128)(2,1)S(1)}, u32[]{:S(2)}, u32[]{:S(2)}) collective-permute-start(bf16[512,128]{1,0:T(8,128)(2,1)S(1)} %get-tuple-element.58.refs_3_.refs_6_), channel_id=1, source_target_pairs={{0,4},{4,0},{8,12},{12,8},{1,5},{5,1},{9,13},{13,9},{2,6},{6,2},{1... | collective-permute-start | bytes 393224 | tf_op jit(solution)/shard_map/ppermute | solution.py:45
  46.7 17.9 %collective-permute-start.13 = (bf16[512,256]{1,0:T(8,128)(2,1)S(1)}, bf16[512,256]{1,0:T(8,128)(2,1)S(1)}, u32[]{:S(2)}, u32[]{:S(2)}) collective-permute-start(bf16[512,256]{1,0:T(8,128)(2,1)S(1)} %get-tuple-element.62.refs_9_), channel_id=1, source_target_pairs={{2,0},{0,2},{3,1},{1,3},{6,4},{4,6},{7,5},{5,7},{10,8},{8,10},{11,... | collective-permute-start | bytes 786440 | tf_op jit(solution)/shard_map/ppermute | solution.py:31
  50.2 8.7 %collective-permute-start.21 = (bf16[512,128]{1,0:T(8,128)(2,1)S(1)}, bf16[512,128]{1,0:T(8,128)(2,1)S(1)}, u32[]{:S(2)}, u32[]{:S(2)}) collective-permute-start(bf16[512,128]{1,0:T(8,128)(2,1)S(1)} %get-tuple-element.67.refs_3_.refs_6_), channel_id=1, source_target_pairs={{0,4},{4,0},{8,12},{12,8},{1,5},{5,1},{9,13},{13,9},{2,6},{6,2},{1... | collective-permute-start | bytes 393224 | tf_op jit(solution)/shard_map/ppermute | solution.py:45
  51.3 9.7 %collective-permute-start.22 = (bf16[512,128]{1,0:T(8,128)(2,1)S(1)}, bf16[512,128]{1,0:T(8,128)(2,1)S(1)}, u32[]{:S(2)}, u32[]{:S(2)}) collective-permute-start(bf16[512,128]{1,0:T(8,128)(2,1)S(1)} %get-tuple-element.67.refs_3_.refs_6_), channel_id=1, source_target_pairs={{4,8},{8,4},{12,0},{0,12},{5,9},{9,5},{13,1},{1,13},{6,10},{10,6},... | collective-permute-start | bytes 393224 | tf_op jit(solution)/shard_map/ppermute | solution.py:46
  55.0 11.1 %collective-permute-start.11 = (bf16[512,128]{1,0:T(8,128)(2,1)S(1)}, bf16[512,128]{1,0:T(8,128)(2,1)S(1)}, u32[]{:S(2)}, u32[]{:S(2)}) collective-permute-start(bf16[512,128]{1,0:T(8,128)(2,1)S(1)} %get-tuple-element.59.refs_3_.refs_2_.refs_0_), channel_id=1, source_target_pairs={{0,4},{4,0},{8,12},{12,8},{1,5},{5,1},{9,13},{13,9},{2,6},{6,2},{1... | collective-permute-start | bytes 393224 | tf_op jit(solution)/shard_map/ppermute | solution.py:45
  55.4 11.3 %collective-permute-start.12 = (bf16[512,128]{1,0:T(8,128)(2,1)S(1)}, bf16[512,128]{1,0:T(8,128)(2,1)S(1)}, u32[]{:S(2)}, u32[]{:S(2)}) collective-permute-start(bf16[512,128]{1,0:T(8,128)(2,1)S(1)} %get-tuple-element.59.refs_3_.refs_2_.refs_0_), channel_id=1, source_target_pairs={{4,8},{8,4},{12,0},{0,12},{5,9},{9,5},{13,1},{1,13},{6,10},{10,6},... | collective-permute-start | bytes 393224 | tf_op jit(solution)/shard_map/ppermute | solution.py:46
  62.2 8.9 %collective-permute-start.23 = (bf16[512,128]{1,0:T(8,128)(2,1)S(1)}, bf16[512,128]{1,0:T(8,128)(2,1)S(1)}, u32[]{:S(2)}, u32[]{:S(2)}) collective-permute-start(bf16[512,128]{1,0:T(8,128)(2,1)S(1)} %get-tuple-element.68.refs_3_.refs_8_.refs_2_), channel_id=1, source_target_pairs={{0,4},{4,0},{8,12},{12,8},{1,5},{5,1},{9,13},{13,9},{2,6},{6,2},{1... | collective-permute-start | bytes 393224 | tf_op jit(solution)/shard_map/ppermute | solution.py:45
  62.2 9.8 %collective-permute-start.24 = (bf16[512,128]{1,0:T(8,128)(2,1)S(1)}, bf16[512,128]{1,0:T(8,128)(2,1)S(1)}, u32[]{:S(2)}, u32[]{:S(2)}) collective-permute-start(bf16[512,128]{1,0:T(8,128)(2,1)S(1)} %get-tuple-element.68.refs_3_.refs_8_.refs_2_), channel_id=1, source_target_pairs={{4,8},{8,4},{12,0},{0,12},{5,9},{9,5},{13,1},{1,13},{6,10},{10,6},... | collective-permute-start | bytes 393224 | tf_op jit(solution)/shard_map/ppermute | solution.py:46
  68.4 11.2 %collective-permute-start.27 = (bf16[256,128]{1,0:T(8,128)(2,1)S(1)}, bf16[256,128]{1,0:T(8,128)(2,1)S(1)}, u32[]{:S(2)}, u32[]{:S(2)}) collective-permute-start(bf16[256,128]{1,0:T(8,128)(2,1)S(1)} %get-tuple-element.75), channel_id=1, source_target_pairs={{2,0},{0,2},{3,1},{1,3},{6,4},{4,6},{7,5},{5,7},{10,8},{8,10},{11,... | collective-permute-start | bytes 196616 | tf_op jit(solution)/shard_map/ppermute | solution.py:31
  70.0 15.7 %collective-permute-start.28 = (f32[256,128]{1,0:T(8,128)S(1)}, f32[256,128]{1,0:T(8,128)S(1)}, u32[]{:S(2)}, u32[]{:S(2)}) collective-permute-start(f32[256,128]{1,0:T(8,128)S(1)} %get-tuple-element.70.refs_8_), channel_id=1, source_target_pairs={{2,0},{0,2},{3,1},{1,3},{6,4},{4,6},{7,5},{5,7},{10,8},{8,10},{11,... | collective-permute-start | bytes 393224 | tf_op jit(solution)/shard_map/ppermute | solution.py:31
  71.0 14.6 %collective-permute-start.16 = (f32[256,128]{1,0:T(8,128)S(1)}, f32[256,128]{1,0:T(8,128)S(1)}, u32[]{:S(2)}, u32[]{:S(2)}) collective-permute-start(f32[256,128]{1,0:T(8,128)S(1)} %get-tuple-element.61.refs_8_), channel_id=1, source_target_pairs={{2,0},{0,2},{3,1},{1,3},{6,4},{4,6},{7,5},{5,7},{10,8},{8,10},{11,... | collective-permute-start | bytes 393224 | tf_op jit(solution)/shard_map/ppermute | solution.py:31
  (18 other events, 94.6 us)

commit v4 on v3

v4 whole, which is shorter than its diff:
```python
import functools

import jax
import jax.numpy as jnp
from jax import lax
from jax.experimental import pallas as pl
from jax.experimental.pallas import tpu as pltpu
from jax.sharding import PartitionSpec as P

STEPS = 4
VMEM = 12 << 20
SCALAR = pl.BlockSpec(memory_space=pltpu.SMEM)
WHOLE = pl.BlockSpec(memory_space=pltpu.VMEM)
PARAMS = pltpu.CompilerParams(vmem_limit_bytes=VMEM)


def bf16(*shape):
    return jax.ShapeDtypeStruct(shape, jnp.bfloat16)


def f32(*shape):
    return jax.ShapeDtypeStruct(shape, jnp.float32)


def cost(moved, flops=0):
    return pl.CostEstimate(flops=flops, transcendentals=0, bytes_accessed=moved)


def from_tile(x, offset, axis="xsec"):
    size = lax.axis_size(axis)
    return lax.ppermute(x, axis, [((i + offset) % size, i) for i in range(size)])


def to_tile(x, offset):
    return from_tile(x, lax.axis_size("xsec") - offset)


def around(x):
    size = lax.axis_size("wire")
    first, second = ([], [])
    for i in range(0, size, 2):
        j, k = (i + 1, (i + 2) % size)
        first += [(i, j), (j, i)]
        second += [(j, k), (k, j)]
    one = lax.ppermute(x, "wire", first)
    two = lax.ppermute(x, "wire", second)
    return one, two


def swap_bits(x, hop):
    return lax.ppermute(x, "wire", [(i, i ^ hop) for i in range(lax.axis_size("wire"))])


def own_block(me, value, offset, count):
    width = value.shape[1] // count
    picked = value[:, :width]
    for b in range(1, count):
        block = value[:, b * width : (b + 1) * width]
        picked = jnp.where((me[0] - offset + count) % count == b, block, picked)
    return picked


def half_of(x, h):
    cells, _, orbs, _, columns = x.shape
    return x[...].astype(jnp.float32)[:, 0, :, h, :].reshape(cells * orbs, columns)


def deal_kernel(offsets, count, me, x, *outs):
    width = x.shape[4] // count
    for h in range(x.shape[3]):
        value = half_of(x, h)
        for offset, out in zip(offsets, outs):
            picked = own_block(me, value, offset, count)
            out[:, h * width : (h + 1) * width] = picked.astype(x.dtype)


def deal(x, me, offsets):
    count = lax.axis_size("xsec")
    cells, _, orbs, halves, columns = x.shape
    shape = (cells * orbs, halves * columns // count)
    return small(
        functools.partial(deal_kernel, offsets, count),
        [me],
        [x],
        [jax.ShapeDtypeStruct(shape, x.dtype)] * len(offsets),
    )


def stack_kernel(count, me, current, *refs):
    got, outs = (refs[: count - 1], refs[count - 1 :])
    width = outs[0].shape[1]
    rows = outs[0].shape[0] // count
    for h, out in enumerate(outs):
        out[:rows] = own_block(me, half_of(current, h), 0, count).astype(out.dtype)
        for i, ref in enumerate(got):
            out[(i + 1) * rows : (i + 2) * rows] = ref[:, h * width : (h + 1) * width]


def rest_kernel(me, sketch, signs, turned, own, *outs):
    cells, _, orbs, ranks = sketch.shape
    count = len(outs) + 1
    rows = cells * orbs
    width = own.shape[1]
    flipped = sketch[...].reshape(rows, ranks).astype(jnp.float32).T.astype(jnp.bfloat16)
    turned[...] = flipped
    value = (2 * signs[...] - 1).astype(jnp.float32).reshape(rows, signs.shape[3])
    own[...] = own_block(me, value, 0, count).astype(jnp.bfloat16)
    for i, out in enumerate(outs):
        out[:ranks] = flipped
        picked = own_block(me, value, i + 1, count).astype(jnp.bfloat16)
        for j in range(rows // width):
            out[ranks:, j * width : (j + 1) * width] = picked[j * width : (j + 1) * width]


def joined(me, refs, lanes, h, b, rows, width):
    value = None
    for i in range(len(lanes)):
        ref, lane = (refs[lanes[i][h][0]], lanes[i][h][1])
        part = ref[:rows, lane : lane + width].astype(jnp.float32)
        here = (me[0] - i + len(lanes)) % len(lanes) == b
        value = part if value is None else jnp.where(here, part, value)
    return value


def before_kernel(lanes, me, *refs):
    out = refs[-1]
    cells, _, orbs, halves, columns = out.shape
    width = columns // len(lanes)
    for h in range(halves):
        for b in range(len(lanes)):
            value = joined(me, refs, lanes, h, b, cells * orbs, width).astype(out.dtype)
            out[:, 0, :, h, b * width : (b + 1) * width] = value.reshape(cells, orbs, width)


def last_kernel(late_lanes, mid_lanes, sum_lanes, start_lanes, me, coef, *refs):
    newest, summed = refs[-2:]
    cells, _, orbs, halves, columns = newest.shape
    count = len(late_lanes)
    width = columns // count
    for h in range(halves):
        for b in range(count):
            late, mid, total, start = [
                joined(me, refs, lanes, h, b, cells * orbs, width)
                for lanes in (late_lanes, mid_lanes, sum_lanes, start_lanes)
            ]
            at = slice(b * width, (b + 1) * width)
            shape = (cells, orbs, width)
            newest[:, 0, :, h, at] = late.astype(newest.dtype).reshape(shape)
            total = start + total + coef[STEPS - 2] * mid
            total = total + coef[STEPS - 1] * late
            summed[:, 0, :, h, at] = total.reshape(shape)


def pack_kernel(core, me, pattern, blocks, out):
    share, orbs, wide = blocks.shape
    span = wide // orbs // 3
    slots = out.shape[2] // orbs // span
    zero = jnp.zeros((orbs, orbs), jnp.bfloat16)
    for c in range(share):
        cell = core[0] * share + c

        def block(d, e):
            column = 3 * d + e
            value = blocks[c, :, column * orbs : (column + 1) * orbs]
            return jnp.where(pattern[cell, column] != 0, value, zero)

        for d in range(span):
            values = [block(d, e) for e in range(3)]
            if slots == 2:
                values = [values[1], jnp.where(me[0] == 0, values[2], values[0])]
            for n, value in enumerate(values):
                at = (slots * d + n) * orbs
                out[c, :, at : at + orbs] = value


def packed(blocks, pattern, core, me, cores, slots):
    cells, orbs, wide = blocks.shape
    share = cells // cores
    shape = (share, orbs, wide // 3 * slots)
    return pl.pallas_call(
        pack_kernel,
        out_shape=bf16(*shape),
        grid_spec=pltpu.PrefetchScalarGridSpec(
            num_scalar_prefetch=3,
            grid=(1,),
            in_specs=[pl.BlockSpec((share, orbs, wide), lambda i, core, me, p: (core[0], 0, 0))],
            out_specs=pl.BlockSpec(shape, lambda i, core, me, p: (0, 0, 0)),
        ),
        compiler_params=PARAMS,
        cost_estimate=cost(4 * share * orbs * wide),
    )(core, me, pattern, blocks)


def band_kernel(tile, sizes, me, place, slot, pattern, *refs):
    cells, orbs, reach, tiles, pieces = sizes
    first, own, second = refs[-3:]
    share = cells // pieces
    span = 2 * reach + 1
    zero = jnp.zeros((orbs, orbs), jnp.bfloat16)
    slots = refs[0].shape[2] // orbs // span
    masked = tile == 0

    def write(parts):
        def block(c, u, x):
            d = x - c
            if d < 0 or d >= span:
                return zero
            ref = parts[c // share]

            def at(e):
                column = slots * d + e
                value = ref[c % share, :, column * orbs : (column + 1) * orbs]
                if masked:
                    value = jnp.where(pattern[c, column] != 0, value, zero)
                return value

            if slots == 2:
                return at(0 if u == tile else 1)
            if u == tile:
                return at(1)
            gap = lax.rem(me[0] + u, tiles) - lax.rem(me[0] + tile, tiles) + 1
            return jnp.where(gap == 0, at(0), jnp.where(gap == 2, at(2), zero))

        turn = lax.rem(place[0], 2) == 0
        for c in range(cells):
            rows = slice(c * orbs, (c + 1) * orbs)
            for u in range(tiles):
                for j in range(cells):
                    at = (u * cells + j) * orbs
                    own[rows, at : at + orbs] = block(c, u, reach + j)
                for j in range(reach):
                    at = (u * reach + j) * orbs
                    left, right = (block(c, u, j), block(c, u, reach + cells + j))
                    first[rows, at : at + orbs] = jnp.where(turn, right, left)
                    second[rows, at : at + orbs] = jnp.where(turn, left, right)

    if pieces == 1:
        write(refs[:1])
        return
    for k in range(pieces):

        @pl.when(slot[0] == k)
        def _():
            write([refs[(piece - k) % pieces] for piece in range(pieces)])


def band_rows(tile, parts, pattern, me, place, slot, sizes, held):
    cells, orbs, reach, tiles, _ = sizes
    rows = cells * orbs
    shapes = [(tiles * rows, tiles * n * orbs) for n in (reach, cells, reach)]
    n_in = 4 + len(parts)
    return pl.pallas_call(
        functools.partial(band_kernel, tile, sizes),
        out_shape=[bf16(*s) for s in shapes],
        grid=(1,),
        in_specs=[SCALAR] * 4
        + [pl.BlockSpec(p.shape, lambda i: (0, 0, 0)) for p in parts]
        + [pl.BlockSpec(memory_space=pl.ANY)] * len(held),
        out_specs=[pl.BlockSpec((rows, s[1]), lambda i: (tile, 0)) for s in shapes],
        input_output_aliases={n_in + i: i for i in range(len(held))},
        compiler_params=PARAMS,
        cost_estimate=cost(4 * rows * tiles * 3 * cells * orbs),
    )(me, place, slot, pattern, *parts, *held)


def step_kernel(step, tiles, width, counts, lanes, kind, *refs):
    refs = list(refs)

    def take(n):
        taken = refs[:n]
        del refs[:n]
        return taken

    place = take(1)[0] if kind == "sketch" else None
    coef = take(1)[0] if kind in ("sum", "sketch", "probe") else None
    own, first, second = take(3)
    field, near, far, older, sums, start, extra = [take(n) for n in counts]
    outs = refs

    def parts(group, lane):
        return [ref[:, low : low + width] for ref, low in zip(group, lane)]

    image = None
    for band, group in zip((own, first, second), (field, near, far)):
        at = 0
        for ref in group:
            depth = ref.shape[0]
            term = jnp.dot(
                band[:, at : at + depth], ref[...], preferred_element_type=jnp.float32
            )
            image = term if image is None else image + term
            at += depth

    old = jnp.concatenate(parts(older, lanes[0])).astype(jnp.float32)
    value = (2.0 * image - old).astype(jnp.bfloat16)
    rows = value.shape[0] // tiles

    if kind in ("plain", "sum", "before"):
        outs.pop(0)[...] = value
    if kind in ("sum", "sketch", "probe"):
        now = jnp.concatenate([ref[...] for ref in field]).astype(jnp.float32)
        total = coef[step - 1] * now + coef[step] * value.astype(jnp.float32)
        if sums:
            total = jnp.concatenate(parts(start, lanes[2])) + jnp.concatenate(parts(sums, lanes[1])) + total
    if kind == "sum":
        for i, out in enumerate(outs):
            mine = total[i * rows : (i + 1) * rows]
            if out.shape[1] == width:
                out[...] = mine
            else:
                out[:, :width] = extra[i - 1][...]
                out[:, width:] = mine
    if kind == "before":
        for i, out in enumerate(outs):
            at = slice((i + 1) * rows, (i + 2) * rows)
            out[:, :width] = extra[0][at]
            out[:, width:] = value[at]
    if kind in ("sketch", "probe"):
        for i in range(len(extra)):
            outs.pop(0)[...] = value[i * rows : (i + 1) * rows]
    if kind == "sketch":
        sketched = total.astype(jnp.bfloat16)
        keep, send = outs
        high = keep.shape[1]
        ranks = 2 * keep.shape[0] * high
        piece = None
        for i, omega in enumerate(extra):
            term = jnp.dot(
                omega[:ranks],
                sketched[i * rows : (i + 1) * rows],
                preferred_element_type=jnp.float32,
            )
            piece = term if piece is None else piece + term
        odd = place[0] % 2 == 1
        for q in range(keep.shape[0]):
            low = piece[2 * q * high : (2 * q + 1) * high]
            top = piece[(2 * q + 1) * high : (2 * q + 2) * high]
            keep[q] = jnp.where(odd, top, low)
            send[q] = jnp.where(odd, low, top).astype(jnp.bfloat16)
    if kind == "probe":
        signs = [extra[0][...]]
        for ref in extra[1:]:
            ranks = ref.shape[0] - width
            signs += [ref[ranks:, j * width : (j + 1) * width] for j in range(rows // width)]
        signs = jnp.concatenate(signs).astype(jnp.float32)
        outs[0][...] = jnp.sum(signs * total, axis=0, keepdims=True)


def advance(step, width, kind, scalars, band, groups, lanes, outs):
    tiles = lax.axis_size("xsec")
    flat = [x for group in groups for x in group]
    rows, depth = band[1].shape
    return pl.pallas_call(
        functools.partial(
            step_kernel, step, tiles, width, [len(group) for group in groups], lanes, kind
        ),
        out_shape=outs,
        in_specs=[SCALAR] * len(scalars) + [WHOLE] * (3 + len(flat)),
        out_specs=[WHOLE] * len(outs),
        compiler_params=PARAMS,
        cost_estimate=cost(6 * rows * depth, 6 * rows * depth * width),
    )(*scalars, band[1], band[0], band[2], *flat)


def fold_kernel(hop, place, keep, got, kept, send):
    odd = (place[0] // hop) % 2 == 1
    for q in range(kept.shape[0]):
        low = keep[2 * q] + got[2 * q].astype(jnp.float32)
        top = keep[2 * q + 1] + got[2 * q + 1].astype(jnp.float32)
        kept[q] = jnp.where(odd, top, low)
        send[q] = jnp.where(odd, low, top).astype(jnp.bfloat16)


def mix_kernel(send, *refs):
    terms, (quad, out) = (refs[:-2], refs[-2:])
    rows = send.shape[1]
    total = terms[0][...]
    for term in terms[1:]:
        total = total + term[...]
    quad[...] = total
    high = total.astype(jnp.bfloat16)
    low = (total - high.astype(jnp.float32)).astype(jnp.bfloat16)
    spare = out.shape[0] - rows - 2
    pad = jnp.zeros((spare, total.shape[1]), jnp.float32)
    tail = jnp.concatenate([high.astype(jnp.float32), low.astype(jnp.float32), pad])
    out[:rows] = send[0]
    out[rows:] = tail.astype(jnp.bfloat16)


def finish_kernel(scale, me, keep, got, quad, *outs):
    rows = keep.shape[1]
    count = len(outs)
    share = rows // count
    tail = got[rows:].astype(jnp.float32)
    total = (quad[...] + tail[0:1] + tail[1:2]) * scale
    spare = jnp.zeros((outs[0].shape[0] - share - 1, total.shape[1]), jnp.float32)
    gram = (keep[0] + got[:rows].astype(jnp.float32)) * scale
    for i in range(count):
        picked = gram[:share]
        for b in range(1, count):
            here = (me[0] + i) % count == b
            picked = jnp.where(here, gram[b * share : (b + 1) * share], picked)
        outs[i][:share] = picked
        outs[i][share:] = jnp.concatenate([total, spare])


def place_kernel(me, *refs):
    parts, (gram, quad) = (refs[:-2], refs[-2:])
    count = len(parts)
    share, columns = gram.shape
    width = columns // count
    for b in range(count):
        value = parts[0][...]
        for i in range(1, count):
            value = jnp.where((me[0] - i + count) % count == b, parts[i][...], value)
        gram[:, b * width : (b + 1) * width] = value[:share]
        quad[:, b * width : (b + 1) * width] = value[share : share + 1]


def small(kernel, scalars, arrays, outs):
    return pl.pallas_call(
        kernel,
        out_shape=outs,
        in_specs=[SCALAR] * len(scalars) + [WHOLE] * len(arrays),
        out_specs=[WHOLE] * len(outs),
        compiler_params=PARAMS,
        cost_estimate=cost(sum(4 * x.size for x in arrays)),
    )(*scalars, *arrays)


def program(blocks, pattern, current, previous, accum, coefs, sketch, signs):
    cells, tiles, orbs, wide = blocks.shape
    halves, local_cols = current.shape[3:]
    reach = wide // orbs // 6
    xs, me = (lax.axis_size("xsec"), lax.axis_index("xsec").astype(jnp.int32))
    wires, place = (lax.axis_size("wire"), lax.axis_index("wire").astype(jnp.int32))
    cores, core = (lax.axis_size("cols"), lax.axis_index("cols").astype(jnp.int32))
    width = local_cols // xs
    rows = cells * orbs
    others = range(1, xs)
    assert tiles == 1 and cells == reach and wires % 2 == 0 and cells % cores == 0
    assert halves == 2 and STEPS == 4

    everyone = range(xs)
    assert rows % width == 0

    leaving = deal(current, me[None], others)
    coming = [from_tile(leaving[i - 1], i) for i in others]
    fields = small(
        functools.partial(stack_kernel, xs), [me[None]], [current, *coming],
        [bf16(xs * rows, width)] * halves,
    )

    blocks = blocks[:, 0]
    pattern = pattern[:, 0]
    mine = packed(blocks, pattern, core[None], me[None], cores, min(xs, 3))
    shares = [from_tile(mine, i) for i in others]

    band = ()
    for i in range(xs):
        parts, slot, pieces = ([blocks], core[None], 1)
        if i > 0:
            parts = [shares[i - 1]]
            parts += [from_tile(shares[i - 1], k, "cols") for k in range(1, cores)]
            slot, pieces = (core[None], cores)
        sizes = (cells, orbs, reach, xs, pieces)
        band = band_rows(i, parts, pattern, me[None], place[None], slot, sizes, band)

    dealt = deal(previous, me[None], everyone)
    older = [dealt[0]] + [from_tile(dealt[i], i) for i in others]
    dealt = deal(accum, me[None], everyone)
    starts = dealt
    accums = [dealt[0]] + [from_tile(dealt[i], i) for i in others]
    ranks = sketch.shape[3]
    turned, signed, *leaving = small(
        rest_kernel, [me[None]], [sketch, signs],
        [bf16(ranks, rows), bf16(rows, width)] + [bf16(ranks + width, rows)] * (xs - 1),
    )
    coming = [from_tile(leaving[i - 1], i) for i in others]
    omega, signed = ([turned, *coming], [signed, *coming])

    full = bf16(xs * rows, width)
    piece = bf16(rows, width)
    info = place[None]
    fields = list(fields)
    olders, totals = ([None] * halves, [None] * halves)
    zero = (0,) * xs

    def run(step, h, kind, older, sums, start, extra, lanes, outs):
        near, far = around(fields[h])
        scalars = {"sum": [coefs], "sketch": [info, coefs], "probe": [coefs]}.get(kind, [])
        return advance(
            step, width, kind, scalars, band,
            ([fields[h]], [near], [far], older, sums, start, extra), lanes, outs,
        )

    for h in range(halves):
        (nxt,) = run(0, h, "plain", older, [], [], [], ((h * width,) * xs, (), ()), [full])
        olders[h], fields[h] = (fields[h], nxt)
    for h in range(halves):
        extra = totals[0][1:] if h else []
        outs = [full, f32(rows, width)] + [f32(rows, (h + 1) * width)] * (xs - 1)
        nxt, *totals[h] = run(
            1, h, "sum", [olders[h]], [], [], extra, (zero, (), ()), outs
        )
        olders[h], fields[h] = (fields[h], nxt)
    for h in range(halves):
        kind, extra, outs = ("plain", [], [])
        if h:
            kind, extra, outs = ("before", [fields[0]], [bf16(rows, 2 * width)] * (xs - 1))
        nxt, *befores = run(2, h, kind, [olders[h]], [], [], extra, (zero, (), ()), [full] + outs)
        olders[h], fields[h] = (fields[h], nxt)
    newest, extras = ([None] * halves, [None] * halves)
    part = (wires // 2, ranks // wires, width)
    ends = [("sketch", omega, [f32(*part), bf16(*part)]), ("probe", signed, [f32(1, width)])]
    for h in range(halves):
        kind, extra, outs = ends[h]
        lanes = (zero, (0,) + (h * width,) * (xs - 1), (h * width,) * xs)
        results = run(
            3, h, kind, [olders[h]], totals[h], accums, extra, lanes, [piece] * xs + outs
        )
        newest[h], extras[h] = (results[:xs], results[xs:])
    (keep, send), (quad,) = extras

    hop = 1
    high = ranks // wires
    terms = [quad]
    while 2 * hop < wires:
        got = swap_bits(send, hop)
        terms = [sum(terms[1:], terms[0])]
        terms.append(swap_bits(terms[0], hop))
        hop *= 2
        part = (wires // hop // 2, high, width)
        keep, send = small(
            functools.partial(fold_kernel, hop), [info], [keep, got],
            [f32(*part), bf16(*part)],
        )
    quad, mixed = small(mix_kernel, [], [send, *terms], [f32(1, width), bf16(high + 16, width)])
    mixed = swap_bits(mixed, hop)
    scale = 1.0 / float(rows * wires * tiles * xs) ** 0.5
    finished = small(
        functools.partial(finish_kernel, scale), [me[None]], [keep, mixed, quad],
        [f32(high // xs + 8, width)] * xs,
    )
    finished = [finished[0]] + [to_tile(finished[i], i) for i in others]
    gram, quadratic = small(
        place_kernel, [me[None]], finished, [f32(high // xs, local_cols), f32(1, local_cols)]
    )
    quadratic = quadratic[0]

    sums_back = [totals[0][0], totals[1][0]]
    sums_back += [to_tile(totals[1][i], i) for i in others]
    before_back = [fields[0], fields[1]]
    before_back += [to_tile(befores[i - 1], i) for i in others]
    newest_back = [newest[0][0], newest[1][0]]
    for i in others:
        newest_back += [to_tile(newest[h][i], i) for h in range(halves)]

    def paired(start):
        return [[(start, 0), (start + 1, 0)]] + [
            [(start + 1 + i, 0), (start + 1 + i, width)] for i in others
        ]

    shape = current.shape
    (before,) = small(
        functools.partial(before_kernel, paired(0)), [me[None]], before_back,
        [bf16(*shape)],
    )
    late = [[(2 * i, 0), (2 * i + 1, 0)] for i in everyone]
    arrays, lanes = (list(newest_back), [late])
    for group in (before_back, sums_back):
        lanes.append(paired(len(arrays)))
        arrays += group
    lanes.append([[(len(arrays) + i, h * width) for h in range(halves)] for i in everyone])
    arrays += starts
    last, total = small(
        functools.partial(last_kernel, *lanes), [me[None], coefs], arrays,
        [bf16(*shape), f32(*shape)],
    )
    return (last, before, total, gram, quadratic)


def solution(mesh):
    return jax.shard_map(
        program,
        mesh=mesh,
        in_specs=(
            P(("sample", "wire"), "xsec", None, None),
            P(("sample", "wire"), "xsec", None),
            P(("sample", "wire"), "xsec", None, None, "cols"),
            P(("sample", "wire"), "xsec", None, None, "cols"),
            P(("sample", "wire"), "xsec", None, None, "cols"),
            P(),
            P(("sample", "wire"), "xsec", None, None),
            P(("sample", "wire"), "xsec", None, "cols"),
        ),
        out_specs=(
            P(("sample", "wire"), "xsec", None, None, "cols"),
            P(("sample", "wire"), "xsec", None, None, "cols"),
            P(("sample", "wire"), "xsec", None, None, "cols"),
            P(("sample", "wire", "xsec"), "cols"),
            P(("sample", "cols")),
        ),
        check_vma=False,
    )
```

time: 89.7 us -> 88.5 us (0.987)
  waiting for transfers between devices: 20.3 us -> 25.9 us
  starting transfers between devices: 45.9 us -> 40.9 us
  local copies, waits for them, and re-layouts: 2.99 us -> 1.89 us
    pallas_call x13 -> x8, Pallas kernels: 15.3 us -> 7.34 us  [advance(): pl.pallas_call(functools.partial(step_kernel, step, tiles, width, [len(gr...]
    pallas_call x5 -> x11, Pallas kernels: 0.85 us -> 8.22 us  [small(): pl.pallas_call(kernel, out_shape=outs, in_specs=[SCALAR] * len(scalars) +...]
    ppermute x14 -> x11, starting transfers between devices: 17.2 us -> 14 us  [from_tile(): lax.ppermute(x, axis, [((i + offset) % size, i) for i in range(size)])]
    ppermute x3, waiting for transfers between devices: 2.16 us -> 5.25 us  [swap_bits(): lax.ppermute(x, 'wire', [(i, i ^ hop) for i in range(lax.axis_size('wire'...]
    ppermute x3, starting transfers between devices: 4.41 us -> 2.35 us  [swap_bits(): lax.ppermute(x, 'wire', [(i, i ^ hop) for i in range(lax.axis_size('wire'...]
    ppermute x14 -> x11, waiting for transfers between devices: 8.65 us -> 10.4 us  [from_tile(): lax.ppermute(x, axis, [((i + offset) % size, i) for i in range(size)])]
    ppermute x8, starting transfers between devices: 5.13 us -> 6.71 us  [around(): one = lax.ppermute(x, 'wire', first)]
    ppermute x8, starting transfers between devices: 19.1 us -> 17.9 us  [around(): two = lax.ppermute(x, 'wire', second)]
  transfers between devices with their start and end apart: 33 -> 30, of which waited for: 12 -> 12; matrix products, arithmetic and copies ran while one was open for 1% -> 0% of each run, Pallas kernels for 20% -> 20%
where the time goes in v4:
time: 88.5 us; the launch traced here: 88.3 us
  starting transfers between devices  40.9 us (46%)
  waiting for transfers between devices  25.9 us (29%)
  Pallas kernels  18.8 us (21%)
  local copies, waits for them, and re-layouts  1.89 us (2%)
    ppermute x8, starting transfers between devices, around(): two = lax.ppermute(x, 'wire', second)  17.9 us
    ppermute x11, starting transfers between devices, from_tile(): lax.ppermute(x, axis, [((i + offset) % size, i) for i in range(size)])  14 us
    ppermute x11, waiting for transfers between devices, from_tile(): lax.ppermute(x, axis, [((i + offset) % size, i) for i in range(size)])  10.4 us
    ppermute x8, waiting for transfers between devices, around(): two = lax.ppermute(x, 'wire', second)  8.33 us
    pallas_call x11, Pallas kernels, small(): pl.pallas_call(kernel, out_shape=outs, in_specs=[SCALAR] * len(scalars) +...  8.22 us
    pallas_call x8, Pallas kernels, advance(): pl.pallas_call(functools.partial(step_kernel, step, tiles, width, [len(gr...  7.34 us
    ppermute x8, starting transfers between devices, around(): one = lax.ppermute(x, 'wire', first)  6.71 us
    ppermute x3, waiting for transfers between devices, swap_bits(): lax.ppermute(x, 'wire', [(i, i ^ hop) for i in range(lax.axis_size('wire'...  5.25 us
  transfers between devices with their start and end apart: 30, of which 12 were waited for; matrix products, arithmetic and copies ran while one was open for 0% of the time, Pallas kernels for 20%

profile of v4, /device:TPU:0, one launch (start us, length us, event | category | flops | bytes accessed | tf_op | source)
XLA Modules:
  0.0 88.3 jit_solution(10027533282957196384)
XLA Ops:
  3.3 3.0 %collective-permute-start = (bf16[2,64,1152]{2,1,0:T(8,128)(2,1)S(1)}, bf16[2,64,1152]{2,1,0:T(8,128)(2,1)S(1)}, u32[]{:S(2)}, u32[]{:S(2)}) collective-permute-start(bf16[2,64,1152]{2,1,0:T(8,128)(2,1)S(1)} %shard_map.119), channel_id=1, source_target_pairs={{2,0},{0,2},{3,1},{1,3},{6,4},{4,6},{7,5},{5,7},{10,8},{8,10},{11,... | collective-permute-start | bytes 884744 | tf_op jit(solution)/shard_map/ppermute | solution.py:31
  6.4 7.0 %collective-permute-done.refs_0_ = bf16[2,64,1152]{2,1,0:T(8,128)(2,1)S(1)} collective-permute-done((bf16[2,64,1152]{2,1,0:T(8,128)(2,1)S(1)}, bf16[2,64,1152]{2,1,0:T(8,128)(2,1)S(1)}, u32[]{:S(2)}, u32[]{:S(2)}) %collective-permute-start) | collective-permute-done | bytes 294944 | tf_op jit(solution)/shard_map/ppermute | solution.py:31
  13.9 1.8 %collective-permute-start.2 = (bf16[256,256]{1,0:T(8,128)(2,1)S(1)}, bf16[256,256]{1,0:T(8,128)(2,1)S(1)}, u32[]{:S(2)}, u32[]{:S(2)}) collective-permute-start(bf16[256,256]{1,0:T(8,128)(2,1)S(1)} %shard_map.122), channel_id=1, source_target_pairs={{2,0},{0,2},{3,1},{1,3},{6,4},{4,6},{7,5},{5,7},{10,8},{8,10},{11,... | collective-permute-start | bytes 393224 | tf_op jit(solution)/shard_map/ppermute | solution.py:31
  16.9 3.3 %collective-permute-done.2.refs_0_ = bf16[256,256]{1,0:T(8,128)(2,1)S(1)} collective-permute-done((bf16[256,256]{1,0:T(8,128)(2,1)S(1)}, bf16[256,256]{1,0:T(8,128)(2,1)S(1)}, u32[]{:S(2)}, u32[]{:S(2)}) %collective-permute-start.2) | collective-permute-done | bytes 131104 | tf_op jit(solution)/shard_map/ppermute | solution.py:31
  20.7 1.9 %collective-permute-start.3 = (bf16[512,128]{1,0:T(8,128)(2,1)S(1)}, bf16[512,128]{1,0:T(8,128)(2,1)S(1)}, u32[]{:S(2)}, u32[]{:S(2)}) collective-permute-start(bf16[512,128]{1,0:T(8,128)(2,1)S(1)} %get-tuple-element.51.refs_3_.refs_7_), channel_id=1, source_target_pairs={{0,4},{4,0},{8,12},{12,8},{1,5},{5,1},{9,13},{13,9},{2,6},{6,2},{1... | collective-permute-start | bytes 393224 | tf_op jit(solution)/shard_map/ppermute | solution.py:45
  22.7 2.5 %collective-permute-start.4 = (bf16[512,128]{1,0:T(8,128)(2,1)S(1)}, bf16[512,128]{1,0:T(8,128)(2,1)S(1)}, u32[]{:S(2)}, u32[]{:S(2)}) collective-permute-start(bf16[512,128]{1,0:T(8,128)(2,1)S(1)} %get-tuple-element.51.refs_3_.refs_7_), channel_id=1, source_target_pairs={{4,8},{8,4},{12,0},{0,12},{5,9},{9,5},{13,1},{1,13},{6,10},{10,6},... | collective-permute-start | bytes 393224 | tf_op jit(solution)/shard_map/ppermute | solution.py:46
  29.2 3.3 %collective-permute-done.4.refs_5_ = bf16[512,128]{1,0:T(8,128)(2,1)S(1)} collective-permute-done((bf16[512,128]{1,0:T(8,128)(2,1)S(1)}, bf16[512,128]{1,0:T(8,128)(2,1)S(1)}, u32[]{:S(2)}, u32[]{:S(2)}) %collective-permute-start.4) | collective-permute-done | bytes 131104 | tf_op jit(solution)/shard_map/ppermute | solution.py:46
  33.1 3.5 %collective-permute-start.7 = (bf16[512,128]{1,0:T(8,128)(2,1)S(1)}, bf16[512,128]{1,0:T(8,128)(2,1)S(1)}, u32[]{:S(2)}, u32[]{:S(2)}) collective-permute-start(bf16[512,128]{1,0:T(8,128)(2,1)S(1)} %shard_map.125.refs_4_.refs_6_), channel_id=1, source_target_pairs={{4,8},{8,4},{12,0},{0,12},{5,9},{9,5},{13,1},{1,13},{6,10},{10,6},... | collective-permute-start | bytes 393224 | tf_op jit(solution)/shard_map/ppermute | solution.py:46
  38.7 3.2 %collective-permute-start.17 = (bf16[512,128]{1,0:T(8,128)(2,1)S(1)}, bf16[512,128]{1,0:T(8,128)(2,1)S(1)}, u32[]{:S(2)}, u32[]{:S(2)}) collective-permute-start(bf16[512,128]{1,0:T(8,128)(2,1)S(1)} %shard_map.131.refs_4_.refs_6_), channel_id=1, source_target_pairs={{4,8},{8,4},{12,0},{0,12},{5,9},{9,5},{13,1},{1,13},{6,10},{10,6},... | collective-permute-start | bytes 393224 | tf_op jit(solution)/shard_map/ppermute | solution.py:46
  42.1 1.6 %collective-permute-start.13 = (bf16[640,256]{1,0:T(8,128)(2,1)S(1)}, bf16[640,256]{1,0:T(8,128)(2,1)S(1)}, u32[]{:S(2)}, u32[]{:S(2)}) collective-permute-start(bf16[640,256]{1,0:T(8,128)(2,1)S(1)} %get-tuple-element.60), channel_id=1, source_target_pairs={{2,0},{0,2},{3,1},{1,3},{6,4},{4,6},{7,5},{5,7},{10,8},{8,10},{11,... | collective-permute-start | bytes 983048 | tf_op jit(solution)/shard_map/ppermute | solution.py:31
  45.9 1.6 %collective-permute-start.12 = (f32[256,256]{1,0:T(8,128)S(1)}, f32[256,256]{1,0:T(8,128)S(1)}, u32[]{:S(2)}, u32[]{:S(2)}) collective-permute-start(f32[256,256]{1,0:T(8,128)S(1)} %get-tuple-element.58.refs_11_), channel_id=1, source_target_pairs={{2,0},{0,2},{3,1},{1,3},{6,4},{4,6},{7,5},{5,7},{10,8},{8,10},{11,... | collective-permute-start | bytes 786440 | tf_op jit(solution)/shard_map/ppermute | solution.py:31
  47.4 3.2 %collective-permute-start.9 = (bf16[512,128]{1,0:T(8,128)(2,1)S(1)}, bf16[512,128]{1,0:T(8,128)(2,1)S(1)}, u32[]{:S(2)}, u32[]{:S(2)}) collective-permute-start(bf16[512,128]{1,0:T(8,128)(2,1)S(1)} %get-tuple-element.54.refs_3_.refs_8_), channel_id=1, source_target_pairs={{4,8},{8,4},{12,0},{0,12},{5,9},{9,5},{13,1},{1,13},{6,10},{10,6},... | collective-permute-start | bytes 393224 | tf_op jit(solution)/shard_map/ppermute | solution.py:46
  51.8 1.6 %collective-permute-done.8.refs_4_ = bf16[512,128]{1,0:T(8,128)(2,1)S(1)} collective-permute-done((bf16[512,128]{1,0:T(8,128)(2,1)S(1)}, bf16[512,128]{1,0:T(8,128)(2,1)S(1)}, u32[]{:S(2)}, u32[]{:S(2)}) %collective-permute-start.8) | collective-permute-done | bytes 131104 | tf_op jit(solution)/shard_map/ppermute | solution.py:45
  53.8 2.0 %collective-permute-done.9.refs_5_ = bf16[512,128]{1,0:T(8,128)(2,1)S(1)} collective-permute-done((bf16[512,128]{1,0:T(8,128)(2,1)S(1)}, bf16[512,128]{1,0:T(8,128)(2,1)S(1)}, u32[]{:S(2)}, u32[]{:S(2)}) %collective-permute-start.9) | collective-permute-done | bytes 131104 | tf_op jit(solution)/shard_map/ppermute | solution.py:46
  56.3 2.2 %collective-permute-start.10 = (bf16[512,128]{1,0:T(8,128)(2,1)S(1)}, bf16[512,128]{1,0:T(8,128)(2,1)S(1)}, u32[]{:S(2)}, u32[]{:S(2)}) collective-permute-start(bf16[512,128]{1,0:T(8,128)(2,1)S(1)} %shard_map.127.refs_5_.refs_7_.refs_4_.refs_0_), channel_id=1, source_target_pairs={{0,4},{4,0},{8,12},{12,8},{1,5},{5,1},{9,13},{13,9},{2,6},{6,2},{1... | collective-permute-start | bytes 393224 | tf_op jit(solution)/shard_map/ppermute | solution.py:45
  58.9 2.8 %collective-permute-start.11 = (bf16[512,128]{1,0:T(8,128)(2,1)S(1)}, bf16[512,128]{1,0:T(8,128)(2,1)S(1)}, u32[]{:S(2)}, u32[]{:S(2)}) collective-permute-start(bf16[512,128]{1,0:T(8,128)(2,1)S(1)} %shard_map.127.refs_5_.refs_7_.refs_4_.refs_0_), channel_id=1, source_target_pairs={{4,8},{8,4},{12,0},{0,12},{5,9},{9,5},{13,1},{1,13},{6,10},{10,6},... | collective-permute-start | bytes 393224 | tf_op jit(solution)/shard_map/ppermute | solution.py:46
  61.7 1.5 %collective-permute-start.25 = (f32[256,256]{1,0:T(8,128)S(1)}, f32[256,256]{1,0:T(8,128)S(1)}, u32[]{:S(2)}, u32[]{:S(2)}) collective-permute-start(f32[256,256]{1,0:T(8,128)S(1)} %get-tuple-element.66.refs_9_), channel_id=1, source_target_pairs={{2,0},{0,2},{3,1},{1,3},{6,4},{4,6},{7,5},{5,7},{10,8},{8,10},{11,... | collective-permute-start | bytes 786440 | tf_op jit(solution)/shard_map/ppermute | solution.py:31
  63.8 1.6 %collective-permute-start.20 = (bf16[512,128]{1,0:T(8,128)(2,1)S(1)}, bf16[512,128]{1,0:T(8,128)(2,1)S(1)}, u32[]{:S(2)}, u32[]{:S(2)}) collective-permute-start(bf16[512,128]{1,0:T(8,128)(2,1)S(1)} %get-tuple-element.64.refs_4_.refs_5_.refs_1_), channel_id=1, source_target_pairs={{0,4},{4,0},{8,12},{12,8},{1,5},{5,1},{9,13},{13,9},{2,6},{6,2},{1... | collective-permute-start | bytes 393224 | tf_op jit(solution)/shard_map/ppermute | solution.py:45
  65.4 1.5 %collective-permute-start.21 = (bf16[512,128]{1,0:T(8,128)(2,1)S(1)}, bf16[512,128]{1,0:T(8,128)(2,1)S(1)}, u32[]{:S(2)}, u32[]{:S(2)}) collective-permute-start(bf16[512,128]{1,0:T(8,128)(2,1)S(1)} %get-tuple-element.64.refs_4_.refs_5_.refs_1_), channel_id=1, source_target_pairs={{4,8},{8,4},{12,0},{0,12},{5,9},{9,5},{13,1},{1,13},{6,10},{10,6},... | collective-permute-start | bytes 393224 | tf_op jit(solution)/shard_map/ppermute | solution.py:46
  67.7 1.6 %shard_map.130 = (bf16[256,128]{1,0:T(8,128)(2,1)S(1)}, bf16[256,128]{1,0:T(8,128)(2,1)S(1)}, f32[2,128,128]{2,1,0:T(8,128)S(1)}, bf16[2,128,128]{2,1,0:T(8,128)(2,1)S(1)}) custom-call(s32[1]{0:T(128)} %bitcast.1.place.refs_0_, f32[4]{0:T(128)S(1)} %copy-done.8, bf16[512,512]{1,0:T(8,128)(2,1)S(1)} %get-tuple-element.48.refs_0_.refs_1_.refs_2_, ...), custom_call_target="tpu_custom_call" | custom-call | flops 201326592 | bytes 1572864 | tf_op jit(solution)/shard_map/pallas_call | solution.py:353
  73.8 3.1 %collective-permute-done.27.refs_1_ = f32[1,128]{1,0:T(1,128)S(1)} collective-permute-done((f32[1,128]{1,0:T(1,128)S(1)}, f32[1,128]{1,0:T(1,128)S(1)}, u32[]{:S(2)}, u32[]{:S(2)}) %collective-permute-start.27) | collective-permute-done | bytes 544 | tf_op jit(solution)/shard_map/ppermute | solution.py:51
  80.0 2.1 %collective-permute-done.28.got = bf16[144,128]{1,0:T(8,128)(2,1)S(1)} collective-permute-done((bf16[144,128]{1,0:T(8,128)(2,1)S(1)}, bf16[144,128]{1,0:T(8,128)(2,1)S(1)}, u32[]{:S(2)}, u32[]{:S(2)}) %collective-permute-start.28) | collective-permute-done | bytes 36896 | tf_op jit(solution)/shard_map/ppermute | solution.py:51
  82.9 1.7 %shard_map.136 = bf16[4,1,64,2,256]{4,3,2,1,0:T(2,128)(2,1)} custom-call(s32[1]{0:T(128)} %bitcast.me, bf16[512,128]{1,0:T(8,128)(2,1)S(1)} %shard_map.127.refs_5_.refs_7_.refs_4_.refs_0_, bf16[512,128]{1,0:T(8,128)(2,1)S(1)} %get-tuple-element.64.refs_4_.refs_5_.refs_1_, bf16[256,256]{1,0:T(8,128)(2,1)S(1)} %collective-permute-done.24.refs_6_.refs_2_), custom_call_target="tpu_custom_call" | custom-call | bytes 786432 | tf_op jit(solution)/shard_map/pallas_call | solution.py:421
  84.7 3.0 %shard_map.135 = (bf16[4,1,64,2,256]{4,3,2,1,0:T(2,128)(2,1)}, f32[4,1,64,2,256]{4,3,2,1,0:T(2,128)}) custom-call(s32[1]{0:T(128)} %bitcast.me, f32[4]{0:T(128)S(1)} %copy-done.8, bf16[256,128]{1,0:T(8,128)(2,1)S(1)} %get-tuple-element.61.refs_0_, bf16[256,128]{1,0:T(8,128)(2,1)S(1)} %get-tuple-element.68.refs_1_, ...), custom_call_target="tpu_custom_call" | custom-call | bytes 2359296 | tf_op jit(solution)/shard_map/pallas_call | solution.py:421
  (76 shorter events, 26.9 us)
Async XLA Ops:
  3.3 10.0 %collective-permute-start = (bf16[2,64,1152]{2,1,0:T(8,128)(2,1)S(1)}, bf16[2,64,1152]{2,1,0:T(8,128)(2,1)S(1)}, u32[]{:S(2)}, u32[]{:S(2)}) collective-permute-start(bf16[2,64,1152]{2,1,0:T(8,128)(2,1)S(1)} %shard_map.119), channel_id=1, source_target_pairs={{2,0},{0,2},{3,1},{1,3},{6,4},{4,6},{7,5},{5,7},{10,8},{8,10},{11,... | collective-permute-start | bytes 884744 | tf_op jit(solution)/shard_map/ppermute | solution.py:31
  13.4 12.4 %collective-permute-start.1 = (bf16[2,64,1152]{2,1,0:T(8,128)(2,1)S(1)}, bf16[2,64,1152]{2,1,0:T(8,128)(2,1)S(1)}, u32[]{:S(2)}, u32[]{:S(2)}) collective-permute-start(bf16[2,64,1152]{2,1,0:T(8,128)(2,1)S(1)} %collective-permute-done.refs_0_), channel_id=1, source_target_pairs={{1,0},{0,1},{3,2},{2,3},{5,4},{4,5},{7,6},{6,7},{9,8},{8,9},{11,10... | collective-permute-start | bytes 884744 | tf_op jit(solution)/shard_map/ppermute | solution.py:31
  16.5 12.6 %collective-permute-start.5 = (bf16[256,256]{1,0:T(8,128)(2,1)S(1)}, bf16[256,256]{1,0:T(8,128)(2,1)S(1)}, u32[]{:S(2)}, u32[]{:S(2)}) collective-permute-start(bf16[256,256]{1,0:T(8,128)(2,1)S(1)} %get-tuple-element.53), channel_id=1, source_target_pairs={{2,0},{0,2},{3,1},{1,3},{6,4},{4,6},{7,5},{5,7},{10,8},{8,10},{11,... | collective-permute-start | bytes 393224 | tf_op jit(solution)/shard_map/ppermute | solution.py:31
  20.7 8.5 %collective-permute-start.3 = (bf16[512,128]{1,0:T(8,128)(2,1)S(1)}, bf16[512,128]{1,0:T(8,128)(2,1)S(1)}, u32[]{:S(2)}, u32[]{:S(2)}) collective-permute-start(bf16[512,128]{1,0:T(8,128)(2,1)S(1)} %get-tuple-element.51.refs_3_.refs_7_), channel_id=1, source_target_pairs={{0,4},{4,0},{8,12},{12,8},{1,5},{5,1},{9,13},{13,9},{2,6},{6,2},{1... | collective-permute-start | bytes 393224 | tf_op jit(solution)/shard_map/ppermute | solution.py:45
  22.7 9.8 %collective-permute-start.4 = (bf16[512,128]{1,0:T(8,128)(2,1)S(1)}, bf16[512,128]{1,0:T(8,128)(2,1)S(1)}, u32[]{:S(2)}, u32[]{:S(2)}) collective-permute-start(bf16[512,128]{1,0:T(8,128)(2,1)S(1)} %get-tuple-element.51.refs_3_.refs_7_), channel_id=1, source_target_pairs={{4,8},{8,4},{12,0},{0,12},{5,9},{9,5},{13,1},{1,13},{6,10},{10,6},... | collective-permute-start | bytes 393224 | tf_op jit(solution)/shard_map/ppermute | solution.py:46
  25.1 11.5 %collective-permute-start.14 = (bf16[512,128]{1,0:T(8,128)(2,1)S(1)}, bf16[512,128]{1,0:T(8,128)(2,1)S(1)}, u32[]{:S(2)}, u32[]{:S(2)}) collective-permute-start(bf16[512,128]{1,0:T(8,128)(2,1)S(1)} %get-tuple-element.62.refs_3_.refs_7_), channel_id=1, source_target_pairs={{0,4},{4,0},{8,12},{12,8},{1,5},{5,1},{9,13},{13,9},{2,6},{6,2},{1... | collective-permute-start | bytes 393224 | tf_op jit(solution)/shard_map/ppermute | solution.py:45
  25.8 12.2 %collective-permute-start.15 = (bf16[512,128]{1,0:T(8,128)(2,1)S(1)}, bf16[512,128]{1,0:T(8,128)(2,1)S(1)}, u32[]{:S(2)}, u32[]{:S(2)}) collective-permute-start(bf16[512,128]{1,0:T(8,128)(2,1)S(1)} %get-tuple-element.62.refs_3_.refs_7_), channel_id=1, source_target_pairs={{4,8},{8,4},{12,0},{0,12},{5,9},{9,5},{13,1},{1,13},{6,10},{10,6},... | collective-permute-start | bytes 393224 | tf_op jit(solution)/shard_map/ppermute | solution.py:46
  33.0 10.6 %collective-permute-start.6 = (bf16[512,128]{1,0:T(8,128)(2,1)S(1)}, bf16[512,128]{1,0:T(8,128)(2,1)S(1)}, u32[]{:S(2)}, u32[]{:S(2)}) collective-permute-start(bf16[512,128]{1,0:T(8,128)(2,1)S(1)} %shard_map.125.refs_4_.refs_6_), channel_id=1, source_target_pairs={{0,4},{4,0},{8,12},{12,8},{1,5},{5,1},{9,13},{13,9},{2,6},{6,2},{1... | collective-permute-start | bytes 393224 | tf_op jit(solution)/shard_map/ppermute | solution.py:45
  33.1 10.7 %collective-permute-start.7 = (bf16[512,128]{1,0:T(8,128)(2,1)S(1)}, bf16[512,128]{1,0:T(8,128)(2,1)S(1)}, u32[]{:S(2)}, u32[]{:S(2)}) collective-permute-start(bf16[512,128]{1,0:T(8,128)(2,1)S(1)} %shard_map.125.refs_4_.refs_6_), channel_id=1, source_target_pairs={{4,8},{8,4},{12,0},{0,12},{5,9},{9,5},{13,1},{1,13},{6,10},{10,6},... | collective-permute-start | bytes 393224 | tf_op jit(solution)/shard_map/ppermute | solution.py:46
  38.6 8.8 %collective-permute-start.16 = (bf16[512,128]{1,0:T(8,128)(2,1)S(1)}, bf16[512,128]{1,0:T(8,128)(2,1)S(1)}, u32[]{:S(2)}, u32[]{:S(2)}) collective-permute-start(bf16[512,128]{1,0:T(8,128)(2,1)S(1)} %shard_map.131.refs_4_.refs_6_), channel_id=1, source_target_pairs={{0,4},{4,0},{8,12},{12,8},{1,5},{5,1},{9,13},{13,9},{2,6},{6,2},{1... | collective-permute-start | bytes 393224 | tf_op jit(solution)/shard_map/ppermute | solution.py:45
  38.7 11.9 %collective-permute-start.17 = (bf16[512,128]{1,0:T(8,128)(2,1)S(1)}, bf16[512,128]{1,0:T(8,128)(2,1)S(1)}, u32[]{:S(2)}, u32[]{:S(2)}) collective-permute-start(bf16[512,128]{1,0:T(8,128)(2,1)S(1)} %shard_map.131.refs_4_.refs_6_), channel_id=1, source_target_pairs={{4,8},{8,4},{12,0},{0,12},{5,9},{9,5},{13,1},{1,13},{6,10},{10,6},... | collective-permute-start | bytes 393224 | tf_op jit(solution)/shard_map/ppermute | solution.py:46
  42.1 23.3 %collective-permute-start.13 = (bf16[640,256]{1,0:T(8,128)(2,1)S(1)}, bf16[640,256]{1,0:T(8,128)(2,1)S(1)}, u32[]{:S(2)}, u32[]{:S(2)}) collective-permute-start(bf16[640,256]{1,0:T(8,128)(2,1)S(1)} %get-tuple-element.60), channel_id=1, source_target_pairs={{2,0},{0,2},{3,1},{1,3},{6,4},{4,6},{7,5},{5,7},{10,8},{8,10},{11,... | collective-permute-start | bytes 983048 | tf_op jit(solution)/shard_map/ppermute | solution.py:31
  45.0 8.4 %collective-permute-start.8 = (bf16[512,128]{1,0:T(8,128)(2,1)S(1)}, bf16[512,128]{1,0:T(8,128)(2,1)S(1)}, u32[]{:S(2)}, u32[]{:S(2)}) collective-permute-start(bf16[512,128]{1,0:T(8,128)(2,1)S(1)} %get-tuple-element.54.refs_3_.refs_8_), channel_id=1, source_target_pairs={{0,4},{4,0},{8,12},{12,8},{1,5},{5,1},{9,13},{13,9},{2,6},{6,2},{1... | collective-permute-start | bytes 393224 | tf_op jit(solution)/shard_map/ppermute | solution.py:45
  45.9 17.9 %collective-permute-start.12 = (f32[256,256]{1,0:T(8,128)S(1)}, f32[256,256]{1,0:T(8,128)S(1)}, u32[]{:S(2)}, u32[]{:S(2)}) collective-permute-start(f32[256,256]{1,0:T(8,128)S(1)} %get-tuple-element.58.refs_11_), channel_id=1, source_target_pairs={{2,0},{0,2},{3,1},{1,3},{6,4},{4,6},{7,5},{5,7},{10,8},{8,10},{11,... | collective-permute-start | bytes 786440 | tf_op jit(solution)/shard_map/ppermute | solution.py:31
  47.4 8.3 %collective-permute-start.9 = (bf16[512,128]{1,0:T(8,128)(2,1)S(1)}, bf16[512,128]{1,0:T(8,128)(2,1)S(1)}, u32[]{:S(2)}, u32[]{:S(2)}) collective-permute-start(bf16[512,128]{1,0:T(8,128)(2,1)S(1)} %get-tuple-element.54.refs_3_.refs_8_), channel_id=1, source_target_pairs={{4,8},{8,4},{12,0},{0,12},{5,9},{9,5},{13,1},{1,13},{6,10},{10,6},... | collective-permute-start | bytes 393224 | tf_op jit(solution)/shard_map/ppermute | solution.py:46
  51.7 7.1 %collective-permute-start.18 = (bf16[512,128]{1,0:T(8,128)(2,1)S(1)}, bf16[512,128]{1,0:T(8,128)(2,1)S(1)}, u32[]{:S(2)}, u32[]{:S(2)}) collective-permute-start(bf16[512,128]{1,0:T(8,128)(2,1)S(1)} %get-tuple-element.63.refs_3_.refs_7_), channel_id=1, source_target_pairs={{0,4},{4,0},{8,12},{12,8},{1,5},{5,1},{9,13},{13,9},{2,6},{6,2},{1... | collective-permute-start | bytes 393224 | tf_op jit(solution)/shard_map/ppermute | solution.py:45
  53.4 8.3 %collective-permute-start.19 = (bf16[512,128]{1,0:T(8,128)(2,1)S(1)}, bf16[512,128]{1,0:T(8,128)(2,1)S(1)}, u32[]{:S(2)}, u32[]{:S(2)}) collective-permute-start(bf16[512,128]{1,0:T(8,128)(2,1)S(1)} %get-tuple-element.63.refs_3_.refs_7_), channel_id=1, source_target_pairs={{4,8},{8,4},{12,0},{0,12},{5,9},{9,5},{13,1},{1,13},{6,10},{10,6},... | collective-permute-start | bytes 393224 | tf_op jit(solution)/shard_map/ppermute | solution.py:46
  56.3 10.5 %collective-permute-start.10 = (bf16[512,128]{1,0:T(8,128)(2,1)S(1)}, bf16[512,128]{1,0:T(8,128)(2,1)S(1)}, u32[]{:S(2)}, u32[]{:S(2)}) collective-permute-start(bf16[512,128]{1,0:T(8,128)(2,1)S(1)} %shard_map.127.refs_5_.refs_7_.refs_4_.refs_0_), channel_id=1, source_target_pairs={{0,4},{4,0},{8,12},{12,8},{1,5},{5,1},{9,13},{13,9},{2,6},{6,2},{1... | collective-permute-start | bytes 393224 | tf_op jit(solution)/shard_map/ppermute | solution.py:45
  58.9 8.8 %collective-permute-start.11 = (bf16[512,128]{1,0:T(8,128)(2,1)S(1)}, bf16[512,128]{1,0:T(8,128)(2,1)S(1)}, u32[]{:S(2)}, u32[]{:S(2)}) collective-permute-start(bf16[512,128]{1,0:T(8,128)(2,1)S(1)} %shard_map.127.refs_5_.refs_7_.refs_4_.refs_0_), channel_id=1, source_target_pairs={{4,8},{8,4},{12,0},{0,12},{5,9},{9,5},{13,1},{1,13},{6,10},{10,6},... | collective-permute-start | bytes 393224 | tf_op jit(solution)/shard_map/ppermute | solution.py:46
  61.7 23.0 %collective-permute-start.25 = (f32[256,256]{1,0:T(8,128)S(1)}, f32[256,256]{1,0:T(8,128)S(1)}, u32[]{:S(2)}, u32[]{:S(2)}) collective-permute-start(f32[256,256]{1,0:T(8,128)S(1)} %get-tuple-element.66.refs_9_), channel_id=1, source_target_pairs={{2,0},{0,2},{3,1},{1,3},{6,4},{4,6},{7,5},{5,7},{10,8},{8,10},{11,... | collective-permute-start | bytes 786440 | tf_op jit(solution)/shard_map/ppermute | solution.py:31
  63.8 7.8 %collective-permute-start.20 = (bf16[512,128]{1,0:T(8,128)(2,1)S(1)}, bf16[512,128]{1,0:T(8,128)(2,1)S(1)}, u32[]{:S(2)}, u32[]{:S(2)}) collective-permute-start(bf16[512,128]{1,0:T(8,128)(2,1)S(1)} %get-tuple-element.64.refs_4_.refs_5_.refs_1_), channel_id=1, source_target_pairs={{0,4},{4,0},{8,12},{12,8},{1,5},{5,1},{9,13},{13,9},{2,6},{6,2},{1... | collective-permute-start | bytes 393224 | tf_op jit(solution)/shard_map/ppermute | solution.py:45
  65.4 6.8 %collective-permute-start.21 = (bf16[512,128]{1,0:T(8,128)(2,1)S(1)}, bf16[512,128]{1,0:T(8,128)(2,1)S(1)}, u32[]{:S(2)}, u32[]{:S(2)}) collective-permute-start(bf16[512,128]{1,0:T(8,128)(2,1)S(1)} %get-tuple-element.64.refs_4_.refs_5_.refs_1_), channel_id=1, source_target_pairs={{4,8},{8,4},{12,0},{0,12},{5,9},{9,5},{13,1},{1,13},{6,10},{10,6},... | collective-permute-start | bytes 393224 | tf_op jit(solution)/shard_map/ppermute | solution.py:46
  70.2 12.8 %collective-permute-start.24 = (bf16[256,256]{1,0:T(8,128)(2,1)S(1)}, bf16[256,256]{1,0:T(8,128)(2,1)S(1)}, u32[]{:S(2)}, u32[]{:S(2)}) collective-permute-start(bf16[256,256]{1,0:T(8,128)(2,1)S(1)} %get-tuple-element.71), channel_id=1, source_target_pairs={{2,0},{0,2},{3,1},{1,3},{6,4},{4,6},{7,5},{5,7},{10,8},{8,10},{11,... | collective-permute-start | bytes 393224 | tf_op jit(solution)/shard_map/ppermute | solution.py:31
  78.0 6.7 %collective-permute-start.23 = (bf16[256,128]{1,0:T(8,128)(2,1)S(1)}, bf16[256,128]{1,0:T(8,128)(2,1)S(1)}, u32[]{:S(2)}, u32[]{:S(2)}) collective-permute-start(bf16[256,128]{1,0:T(8,128)(2,1)S(1)} %get-tuple-element.70), channel_id=1, source_target_pairs={{2,0},{0,2},{3,1},{1,3},{6,4},{4,6},{7,5},{5,7},{10,8},{8,10},{11,... | collective-permute-start | bytes 196616 | tf_op jit(solution)/shard_map/ppermute | solution.py:31
  (15 other events, 102.5 us)

commit v5 on v4

--- a/solution.py
+++ b/solution.py
@@ -86,14 +86,13 @@
     )
 
 
-def stack_kernel(count, me, current, *refs):
-    got, outs = (refs[: count - 1], refs[count - 1 :])
-    width = outs[0].shape[1]
-    rows = outs[0].shape[0] // count
-    for h, out in enumerate(outs):
-        out[:rows] = own_block(me, half_of(current, h), 0, count).astype(out.dtype)
-        for i, ref in enumerate(got):
-            out[(i + 1) * rows : (i + 2) * rows] = ref[:, h * width : (h + 1) * width]
+def stack_kernel(*refs):
+    count = len(refs) - 2
+    width = refs[-1].shape[1]
+    rows = refs[0].shape[0]
+    for h, out in enumerate(refs[count:]):
+        for i, ref in enumerate(refs[:count]):
+            out[i * rows : (i + 1) * rows] = ref[:, h * width : (h + 1) * width]
 
 
 def rest_kernel(me, sketch, signs, turned, own, *outs):
@@ -146,8 +145,8 @@
             at = slice(b * width, (b + 1) * width)
             shape = (cells, orbs, width)
             newest[:, 0, :, h, at] = late.astype(newest.dtype).reshape(shape)
-            total = start + total + coef[STEPS - 2] * mid
-            total = total + coef[STEPS - 1] * late
+            total = start + total + coef[:, STEPS - 2 : STEPS - 1] * mid
+            total = total + coef[:, STEPS - 1 : STEPS] * late
             summed[:, 0, :, h, at] = total.reshape(shape)
 
 
@@ -272,8 +271,8 @@
         return taken
 
     place = take(1)[0] if kind == "sketch" else None
+    own, first, second = take(3)
     coef = take(1)[0] if kind in ("sum", "sketch", "probe") else None
-    own, first, second = take(3)
     field, near, far, older, sums, start, extra = [take(n) for n in counts]
     outs = refs
 
@@ -299,7 +298,7 @@
         outs.pop(0)[...] = value
     if kind in ("sum", "sketch", "probe"):
         now = jnp.concatenate([ref[...] for ref in field]).astype(jnp.float32)
-        total = coef[step - 1] * now + coef[step] * value.astype(jnp.float32)
+        total = coef[:, step - 1 : step] * now + coef[:, step : step + 1] * value.astype(jnp.float32)
         if sums:
             total = jnp.concatenate(parts(start, lanes[2])) + jnp.concatenate(parts(sums, lanes[1])) + total
     if kind == "sum":
@@ -346,9 +345,9 @@
         outs[0][...] = jnp.sum(signs * total, axis=0, keepdims=True)
 
 
-def advance(step, width, kind, scalars, band, groups, lanes, outs):
+def advance(step, width, kind, scalars, coefs, band, groups, lanes, outs):
     tiles = lax.axis_size("xsec")
-    flat = [x for group in groups for x in group]
+    flat = coefs + [x for group in groups for x in group]
     rows, depth = band[1].shape
     return pl.pallas_call(
         functools.partial(
@@ -387,12 +386,15 @@
     out[rows:] = tail.astype(jnp.bfloat16)
 
 
-def finish_kernel(scale, me, keep, got, quad, *outs):
+def finish_kernel(count, scale, me, keep, got, quad, *refs):
+    rest, outs = (refs[:-count], refs[-count:])
     rows = keep.shape[1]
-    count = len(outs)
     share = rows // count
     tail = got[rows:].astype(jnp.float32)
-    total = (quad[...] + tail[0:1] + tail[1:2]) * scale
+    total = quad[...] + tail[0:1] + tail[1:2]
+    for term in rest:
+        total = total + term[...]
+    total = total * scale
     spare = jnp.zeros((outs[0].shape[0] - share - 1, total.shape[1]), jnp.float32)
     gram = (keep[0] + got[:rows].astype(jnp.float32)) * scale
     for i in range(count):
@@ -442,14 +444,13 @@
     assert halves == 2 and STEPS == 4
 
     everyone = range(xs)
+    coefs = coefs[None]
     assert rows % width == 0
 
     leaving = deal(current, me[None], others)
     coming = [from_tile(leaving[i - 1], i) for i in others]
-    fields = small(
-        functools.partial(stack_kernel, xs), [me[None]], [current, *coming],
-        [bf16(xs * rows, width)] * halves,
-    )
+    staying = deal(current, me[None], [0])
+    fields = small(stack_kernel, [], [*staying, *coming], [bf16(xs * rows, width)] * halves)
 
     blocks = blocks[:, 0]
     pattern = pattern[:, 0]
@@ -488,9 +489,10 @@
 
     def run(step, h, kind, older, sums, start, extra, lanes, outs):
         near, far = around(fields[h])
-        scalars = {"sum": [coefs], "sketch": [info, coefs], "probe": [coefs]}.get(kind, [])
+        scalars = [info] if kind == "sketch" else []
+        weights = [coefs] if kind in ("sum", "sketch", "probe") else []
         return advance(
-            step, width, kind, scalars, band,
+            step, width, kind, scalars, weights, band,
             ([fields[h]], [near], [far], older, sums, start, extra), lanes, outs,
         )
 
@@ -527,8 +529,9 @@
     terms = [quad]
     while 2 * hop < wires:
         got = swap_bits(send, hop)
-        terms = [sum(terms[1:], terms[0])]
-        terms.append(swap_bits(terms[0], hop))
+        if 4 * hop < wires:
+            terms = [sum(terms[1:], terms[0])]
+            terms.append(swap_bits(terms[0], hop))
         hop *= 2
         part = (wires // hop // 2, high, width)
         keep, send = small(
@@ -536,10 +539,11 @@
             [f32(*part), bf16(*part)],
         )
     quad, mixed = small(mix_kernel, [], [send, *terms], [f32(1, width), bf16(high + 16, width)])
+    rest = [swap_bits(quad, k * hop // 2) for k in (1, 3)] if wires > 2 else []
     mixed = swap_bits(mixed, hop)
     scale = 1.0 / float(rows * wires * tiles * xs) ** 0.5
     finished = small(
-        functools.partial(finish_kernel, scale), [me[None]], [keep, mixed, quad],
+        functools.partial(finish_kernel, xs, scale), [me[None]], [keep, mixed, quad, *rest],
         [f32(high // xs + 8, width)] * xs,
     )
     finished = [finished[0]] + [to_tile(finished[i], i) for i in others]
@@ -574,7 +578,7 @@
     lanes.append([[(len(arrays) + i, h * width) for h in range(halves)] for i in everyone])
     arrays += starts
     last, total = small(
-        functools.partial(last_kernel, *lanes), [me[None], coefs], arrays,
+        functools.partial(last_kernel, *lanes), [me[None]], [coefs] + arrays,
         [bf16(*shape), f32(*shape)],
     )
     return (last, before, total, gram, quadratic)

time: 88.5 us -> 88.7 us (level)
  starting transfers between devices: 40.9 us -> 44.4 us
  Pallas kernels: 18.8 us -> 16.1 us
  waiting for transfers between devices: 25.9 us -> 24.8 us
    ppermute x3 -> x4, starting transfers between devices: 2.35 us -> 5.51 us  [swap_bits(): lax.ppermute(x, 'wire', [(i, i ^ hop) for i in range(lax.axis_size('wire'...]
    pallas_call x8, Pallas kernels: 7.34 us -> 5.18 us  [advance(): pl.pallas_call(functools.partial(step_kernel, step, tiles, width, [len(gr...]
    ppermute x3 -> x4, waiting for transfers between devices: 5.25 us -> 3.19 us  [swap_bits(): lax.ppermute(x, 'wire', [(i, i ^ hop) for i in range(lax.axis_size('wire'...]
    ppermute x8, waiting for transfers between devices: 1.92 us -> 3 us  [around(): one = lax.ppermute(x, 'wire', first)]
    ppermute x11, starting transfers between devices: 14 us -> 14.9 us  [from_tile(): lax.ppermute(x, axis, [((i + offset) % size, i) for i in range(size)])]
    pallas_call x11 -> x12, Pallas kernels: 8.22 us -> 7.72 us  [small(): pl.pallas_call(kernel, out_shape=outs, in_specs=[SCALAR] * len(scalars) +...]
  transfers between devices with their start and end apart: 30 -> 31, of which waited for: 12 -> 15; matrix products, arithmetic and copies ran while one was open for 0% -> 0% of each run, Pallas kernels for 20% -> 17%
where the time goes in v5:
time: 88.7 us; the launch traced here: 88.5 us
  starting transfers between devices  44.4 us (50%)
  waiting for transfers between devices  24.8 us (28%)
  Pallas kernels  16.1 us (18%)
  local copies, waits for them, and re-layouts  2.26 us (3%)
    ppermute x8, starting transfers between devices, around(): two = lax.ppermute(x, 'wire', second)  17.3 us
    ppermute x11, starting transfers between devices, from_tile(): lax.ppermute(x, axis, [((i + offset) % size, i) for i in range(size)])  14.9 us
    ppermute x11, waiting for transfers between devices, from_tile(): lax.ppermute(x, axis, [((i + offset) % size, i) for i in range(size)])  10.3 us
    ppermute x8, waiting for transfers between devices, around(): two = lax.ppermute(x, 'wire', second)  8.3 us
    pallas_call x12, Pallas kernels, small(): pl.pallas_call(kernel, out_shape=outs, in_specs=[SCALAR] * len(scalars) +...  7.72 us
    ppermute x8, starting transfers between devices, around(): one = lax.ppermute(x, 'wire', first)  6.74 us
    ppermute x4, starting transfers between devices, swap_bits(): lax.ppermute(x, 'wire', [(i, i ^ hop) for i in range(lax.axis_size('wire'...  5.51 us
    pallas_call x8, Pallas kernels, advance(): pl.pallas_call(functools.partial(step_kernel, step, tiles, width, [len(gr...  5.18 us
  transfers between devices with their start and end apart: 31, of which 15 were waited for; matrix products, arithmetic and copies ran while one was open for 0% of the time, Pallas kernels for 17%

profile of v5, /device:TPU:0, one launch (start us, length us, event | category | flops | bytes accessed | tf_op | source)
XLA Modules:
  0.0 88.5 jit_solution(9583255683851721261)
XLA Ops:
  3.3 3.0 %collective-permute-start = (bf16[2,64,1152]{2,1,0:T(8,128)(2,1)S(1)}, bf16[2,64,1152]{2,1,0:T(8,128)(2,1)S(1)}, u32[]{:S(2)}, u32[]{:S(2)}) collective-permute-start(bf16[2,64,1152]{2,1,0:T(8,128)(2,1)S(1)} %shard_map.119), channel_id=1, source_target_pairs={{2,0},{0,2},{3,1},{1,3},{6,4},{4,6},{7,5},{5,7},{10,8},{8,10},{11,... | collective-permute-start | bytes 884744 | tf_op jit(solution)/shard_map/ppermute | solution.py:31
  6.4 7.0 %collective-permute-done.refs_0_ = bf16[2,64,1152]{2,1,0:T(8,128)(2,1)S(1)} collective-permute-done((bf16[2,64,1152]{2,1,0:T(8,128)(2,1)S(1)}, bf16[2,64,1152]{2,1,0:T(8,128)(2,1)S(1)}, u32[]{:S(2)}, u32[]{:S(2)}) %collective-permute-start) | collective-permute-done | bytes 294944 | tf_op jit(solution)/shard_map/ppermute | solution.py:31
  13.9 1.8 %collective-permute-start.2 = (bf16[256,256]{1,0:T(8,128)(2,1)S(1)}, bf16[256,256]{1,0:T(8,128)(2,1)S(1)}, u32[]{:S(2)}, u32[]{:S(2)}) collective-permute-start(bf16[256,256]{1,0:T(8,128)(2,1)S(1)} %shard_map.123), channel_id=1, source_target_pairs={{2,0},{0,2},{3,1},{1,3},{6,4},{4,6},{7,5},{5,7},{10,8},{8,10},{11,... | collective-permute-start | bytes 393224 | tf_op jit(solution)/shard_map/ppermute | solution.py:31
  17.4 2.9 %collective-permute-done.2.refs_1_ = bf16[256,256]{1,0:T(8,128)(2,1)S(1)} collective-permute-done((bf16[256,256]{1,0:T(8,128)(2,1)S(1)}, bf16[256,256]{1,0:T(8,128)(2,1)S(1)}, u32[]{:S(2)}, u32[]{:S(2)}) %collective-permute-start.2) | collective-permute-done | bytes 131104 | tf_op jit(solution)/shard_map/ppermute | solution.py:31
  20.3 1.9 %collective-permute-start.3 = (bf16[512,128]{1,0:T(8,128)(2,1)S(1)}, bf16[512,128]{1,0:T(8,128)(2,1)S(1)}, u32[]{:S(2)}, u32[]{:S(2)}) collective-permute-start(bf16[512,128]{1,0:T(8,128)(2,1)S(1)} %get-tuple-element.51.refs_3_.refs_7_), channel_id=1, source_target_pairs={{0,4},{4,0},{8,12},{12,8},{1,5},{5,1},{9,13},{13,9},{2,6},{6,2},{1... | collective-permute-start | bytes 393224 | tf_op jit(solution)/shard_map/ppermute | solution.py:45
  22.2 2.5 %collective-permute-start.4 = (bf16[512,128]{1,0:T(8,128)(2,1)S(1)}, bf16[512,128]{1,0:T(8,128)(2,1)S(1)}, u32[]{:S(2)}, u32[]{:S(2)}) collective-permute-start(bf16[512,128]{1,0:T(8,128)(2,1)S(1)} %get-tuple-element.51.refs_3_.refs_7_), channel_id=1, source_target_pairs={{4,8},{8,4},{12,0},{0,12},{5,9},{9,5},{13,1},{1,13},{6,10},{10,6},... | collective-permute-start | bytes 393224 | tf_op jit(solution)/shard_map/ppermute | solution.py:46
  28.7 3.3 %collective-permute-done.4.refs_5_ = bf16[512,128]{1,0:T(8,128)(2,1)S(1)} collective-permute-done((bf16[512,128]{1,0:T(8,128)(2,1)S(1)}, bf16[512,128]{1,0:T(8,128)(2,1)S(1)}, u32[]{:S(2)}, u32[]{:S(2)}) %collective-permute-start.4) | collective-permute-done | bytes 131104 | tf_op jit(solution)/shard_map/ppermute | solution.py:46
  32.7 3.5 %collective-permute-start.7 = (bf16[512,128]{1,0:T(8,128)(2,1)S(1)}, bf16[512,128]{1,0:T(8,128)(2,1)S(1)}, u32[]{:S(2)}, u32[]{:S(2)}) collective-permute-start(bf16[512,128]{1,0:T(8,128)(2,1)S(1)} %shard_map.126.refs_4_.refs_6_), channel_id=1, source_target_pairs={{4,8},{8,4},{12,0},{0,12},{5,9},{9,5},{13,1},{1,13},{6,10},{10,6},... | collective-permute-start | bytes 393224 | tf_op jit(solution)/shard_map/ppermute | solution.py:46
  38.2 3.2 %collective-permute-start.17 = (bf16[512,128]{1,0:T(8,128)(2,1)S(1)}, bf16[512,128]{1,0:T(8,128)(2,1)S(1)}, u32[]{:S(2)}, u32[]{:S(2)}) collective-permute-start(bf16[512,128]{1,0:T(8,128)(2,1)S(1)} %shard_map.132.refs_4_.refs_6_), channel_id=1, source_target_pairs={{4,8},{8,4},{12,0},{0,12},{5,9},{9,5},{13,1},{1,13},{6,10},{10,6},... | collective-permute-start | bytes 393224 | tf_op jit(solution)/shard_map/ppermute | solution.py:46
  41.6 1.6 %collective-permute-start.13 = (bf16[640,256]{1,0:T(8,128)(2,1)S(1)}, bf16[640,256]{1,0:T(8,128)(2,1)S(1)}, u32[]{:S(2)}, u32[]{:S(2)}) collective-permute-start(bf16[640,256]{1,0:T(8,128)(2,1)S(1)} %get-tuple-element.60), channel_id=1, source_target_pairs={{2,0},{0,2},{3,1},{1,3},{6,4},{4,6},{7,5},{5,7},{10,8},{8,10},{11,... | collective-permute-start | bytes 983048 | tf_op jit(solution)/shard_map/ppermute | solution.py:31
  45.3 1.6 %collective-permute-start.12 = (f32[256,256]{1,0:T(8,128)S(1)}, f32[256,256]{1,0:T(8,128)S(1)}, u32[]{:S(2)}, u32[]{:S(2)}) collective-permute-start(f32[256,256]{1,0:T(8,128)S(1)} %get-tuple-element.58.refs_11_), channel_id=1, source_target_pairs={{2,0},{0,2},{3,1},{1,3},{6,4},{4,6},{7,5},{5,7},{10,8},{8,10},{11,... | collective-permute-start | bytes 786440 | tf_op jit(solution)/shard_map/ppermute | solution.py:31
  46.8 2.8 %collective-permute-start.9 = (bf16[512,128]{1,0:T(8,128)(2,1)S(1)}, bf16[512,128]{1,0:T(8,128)(2,1)S(1)}, u32[]{:S(2)}, u32[]{:S(2)}) collective-permute-start(bf16[512,128]{1,0:T(8,128)(2,1)S(1)} %get-tuple-element.54.refs_3_.refs_8_), channel_id=1, source_target_pairs={{4,8},{8,4},{12,0},{0,12},{5,9},{9,5},{13,1},{1,13},{6,10},{10,6},... | collective-permute-start | bytes 393224 | tf_op jit(solution)/shard_map/ppermute | solution.py:46
  50.3 2.2 %collective-permute-done.8.refs_4_ = bf16[512,128]{1,0:T(8,128)(2,1)S(1)} collective-permute-done((bf16[512,128]{1,0:T(8,128)(2,1)S(1)}, bf16[512,128]{1,0:T(8,128)(2,1)S(1)}, u32[]{:S(2)}, u32[]{:S(2)}) %collective-permute-start.8) | collective-permute-done | bytes 131104 | tf_op jit(solution)/shard_map/ppermute | solution.py:45
  53.6 1.6 %collective-permute-done.9.refs_5_ = bf16[512,128]{1,0:T(8,128)(2,1)S(1)} collective-permute-done((bf16[512,128]{1,0:T(8,128)(2,1)S(1)}, bf16[512,128]{1,0:T(8,128)(2,1)S(1)}, u32[]{:S(2)}, u32[]{:S(2)}) %collective-permute-start.9) | collective-permute-done | bytes 131104 | tf_op jit(solution)/shard_map/ppermute | solution.py:46
  55.8 2.3 %collective-permute-start.10 = (bf16[512,128]{1,0:T(8,128)(2,1)S(1)}, bf16[512,128]{1,0:T(8,128)(2,1)S(1)}, u32[]{:S(2)}, u32[]{:S(2)}) collective-permute-start(bf16[512,128]{1,0:T(8,128)(2,1)S(1)} %shard_map.128.refs_5_.refs_7_.refs_4_.refs_0_), channel_id=1, source_target_pairs={{0,4},{4,0},{8,12},{12,8},{1,5},{5,1},{9,13},{13,9},{2,6},{6,2},{1... | collective-permute-start | bytes 393224 | tf_op jit(solution)/shard_map/ppermute | solution.py:45
  60.8 1.5 %collective-permute-start.25 = (f32[256,256]{1,0:T(8,128)S(1)}, f32[256,256]{1,0:T(8,128)S(1)}, u32[]{:S(2)}, u32[]{:S(2)}) collective-permute-start(f32[256,256]{1,0:T(8,128)S(1)} %get-tuple-element.66.refs_9_), channel_id=1, source_target_pairs={{2,0},{0,2},{3,1},{1,3},{6,4},{4,6},{7,5},{5,7},{10,8},{8,10},{11,... | collective-permute-start | bytes 786440 | tf_op jit(solution)/shard_map/ppermute | solution.py:31
  63.0 1.5 %collective-permute-start.20 = (bf16[512,128]{1,0:T(8,128)(2,1)S(1)}, bf16[512,128]{1,0:T(8,128)(2,1)S(1)}, u32[]{:S(2)}, u32[]{:S(2)}) collective-permute-start(bf16[512,128]{1,0:T(8,128)(2,1)S(1)} %get-tuple-element.64.refs_4_.refs_5_.refs_1_), channel_id=1, source_target_pairs={{0,4},{4,0},{8,12},{12,8},{1,5},{5,1},{9,13},{13,9},{2,6},{6,2},{1... | collective-permute-start | bytes 393224 | tf_op jit(solution)/shard_map/ppermute | solution.py:45
  64.5 1.9 %collective-permute-start.21 = (bf16[512,128]{1,0:T(8,128)(2,1)S(1)}, bf16[512,128]{1,0:T(8,128)(2,1)S(1)}, u32[]{:S(2)}, u32[]{:S(2)}) collective-permute-start(bf16[512,128]{1,0:T(8,128)(2,1)S(1)} %get-tuple-element.64.refs_4_.refs_5_.refs_1_), channel_id=1, source_target_pairs={{4,8},{8,4},{12,0},{0,12},{5,9},{9,5},{13,1},{1,13},{6,10},{10,6},... | collective-permute-start | bytes 393224 | tf_op jit(solution)/shard_map/ppermute | solution.py:46
  74.0 1.7 %collective-permute-start.28 = (f32[1,128]{1,0:T(1,128)S(1)}, f32[1,128]{1,0:T(1,128)S(1)}, u32[]{:S(2)}, u32[]{:S(2)}) collective-permute-start(f32[1,128]{1,0:T(1,128)S(1)} %get-tuple-element.80.quad), channel_id=1, source_target_pairs={{0,4},{4,0},{8,12},{12,8},{1,5},{5,1},{9,13},{13,9},{2,6},{6,2},{1... | collective-permute-start | bytes 1544 | tf_op jit(solution)/shard_map/ppermute | solution.py:51
  75.7 1.7 %collective-permute-start.29 = (f32[1,128]{1,0:T(1,128)S(1)}, f32[1,128]{1,0:T(1,128)S(1)}, u32[]{:S(2)}, u32[]{:S(2)}) collective-permute-start(f32[1,128]{1,0:T(1,128)S(1)} %get-tuple-element.80.quad), channel_id=1, source_target_pairs={{0,12},{4,8},{8,4},{12,0},{1,13},{5,9},{9,5},{13,1},{2,14},{6,10},... | collective-permute-start | bytes 1544 | tf_op jit(solution)/shard_map/ppermute | solution.py:51
  77.6 1.5 %collective-permute-start.23 = (bf16[256,128]{1,0:T(8,128)(2,1)S(1)}, bf16[256,128]{1,0:T(8,128)(2,1)S(1)}, u32[]{:S(2)}, u32[]{:S(2)}) collective-permute-start(bf16[256,128]{1,0:T(8,128)(2,1)S(1)} %get-tuple-element.70), channel_id=1, source_target_pairs={{2,0},{0,2},{3,1},{1,3},{6,4},{4,6},{7,5},{5,7},{10,8},{8,10},{11,... | collective-permute-start | bytes 196616 | tf_op jit(solution)/shard_map/ppermute | solution.py:31
  79.1 2.0 %collective-permute-done.29.refs_1_ = f32[1,128]{1,0:T(1,128)S(1)} collective-permute-done((f32[1,128]{1,0:T(1,128)S(1)}, f32[1,128]{1,0:T(1,128)S(1)}, u32[]{:S(2)}, u32[]{:S(2)}) %collective-permute-start.29) | collective-permute-done | bytes 544 | tf_op jit(solution)/shard_map/ppermute | solution.py:51
  83.2 1.7 %shard_map.137 = bf16[4,1,64,2,256]{4,3,2,1,0:T(2,128)(2,1)} custom-call(s32[1]{0:T(128)} %bitcast.me, bf16[512,128]{1,0:T(8,128)(2,1)S(1)} %shard_map.128.refs_5_.refs_7_.refs_4_.refs_0_, bf16[512,128]{1,0:T(8,128)(2,1)S(1)} %get-tuple-element.64.refs_4_.refs_5_.refs_1_, bf16[256,256]{1,0:T(8,128)(2,1)S(1)} %collective-permute-done.24.refs_6_.refs_2_), custom_call_target="tpu_custom_call" | custom-call | bytes 786432 | tf_op jit(solution)/shard_map/pallas_call | solution.py:423
  85.3 2.5 %shard_map.136 = (bf16[4,1,64,2,256]{4,3,2,1,0:T(2,128)(2,1)}, f32[4,1,64,2,256]{4,3,2,1,0:T(2,128)}) custom-call(s32[1]{0:T(128)} %bitcast.me, f32[1,4]{1,0:T(1,128)S(1)} %bitcast.16, bf16[256,128]{1,0:T(8,128)(2,1)S(1)} %get-tuple-element.61.refs_0_, bf16[256,128]{1,0:T(8,128)(2,1)S(1)} %get-tuple-element.68.refs_1_, ...), custom_call_target="tpu_custom_call" | custom-call | bytes 2359312 | tf_op jit(solution)/shard_map/pallas_call | solution.py:423
  (79 shorter events, 30.4 us)
Async XLA Ops:
  3.3 10.0 %collective-permute-start = (bf16[2,64,1152]{2,1,0:T(8,128)(2,1)S(1)}, bf16[2,64,1152]{2,1,0:T(8,128)(2,1)S(1)}, u32[]{:S(2)}, u32[]{:S(2)}) collective-permute-start(bf16[2,64,1152]{2,1,0:T(8,128)(2,1)S(1)} %shard_map.119), channel_id=1, source_target_pairs={{2,0},{0,2},{3,1},{1,3},{6,4},{4,6},{7,5},{5,7},{10,8},{8,10},{11,... | collective-permute-start | bytes 884744 | tf_op jit(solution)/shard_map/ppermute | solution.py:31
  13.4 12.0 %collective-permute-start.1 = (bf16[2,64,1152]{2,1,0:T(8,128)(2,1)S(1)}, bf16[2,64,1152]{2,1,0:T(8,128)(2,1)S(1)}, u32[]{:S(2)}, u32[]{:S(2)}) collective-permute-start(bf16[2,64,1152]{2,1,0:T(8,128)(2,1)S(1)} %collective-permute-done.refs_0_), channel_id=1, source_target_pairs={{1,0},{0,1},{3,2},{2,3},{5,4},{4,5},{7,6},{6,7},{9,8},{8,9},{11,10... | collective-permute-start | bytes 884744 | tf_op jit(solution)/shard_map/ppermute | solution.py:31
  16.5 12.2 %collective-permute-start.5 = (bf16[256,256]{1,0:T(8,128)(2,1)S(1)}, bf16[256,256]{1,0:T(8,128)(2,1)S(1)}, u32[]{:S(2)}, u32[]{:S(2)}) collective-permute-start(bf16[256,256]{1,0:T(8,128)(2,1)S(1)} %get-tuple-element.53), channel_id=1, source_target_pairs={{2,0},{0,2},{3,1},{1,3},{6,4},{4,6},{7,5},{5,7},{10,8},{8,10},{11,... | collective-permute-start | bytes 393224 | tf_op jit(solution)/shard_map/ppermute | solution.py:31
  20.3 8.5 %collective-permute-start.3 = (bf16[512,128]{1,0:T(8,128)(2,1)S(1)}, bf16[512,128]{1,0:T(8,128)(2,1)S(1)}, u32[]{:S(2)}, u32[]{:S(2)}) collective-permute-start(bf16[512,128]{1,0:T(8,128)(2,1)S(1)} %get-tuple-element.51.refs_3_.refs_7_), channel_id=1, source_target_pairs={{0,4},{4,0},{8,12},{12,8},{1,5},{5,1},{9,13},{13,9},{2,6},{6,2},{1... | collective-permute-start | bytes 393224 | tf_op jit(solution)/shard_map/ppermute | solution.py:45
  22.2 9.8 %collective-permute-start.4 = (bf16[512,128]{1,0:T(8,128)(2,1)S(1)}, bf16[512,128]{1,0:T(8,128)(2,1)S(1)}, u32[]{:S(2)}, u32[]{:S(2)}) collective-permute-start(bf16[512,128]{1,0:T(8,128)(2,1)S(1)} %get-tuple-element.51.refs_3_.refs_7_), channel_id=1, source_target_pairs={{4,8},{8,4},{12,0},{0,12},{5,9},{9,5},{13,1},{1,13},{6,10},{10,6},... | collective-permute-start | bytes 393224 | tf_op jit(solution)/shard_map/ppermute | solution.py:46
  24.7 11.5 %collective-permute-start.14 = (bf16[512,128]{1,0:T(8,128)(2,1)S(1)}, bf16[512,128]{1,0:T(8,128)(2,1)S(1)}, u32[]{:S(2)}, u32[]{:S(2)}) collective-permute-start(bf16[512,128]{1,0:T(8,128)(2,1)S(1)} %get-tuple-element.62.refs_3_.refs_7_), channel_id=1, source_target_pairs={{0,4},{4,0},{8,12},{12,8},{1,5},{5,1},{9,13},{13,9},{2,6},{6,2},{1... | collective-permute-start | bytes 393224 | tf_op jit(solution)/shard_map/ppermute | solution.py:45
  25.4 12.2 %collective-permute-start.15 = (bf16[512,128]{1,0:T(8,128)(2,1)S(1)}, bf16[512,128]{1,0:T(8,128)(2,1)S(1)}, u32[]{:S(2)}, u32[]{:S(2)}) collective-permute-start(bf16[512,128]{1,0:T(8,128)(2,1)S(1)} %get-tuple-element.62.refs_3_.refs_7_), channel_id=1, source_target_pairs={{4,8},{8,4},{12,0},{0,12},{5,9},{9,5},{13,1},{1,13},{6,10},{10,6},... | collective-permute-start | bytes 393224 | tf_op jit(solution)/shard_map/ppermute | solution.py:46
  32.6 10.6 %collective-permute-start.6 = (bf16[512,128]{1,0:T(8,128)(2,1)S(1)}, bf16[512,128]{1,0:T(8,128)(2,1)S(1)}, u32[]{:S(2)}, u32[]{:S(2)}) collective-permute-start(bf16[512,128]{1,0:T(8,128)(2,1)S(1)} %shard_map.126.refs_4_.refs_6_), channel_id=1, source_target_pairs={{0,4},{4,0},{8,12},{12,8},{1,5},{5,1},{9,13},{13,9},{2,6},{6,2},{1... | collective-permute-start | bytes 393224 | tf_op jit(solution)/shard_map/ppermute | solution.py:45
  32.7 10.7 %collective-permute-start.7 = (bf16[512,128]{1,0:T(8,128)(2,1)S(1)}, bf16[512,128]{1,0:T(8,128)(2,1)S(1)}, u32[]{:S(2)}, u32[]{:S(2)}) collective-permute-start(bf16[512,128]{1,0:T(8,128)(2,1)S(1)} %shard_map.126.refs_4_.refs_6_), channel_id=1, source_target_pairs={{4,8},{8,4},{12,0},{0,12},{5,9},{9,5},{13,1},{1,13},{6,10},{10,6},... | collective-permute-start | bytes 393224 | tf_op jit(solution)/shard_map/ppermute | solution.py:46
  38.2 8.7 %collective-permute-start.16 = (bf16[512,128]{1,0:T(8,128)(2,1)S(1)}, bf16[512,128]{1,0:T(8,128)(2,1)S(1)}, u32[]{:S(2)}, u32[]{:S(2)}) collective-permute-start(bf16[512,128]{1,0:T(8,128)(2,1)S(1)} %shard_map.132.refs_4_.refs_6_), channel_id=1, source_target_pairs={{0,4},{4,0},{8,12},{12,8},{1,5},{5,1},{9,13},{13,9},{2,6},{6,2},{1... | collective-permute-start | bytes 393224 | tf_op jit(solution)/shard_map/ppermute | solution.py:45
  38.2 11.4 %collective-permute-start.17 = (bf16[512,128]{1,0:T(8,128)(2,1)S(1)}, bf16[512,128]{1,0:T(8,128)(2,1)S(1)}, u32[]{:S(2)}, u32[]{:S(2)}) collective-permute-start(bf16[512,128]{1,0:T(8,128)(2,1)S(1)} %shard_map.132.refs_4_.refs_6_), channel_id=1, source_target_pairs={{4,8},{8,4},{12,0},{0,12},{5,9},{9,5},{13,1},{1,13},{6,10},{10,6},... | collective-permute-start | bytes 393224 | tf_op jit(solution)/shard_map/ppermute | solution.py:46
  41.6 22.9 %collective-permute-start.13 = (bf16[640,256]{1,0:T(8,128)(2,1)S(1)}, bf16[640,256]{1,0:T(8,128)(2,1)S(1)}, u32[]{:S(2)}, u32[]{:S(2)}) collective-permute-start(bf16[640,256]{1,0:T(8,128)(2,1)S(1)} %get-tuple-element.60), channel_id=1, source_target_pairs={{2,0},{0,2},{3,1},{1,3},{6,4},{4,6},{7,5},{5,7},{10,8},{8,10},{11,... | collective-permute-start | bytes 983048 | tf_op jit(solution)/shard_map/ppermute | solution.py:31
  44.0 8.5 %collective-permute-start.8 = (bf16[512,128]{1,0:T(8,128)(2,1)S(1)}, bf16[512,128]{1,0:T(8,128)(2,1)S(1)}, u32[]{:S(2)}, u32[]{:S(2)}) collective-permute-start(bf16[512,128]{1,0:T(8,128)(2,1)S(1)} %get-tuple-element.54.refs_3_.refs_8_), channel_id=1, source_target_pairs={{0,4},{4,0},{8,12},{12,8},{1,5},{5,1},{9,13},{13,9},{2,6},{6,2},{1... | collective-permute-start | bytes 393224 | tf_op jit(solution)/shard_map/ppermute | solution.py:45
  45.3 17.7 %collective-permute-start.12 = (f32[256,256]{1,0:T(8,128)S(1)}, f32[256,256]{1,0:T(8,128)S(1)}, u32[]{:S(2)}, u32[]{:S(2)}) collective-permute-start(f32[256,256]{1,0:T(8,128)S(1)} %get-tuple-element.58.refs_11_), channel_id=1, source_target_pairs={{2,0},{0,2},{3,1},{1,3},{6,4},{4,6},{7,5},{5,7},{10,8},{8,10},{11,... | collective-permute-start | bytes 786440 | tf_op jit(solution)/shard_map/ppermute | solution.py:31
  46.8 8.4 %collective-permute-start.9 = (bf16[512,128]{1,0:T(8,128)(2,1)S(1)}, bf16[512,128]{1,0:T(8,128)(2,1)S(1)}, u32[]{:S(2)}, u32[]{:S(2)}) collective-permute-start(bf16[512,128]{1,0:T(8,128)(2,1)S(1)} %get-tuple-element.54.refs_3_.refs_8_), channel_id=1, source_target_pairs={{4,8},{8,4},{12,0},{0,12},{5,9},{9,5},{13,1},{1,13},{6,10},{10,6},... | collective-permute-start | bytes 393224 | tf_op jit(solution)/shard_map/ppermute | solution.py:46
  50.2 8.6 %collective-permute-start.18 = (bf16[512,128]{1,0:T(8,128)(2,1)S(1)}, bf16[512,128]{1,0:T(8,128)(2,1)S(1)}, u32[]{:S(2)}, u32[]{:S(2)}) collective-permute-start(bf16[512,128]{1,0:T(8,128)(2,1)S(1)} %get-tuple-element.63.refs_3_.refs_7_), channel_id=1, source_target_pairs={{0,4},{4,0},{8,12},{12,8},{1,5},{5,1},{9,13},{13,9},{2,6},{6,2},{1... | collective-permute-start | bytes 393224 | tf_op jit(solution)/shard_map/ppermute | solution.py:45
  52.5 8.3 %collective-permute-start.19 = (bf16[512,128]{1,0:T(8,128)(2,1)S(1)}, bf16[512,128]{1,0:T(8,128)(2,1)S(1)}, u32[]{:S(2)}, u32[]{:S(2)}) collective-permute-start(bf16[512,128]{1,0:T(8,128)(2,1)S(1)} %get-tuple-element.63.refs_3_.refs_7_), channel_id=1, source_target_pairs={{4,8},{8,4},{12,0},{0,12},{5,9},{9,5},{13,1},{1,13},{6,10},{10,6},... | collective-permute-start | bytes 393224 | tf_op jit(solution)/shard_map/ppermute | solution.py:46
  55.8 10.7 %collective-permute-start.10 = (bf16[512,128]{1,0:T(8,128)(2,1)S(1)}, bf16[512,128]{1,0:T(8,128)(2,1)S(1)}, u32[]{:S(2)}, u32[]{:S(2)}) collective-permute-start(bf16[512,128]{1,0:T(8,128)(2,1)S(1)} %shard_map.128.refs_5_.refs_7_.refs_4_.refs_0_), channel_id=1, source_target_pairs={{0,4},{4,0},{8,12},{12,8},{1,5},{5,1},{9,13},{13,9},{2,6},{6,2},{1... | collective-permute-start | bytes 393224 | tf_op jit(solution)/shard_map/ppermute | solution.py:45
  58.8 8.2 %collective-permute-start.11 = (bf16[512,128]{1,0:T(8,128)(2,1)S(1)}, bf16[512,128]{1,0:T(8,128)(2,1)S(1)}, u32[]{:S(2)}, u32[]{:S(2)}) collective-permute-start(bf16[512,128]{1,0:T(8,128)(2,1)S(1)} %shard_map.128.refs_5_.refs_7_.refs_4_.refs_0_), channel_id=1, source_target_pairs={{4,8},{8,4},{12,0},{0,12},{5,9},{9,5},{13,1},{1,13},{6,10},{10,6},... | collective-permute-start | bytes 393224 | tf_op jit(solution)/shard_map/ppermute | solution.py:46
  60.8 24.1 %collective-permute-start.25 = (f32[256,256]{1,0:T(8,128)S(1)}, f32[256,256]{1,0:T(8,128)S(1)}, u32[]{:S(2)}, u32[]{:S(2)}) collective-permute-start(f32[256,256]{1,0:T(8,128)S(1)} %get-tuple-element.66.refs_9_), channel_id=1, source_target_pairs={{2,0},{0,2},{3,1},{1,3},{6,4},{4,6},{7,5},{5,7},{10,8},{8,10},{11,... | collective-permute-start | bytes 786440 | tf_op jit(solution)/shard_map/ppermute | solution.py:31
  63.0 7.7 %collective-permute-start.20 = (bf16[512,128]{1,0:T(8,128)(2,1)S(1)}, bf16[512,128]{1,0:T(8,128)(2,1)S(1)}, u32[]{:S(2)}, u32[]{:S(2)}) collective-permute-start(bf16[512,128]{1,0:T(8,128)(2,1)S(1)} %get-tuple-element.64.refs_4_.refs_5_.refs_1_), channel_id=1, source_target_pairs={{0,4},{4,0},{8,12},{12,8},{1,5},{5,1},{9,13},{13,9},{2,6},{6,2},{1... | collective-permute-start | bytes 393224 | tf_op jit(solution)/shard_map/ppermute | solution.py:45
  69.2 14.0 %collective-permute-start.24 = (bf16[256,256]{1,0:T(8,128)(2,1)S(1)}, bf16[256,256]{1,0:T(8,128)(2,1)S(1)}, u32[]{:S(2)}, u32[]{:S(2)}) collective-permute-start(bf16[256,256]{1,0:T(8,128)(2,1)S(1)} %get-tuple-element.71), channel_id=1, source_target_pairs={{2,0},{0,2},{3,1},{1,3},{6,4},{4,6},{7,5},{5,7},{10,8},{8,10},{11,... | collective-permute-start | bytes 393224 | tf_op jit(solution)/shard_map/ppermute | solution.py:31
  72.9 9.3 %collective-permute-start.27 = (bf16[144,128]{1,0:T(8,128)(2,1)S(1)}, bf16[144,128]{1,0:T(8,128)(2,1)S(1)}, u32[]{:S(2)}, u32[]{:S(2)}) collective-permute-start(bf16[144,128]{1,0:T(8,128)(2,1)S(1)} %get-tuple-element.79), channel_id=1, source_target_pairs={{0,8},{4,12},{8,0},{12,4},{1,9},{5,13},{9,1},{13,5},{2,10},{6,14},... | collective-permute-start | bytes 110600 | tf_op jit(solution)/shard_map/ppermute | solution.py:51
  77.6 7.3 %collective-permute-start.23 = (bf16[256,128]{1,0:T(8,128)(2,1)S(1)}, bf16[256,128]{1,0:T(8,128)(2,1)S(1)}, u32[]{:S(2)}, u32[]{:S(2)}) collective-permute-start(bf16[256,128]{1,0:T(8,128)(2,1)S(1)} %get-tuple-element.70), channel_id=1, source_target_pairs={{2,0},{0,2},{3,1},{1,3},{6,4},{4,6},{7,5},{5,7},{10,8},{8,10},{11,... | collective-permute-start | bytes 196616 | tf_op jit(solution)/shard_map/ppermute | solution.py:31
  (16 other events, 106.1 us)

commit v6 on v5

--- a/solution.py
+++ b/solution.py
@@ -111,11 +111,11 @@
             out[ranks:, j * width : (j + 1) * width] = picked[j * width : (j + 1) * width]
 
 
-def joined(me, refs, lanes, h, b, rows, width):
+def joined(me, refs, lanes, h, b, rows, width, start=0):
     value = None
     for i in range(len(lanes)):
         ref, lane = (refs[lanes[i][h][0]], lanes[i][h][1])
-        part = ref[:rows, lane : lane + width].astype(jnp.float32)
+        part = ref[pl.ds(start, rows), lane : lane + width]
         here = (me[0] - i + len(lanes)) % len(lanes) == b
         value = part if value is None else jnp.where(here, part, value)
     return value
@@ -125,29 +125,33 @@
     out = refs[-1]
     cells, _, orbs, halves, columns = out.shape
     width = columns // len(lanes)
-    for h in range(halves):
-        for b in range(len(lanes)):
-            value = joined(me, refs, lanes, h, b, cells * orbs, width).astype(out.dtype)
-            out[:, 0, :, h, b * width : (b + 1) * width] = value.reshape(cells, orbs, width)
+    for b in range(len(lanes)):
+        both = [
+            joined(me, refs, lanes, h, b, cells * orbs, width).reshape(cells, orbs, width)
+            for h in range(halves)
+        ]
+        out[:, 0, :, :, b * width : (b + 1) * width] = jnp.stack(both, axis=2)
 
 
 def last_kernel(late_lanes, mid_lanes, sum_lanes, start_lanes, me, coef, *refs):
     newest, summed = refs[-2:]
-    cells, _, orbs, halves, columns = newest.shape
+    _, _, orbs, halves, columns = newest.shape
     count = len(late_lanes)
     width = columns // count
-    for h in range(halves):
-        for b in range(count):
+    low = pl.multiple_of(pl.program_id(0) * orbs, orbs)
+    for b in range(count):
+        at = slice(b * width, (b + 1) * width)
+        lates = []
+        for h in range(halves):
             late, mid, total, start = [
-                joined(me, refs, lanes, h, b, cells * orbs, width)
+                joined(me, refs, lanes, h, b, orbs, width, low)
                 for lanes in (late_lanes, mid_lanes, sum_lanes, start_lanes)
             ]
-            at = slice(b * width, (b + 1) * width)
-            shape = (cells, orbs, width)
-            newest[:, 0, :, h, at] = late.astype(newest.dtype).reshape(shape)
+            lates.append(late)
+            late, mid = (late.astype(jnp.float32), mid.astype(jnp.float32))
             total = start + total + coef[:, STEPS - 2 : STEPS - 1] * mid
-            total = total + coef[:, STEPS - 1 : STEPS] * late
-            summed[:, 0, :, h, at] = total.reshape(shape)
+            summed[0, 0, :, h, at] = total + coef[:, STEPS - 1 : STEPS] * late
+        newest[0, 0, :, :, at] = jnp.stack(lates, axis=1)
 
 
 def pack_kernel(core, me, pattern, blocks, out):
@@ -577,10 +581,16 @@
         arrays += group
     lanes.append([[(len(arrays) + i, h * width) for h in range(halves)] for i in everyone])
     arrays += starts
-    last, total = small(
-        functools.partial(last_kernel, *lanes), [me[None]], [coefs] + arrays,
-        [bf16(*shape), f32(*shape)],
-    )
+    cell = pl.BlockSpec((1,) + shape[1:], lambda i: (i, 0, 0, 0, 0))
+    last, total = pl.pallas_call(
+        functools.partial(last_kernel, *lanes),
+        out_shape=[bf16(*shape), f32(*shape)],
+        grid=(cells,),
+        in_specs=[SCALAR] + [WHOLE] * (1 + len(arrays)),
+        out_specs=[cell, cell],
+        compiler_params=PARAMS,
+        cost_estimate=cost(16 * current.size),
+    )(me[None], coefs, *arrays)
     return (last, before, total, gram, quadratic)
 
 

time: 88.7 us -> 88.5 us (level)
  Pallas kernels: 16.1 us -> 15.2 us
    pallas_call x12 -> x11, Pallas kernels: 7.72 us -> 4.74 us  [small(): pl.pallas_call(kernel, out_shape=outs, in_specs=[SCALAR] * len(scalars) +...]
    pallas_call x0 -> x1, Pallas kernels: none -> 2.25 us  [program(): pl.pallas_call(functools.partial(last_kernel, *lanes), out_shape=[bf16(*s...]
  transfers between devices with their start and end apart: 31 -> 31, of which waited for: 15 -> 15; matrix products, arithmetic and copies ran while one was open for 0% -> 0% of each run, Pallas kernels for 17% -> 16%
where the time goes in v6:
time: 88.5 us; the launch traced here: 88.2 us
  starting transfers between devices  44.4 us (50%)
  waiting for transfers between devices  25.5 us (29%)
  Pallas kernels  15.2 us (17%)
  local copies, waits for them, and re-layouts  2.26 us (3%)
    ppermute x8, starting transfers between devices, around(): two = lax.ppermute(x, 'wire', second)  17.3 us
    ppermute x11, starting transfers between devices, from_tile(): lax.ppermute(x, axis, [((i + offset) % size, i) for i in range(size)])  14.9 us
    ppermute x11, waiting for transfers between devices, from_tile(): lax.ppermute(x, axis, [((i + offset) % size, i) for i in range(size)])  10.8 us
    ppermute x8, waiting for transfers between devices, around(): two = lax.ppermute(x, 'wire', second)  8.46 us
    ppermute x8, starting transfers between devices, around(): one = lax.ppermute(x, 'wire', first)  6.74 us
    ppermute x4, starting transfers between devices, swap_bits(): lax.ppermute(x, 'wire', [(i, i ^ hop) for i in range(lax.axis_size('wire'...  5.51 us
    pallas_call x8, Pallas kernels, advance(): pl.pallas_call(functools.partial(step_kernel, step, tiles, width, [len(gr...  5.18 us
    pallas_call x11, Pallas kernels, small(): pl.pallas_call(kernel, out_shape=outs, in_specs=[SCALAR] * len(scalars) +...  4.74 us
  transfers between devices with their start and end apart: 31, of which 15 were waited for; matrix products, arithmetic and copies ran while one was open for 0% of the time, Pallas kernels for 16%

profile of v6, /device:TPU:0, one launch (start us, length us, event | category | flops | bytes accessed | tf_op | source)
XLA Modules:
  0.0 88.2 jit_solution(1914452847797374200)
XLA Ops:
  3.3 3.0 %collective-permute-start = (bf16[2,64,1152]{2,1,0:T(8,128)(2,1)S(1)}, bf16[2,64,1152]{2,1,0:T(8,128)(2,1)S(1)}, u32[]{:S(2)}, u32[]{:S(2)}) collective-permute-start(bf16[2,64,1152]{2,1,0:T(8,128)(2,1)S(1)} %shard_map.119), channel_id=1, source_target_pairs={{2,0},{0,2},{3,1},{1,3},{6,4},{4,6},{7,5},{5,7},{10,8},{8,10},{11,... | collective-permute-start | bytes 884744 | tf_op jit(solution)/shard_map/ppermute | solution.py:31
  6.4 7.0 %collective-permute-done.refs_0_ = bf16[2,64,1152]{2,1,0:T(8,128)(2,1)S(1)} collective-permute-done((bf16[2,64,1152]{2,1,0:T(8,128)(2,1)S(1)}, bf16[2,64,1152]{2,1,0:T(8,128)(2,1)S(1)}, u32[]{:S(2)}, u32[]{:S(2)}) %collective-permute-start) | collective-permute-done | bytes 294944 | tf_op jit(solution)/shard_map/ppermute | solution.py:31
  13.9 1.8 %collective-permute-start.2 = (bf16[256,256]{1,0:T(8,128)(2,1)S(1)}, bf16[256,256]{1,0:T(8,128)(2,1)S(1)}, u32[]{:S(2)}, u32[]{:S(2)}) collective-permute-start(bf16[256,256]{1,0:T(8,128)(2,1)S(1)} %shard_map.123), channel_id=1, source_target_pairs={{2,0},{0,2},{3,1},{1,3},{6,4},{4,6},{7,5},{5,7},{10,8},{8,10},{11,... | collective-permute-start | bytes 393224 | tf_op jit(solution)/shard_map/ppermute | solution.py:31
  17.4 2.9 %collective-permute-done.2.refs_1_ = bf16[256,256]{1,0:T(8,128)(2,1)S(1)} collective-permute-done((bf16[256,256]{1,0:T(8,128)(2,1)S(1)}, bf16[256,256]{1,0:T(8,128)(2,1)S(1)}, u32[]{:S(2)}, u32[]{:S(2)}) %collective-permute-start.2) | collective-permute-done | bytes 131104 | tf_op jit(solution)/shard_map/ppermute | solution.py:31
  20.3 1.9 %collective-permute-start.3 = (bf16[512,128]{1,0:T(8,128)(2,1)S(1)}, bf16[512,128]{1,0:T(8,128)(2,1)S(1)}, u32[]{:S(2)}, u32[]{:S(2)}) collective-permute-start(bf16[512,128]{1,0:T(8,128)(2,1)S(1)} %get-tuple-element.51.refs_3_.refs_7_), channel_id=1, source_target_pairs={{0,4},{4,0},{8,12},{12,8},{1,5},{5,1},{9,13},{13,9},{2,6},{6,2},{1... | collective-permute-start | bytes 393224 | tf_op jit(solution)/shard_map/ppermute | solution.py:45
  22.2 2.5 %collective-permute-start.4 = (bf16[512,128]{1,0:T(8,128)(2,1)S(1)}, bf16[512,128]{1,0:T(8,128)(2,1)S(1)}, u32[]{:S(2)}, u32[]{:S(2)}) collective-permute-start(bf16[512,128]{1,0:T(8,128)(2,1)S(1)} %get-tuple-element.51.refs_3_.refs_7_), channel_id=1, source_target_pairs={{4,8},{8,4},{12,0},{0,12},{5,9},{9,5},{13,1},{1,13},{6,10},{10,6},... | collective-permute-start | bytes 393224 | tf_op jit(solution)/shard_map/ppermute | solution.py:46
  28.6 3.4 %collective-permute-done.4.refs_5_ = bf16[512,128]{1,0:T(8,128)(2,1)S(1)} collective-permute-done((bf16[512,128]{1,0:T(8,128)(2,1)S(1)}, bf16[512,128]{1,0:T(8,128)(2,1)S(1)}, u32[]{:S(2)}, u32[]{:S(2)}) %collective-permute-start.4) | collective-permute-done | bytes 131104 | tf_op jit(solution)/shard_map/ppermute | solution.py:46
  32.7 3.5 %collective-permute-start.7 = (bf16[512,128]{1,0:T(8,128)(2,1)S(1)}, bf16[512,128]{1,0:T(8,128)(2,1)S(1)}, u32[]{:S(2)}, u32[]{:S(2)}) collective-permute-start(bf16[512,128]{1,0:T(8,128)(2,1)S(1)} %shard_map.126.refs_4_.refs_6_), channel_id=1, source_target_pairs={{4,8},{8,4},{12,0},{0,12},{5,9},{9,5},{13,1},{1,13},{6,10},{10,6},... | collective-permute-start | bytes 393224 | tf_op jit(solution)/shard_map/ppermute | solution.py:46
  38.2 3.2 %collective-permute-start.17 = (bf16[512,128]{1,0:T(8,128)(2,1)S(1)}, bf16[512,128]{1,0:T(8,128)(2,1)S(1)}, u32[]{:S(2)}, u32[]{:S(2)}) collective-permute-start(bf16[512,128]{1,0:T(8,128)(2,1)S(1)} %shard_map.132.refs_4_.refs_6_), channel_id=1, source_target_pairs={{4,8},{8,4},{12,0},{0,12},{5,9},{9,5},{13,1},{1,13},{6,10},{10,6},... | collective-permute-start | bytes 393224 | tf_op jit(solution)/shard_map/ppermute | solution.py:46
  41.6 1.6 %collective-permute-start.13 = (bf16[640,256]{1,0:T(8,128)(2,1)S(1)}, bf16[640,256]{1,0:T(8,128)(2,1)S(1)}, u32[]{:S(2)}, u32[]{:S(2)}) collective-permute-start(bf16[640,256]{1,0:T(8,128)(2,1)S(1)} %get-tuple-element.60), channel_id=1, source_target_pairs={{2,0},{0,2},{3,1},{1,3},{6,4},{4,6},{7,5},{5,7},{10,8},{8,10},{11,... | collective-permute-start | bytes 983048 | tf_op jit(solution)/shard_map/ppermute | solution.py:31
  45.3 1.6 %collective-permute-start.12 = (f32[256,256]{1,0:T(8,128)S(1)}, f32[256,256]{1,0:T(8,128)S(1)}, u32[]{:S(2)}, u32[]{:S(2)}) collective-permute-start(f32[256,256]{1,0:T(8,128)S(1)} %get-tuple-element.58.refs_11_), channel_id=1, source_target_pairs={{2,0},{0,2},{3,1},{1,3},{6,4},{4,6},{7,5},{5,7},{10,8},{8,10},{11,... | collective-permute-start | bytes 786440 | tf_op jit(solution)/shard_map/ppermute | solution.py:31
  46.8 2.8 %collective-permute-start.9 = (bf16[512,128]{1,0:T(8,128)(2,1)S(1)}, bf16[512,128]{1,0:T(8,128)(2,1)S(1)}, u32[]{:S(2)}, u32[]{:S(2)}) collective-permute-start(bf16[512,128]{1,0:T(8,128)(2,1)S(1)} %get-tuple-element.54.refs_3_.refs_8_), channel_id=1, source_target_pairs={{4,8},{8,4},{12,0},{0,12},{5,9},{9,5},{13,1},{1,13},{6,10},{10,6},... | collective-permute-start | bytes 393224 | tf_op jit(solution)/shard_map/ppermute | solution.py:46
  50.3 2.3 %collective-permute-done.8.refs_4_ = bf16[512,128]{1,0:T(8,128)(2,1)S(1)} collective-permute-done((bf16[512,128]{1,0:T(8,128)(2,1)S(1)}, bf16[512,128]{1,0:T(8,128)(2,1)S(1)}, u32[]{:S(2)}, u32[]{:S(2)}) %collective-permute-start.8) | collective-permute-done | bytes 131104 | tf_op jit(solution)/shard_map/ppermute | solution.py:45
  53.6 1.6 %collective-permute-done.9.refs_5_ = bf16[512,128]{1,0:T(8,128)(2,1)S(1)} collective-permute-done((bf16[512,128]{1,0:T(8,128)(2,1)S(1)}, bf16[512,128]{1,0:T(8,128)(2,1)S(1)}, u32[]{:S(2)}, u32[]{:S(2)}) %collective-permute-start.9) | collective-permute-done | bytes 131104 | tf_op jit(solution)/shard_map/ppermute | solution.py:46
  55.8 2.3 %collective-permute-start.10 = (bf16[512,128]{1,0:T(8,128)(2,1)S(1)}, bf16[512,128]{1,0:T(8,128)(2,1)S(1)}, u32[]{:S(2)}, u32[]{:S(2)}) collective-permute-start(bf16[512,128]{1,0:T(8,128)(2,1)S(1)} %shard_map.128.refs_5_.refs_7_.refs_4_.refs_0_), channel_id=1, source_target_pairs={{0,4},{4,0},{8,12},{12,8},{1,5},{5,1},{9,13},{13,9},{2,6},{6,2},{1... | collective-permute-start | bytes 393224 | tf_op jit(solution)/shard_map/ppermute | solution.py:45
  58.8 1.5 %collective-permute-start.11 = (bf16[512,128]{1,0:T(8,128)(2,1)S(1)}, bf16[512,128]{1,0:T(8,128)(2,1)S(1)}, u32[]{:S(2)}, u32[]{:S(2)}) collective-permute-start(bf16[512,128]{1,0:T(8,128)(2,1)S(1)} %shard_map.128.refs_5_.refs_7_.refs_4_.refs_0_), channel_id=1, source_target_pairs={{4,8},{8,4},{12,0},{0,12},{5,9},{9,5},{13,1},{1,13},{6,10},{10,6},... | collective-permute-start | bytes 393224 | tf_op jit(solution)/shard_map/ppermute | solution.py:46
  60.9 1.5 %collective-permute-start.25 = (f32[256,256]{1,0:T(8,128)S(1)}, f32[256,256]{1,0:T(8,128)S(1)}, u32[]{:S(2)}, u32[]{:S(2)}) collective-permute-start(f32[256,256]{1,0:T(8,128)S(1)} %get-tuple-element.66.refs_9_), channel_id=1, source_target_pairs={{2,0},{0,2},{3,1},{1,3},{6,4},{4,6},{7,5},{5,7},{10,8},{8,10},{11,... | collective-permute-start | bytes 786440 | tf_op jit(solution)/shard_map/ppermute | solution.py:31
  63.0 1.5 %collective-permute-start.20 = (bf16[512,128]{1,0:T(8,128)(2,1)S(1)}, bf16[512,128]{1,0:T(8,128)(2,1)S(1)}, u32[]{:S(2)}, u32[]{:S(2)}) collective-permute-start(bf16[512,128]{1,0:T(8,128)(2,1)S(1)} %get-tuple-element.64.refs_4_.refs_5_.refs_1_), channel_id=1, source_target_pairs={{0,4},{4,0},{8,12},{12,8},{1,5},{5,1},{9,13},{13,9},{2,6},{6,2},{1... | collective-permute-start | bytes 393224 | tf_op jit(solution)/shard_map/ppermute | solution.py:45
  64.5 1.9 %collective-permute-start.21 = (bf16[512,128]{1,0:T(8,128)(2,1)S(1)}, bf16[512,128]{1,0:T(8,128)(2,1)S(1)}, u32[]{:S(2)}, u32[]{:S(2)}) collective-permute-start(bf16[512,128]{1,0:T(8,128)(2,1)S(1)} %get-tuple-element.64.refs_4_.refs_5_.refs_1_), channel_id=1, source_target_pairs={{4,8},{8,4},{12,0},{0,12},{5,9},{9,5},{13,1},{1,13},{6,10},{10,6},... | collective-permute-start | bytes 393224 | tf_op jit(solution)/shard_map/ppermute | solution.py:46
  74.0 1.7 %collective-permute-start.28 = (f32[1,128]{1,0:T(1,128)S(1)}, f32[1,128]{1,0:T(1,128)S(1)}, u32[]{:S(2)}, u32[]{:S(2)}) collective-permute-start(f32[1,128]{1,0:T(1,128)S(1)} %get-tuple-element.80.quad), channel_id=1, source_target_pairs={{0,4},{4,0},{8,12},{12,8},{1,5},{5,1},{9,13},{13,9},{2,6},{6,2},{1... | collective-permute-start | bytes 1544 | tf_op jit(solution)/shard_map/ppermute | solution.py:51
  75.7 1.7 %collective-permute-start.29 = (f32[1,128]{1,0:T(1,128)S(1)}, f32[1,128]{1,0:T(1,128)S(1)}, u32[]{:S(2)}, u32[]{:S(2)}) collective-permute-start(f32[1,128]{1,0:T(1,128)S(1)} %get-tuple-element.80.quad), channel_id=1, source_target_pairs={{0,12},{4,8},{8,4},{12,0},{1,13},{5,9},{9,5},{13,1},{2,14},{6,10},... | collective-permute-start | bytes 1544 | tf_op jit(solution)/shard_map/ppermute | solution.py:51
  77.6 1.5 %collective-permute-start.23 = (bf16[256,128]{1,0:T(8,128)(2,1)S(1)}, bf16[256,128]{1,0:T(8,128)(2,1)S(1)}, u32[]{:S(2)}, u32[]{:S(2)}) collective-permute-start(bf16[256,128]{1,0:T(8,128)(2,1)S(1)} %get-tuple-element.70), channel_id=1, source_target_pairs={{2,0},{0,2},{3,1},{1,3},{6,4},{4,6},{7,5},{5,7},{10,8},{8,10},{11,... | collective-permute-start | bytes 196616 | tf_op jit(solution)/shard_map/ppermute | solution.py:31
  79.1 2.0 %collective-permute-done.29.refs_1_ = f32[1,128]{1,0:T(1,128)S(1)} collective-permute-done((f32[1,128]{1,0:T(1,128)S(1)}, f32[1,128]{1,0:T(1,128)S(1)}, u32[]{:S(2)}, u32[]{:S(2)}) %collective-permute-start.29) | collective-permute-done | bytes 544 | tf_op jit(solution)/shard_map/ppermute | solution.py:51
  85.3 2.3 %shard_map.136 = (bf16[4,1,64,2,256]{4,3,2,1,0:T(2,128)(2,1)}, f32[4,1,64,2,256]{4,3,2,1,0:T(2,128)}) custom-call(s32[1]{0:T(128)} %bitcast.me, f32[1,4]{1,0:T(1,128)S(1)} %bitcast.16, bf16[256,128]{1,0:T(8,128)(2,1)S(1)} %get-tuple-element.61.refs_0_, bf16[256,128]{1,0:T(8,128)(2,1)S(1)} %get-tuple-element.68.refs_1_, ...), custom_call_target="tpu_custom_call" | custom-call | bytes 2097152 | tf_op jit(solution)/shard_map/pallas_call | solution.py:585
  (79 shorter events, 30.5 us)
Async XLA Ops:
  3.3 10.0 %collective-permute-start = (bf16[2,64,1152]{2,1,0:T(8,128)(2,1)S(1)}, bf16[2,64,1152]{2,1,0:T(8,128)(2,1)S(1)}, u32[]{:S(2)}, u32[]{:S(2)}) collective-permute-start(bf16[2,64,1152]{2,1,0:T(8,128)(2,1)S(1)} %shard_map.119), channel_id=1, source_target_pairs={{2,0},{0,2},{3,1},{1,3},{6,4},{4,6},{7,5},{5,7},{10,8},{8,10},{11,... | collective-permute-start | bytes 884744 | tf_op jit(solution)/shard_map/ppermute | solution.py:31
  13.4 12.0 %collective-permute-start.1 = (bf16[2,64,1152]{2,1,0:T(8,128)(2,1)S(1)}, bf16[2,64,1152]{2,1,0:T(8,128)(2,1)S(1)}, u32[]{:S(2)}, u32[]{:S(2)}) collective-permute-start(bf16[2,64,1152]{2,1,0:T(8,128)(2,1)S(1)} %collective-permute-done.refs_0_), channel_id=1, source_target_pairs={{1,0},{0,1},{3,2},{2,3},{5,4},{4,5},{7,6},{6,7},{9,8},{8,9},{11,10... | collective-permute-start | bytes 884744 | tf_op jit(solution)/shard_map/ppermute | solution.py:31
  16.5 12.0 %collective-permute-start.5 = (bf16[256,256]{1,0:T(8,128)(2,1)S(1)}, bf16[256,256]{1,0:T(8,128)(2,1)S(1)}, u32[]{:S(2)}, u32[]{:S(2)}) collective-permute-start(bf16[256,256]{1,0:T(8,128)(2,1)S(1)} %get-tuple-element.53), channel_id=1, source_target_pairs={{2,0},{0,2},{3,1},{1,3},{6,4},{4,6},{7,5},{5,7},{10,8},{8,10},{11,... | collective-permute-start | bytes 393224 | tf_op jit(solution)/shard_map/ppermute | solution.py:31
  20.3 8.3 %collective-permute-start.3 = (bf16[512,128]{1,0:T(8,128)(2,1)S(1)}, bf16[512,128]{1,0:T(8,128)(2,1)S(1)}, u32[]{:S(2)}, u32[]{:S(2)}) collective-permute-start(bf16[512,128]{1,0:T(8,128)(2,1)S(1)} %get-tuple-element.51.refs_3_.refs_7_), channel_id=1, source_target_pairs={{0,4},{4,0},{8,12},{12,8},{1,5},{5,1},{9,13},{13,9},{2,6},{6,2},{1... | collective-permute-start | bytes 393224 | tf_op jit(solution)/shard_map/ppermute | solution.py:45
  22.2 9.8 %collective-permute-start.4 = (bf16[512,128]{1,0:T(8,128)(2,1)S(1)}, bf16[512,128]{1,0:T(8,128)(2,1)S(1)}, u32[]{:S(2)}, u32[]{:S(2)}) collective-permute-start(bf16[512,128]{1,0:T(8,128)(2,1)S(1)} %get-tuple-element.51.refs_3_.refs_7_), channel_id=1, source_target_pairs={{4,8},{8,4},{12,0},{0,12},{5,9},{9,5},{13,1},{1,13},{6,10},{10,6},... | collective-permute-start | bytes 393224 | tf_op jit(solution)/shard_map/ppermute | solution.py:46
  24.7 11.5 %collective-permute-start.14 = (bf16[512,128]{1,0:T(8,128)(2,1)S(1)}, bf16[512,128]{1,0:T(8,128)(2,1)S(1)}, u32[]{:S(2)}, u32[]{:S(2)}) collective-permute-start(bf16[512,128]{1,0:T(8,128)(2,1)S(1)} %get-tuple-element.62.refs_3_.refs_7_), channel_id=1, source_target_pairs={{0,4},{4,0},{8,12},{12,8},{1,5},{5,1},{9,13},{13,9},{2,6},{6,2},{1... | collective-permute-start | bytes 393224 | tf_op jit(solution)/shard_map/ppermute | solution.py:45
  25.4 12.2 %collective-permute-start.15 = (bf16[512,128]{1,0:T(8,128)(2,1)S(1)}, bf16[512,128]{1,0:T(8,128)(2,1)S(1)}, u32[]{:S(2)}, u32[]{:S(2)}) collective-permute-start(bf16[512,128]{1,0:T(8,128)(2,1)S(1)} %get-tuple-element.62.refs_3_.refs_7_), channel_id=1, source_target_pairs={{4,8},{8,4},{12,0},{0,12},{5,9},{9,5},{13,1},{1,13},{6,10},{10,6},... | collective-permute-start | bytes 393224 | tf_op jit(solution)/shard_map/ppermute | solution.py:46
  32.6 10.6 %collective-permute-start.6 = (bf16[512,128]{1,0:T(8,128)(2,1)S(1)}, bf16[512,128]{1,0:T(8,128)(2,1)S(1)}, u32[]{:S(2)}, u32[]{:S(2)}) collective-permute-start(bf16[512,128]{1,0:T(8,128)(2,1)S(1)} %shard_map.126.refs_4_.refs_6_), channel_id=1, source_target_pairs={{0,4},{4,0},{8,12},{12,8},{1,5},{5,1},{9,13},{13,9},{2,6},{6,2},{1... | collective-permute-start | bytes 393224 | tf_op jit(solution)/shard_map/ppermute | solution.py:45
  32.7 10.7 %collective-permute-start.7 = (bf16[512,128]{1,0:T(8,128)(2,1)S(1)}, bf16[512,128]{1,0:T(8,128)(2,1)S(1)}, u32[]{:S(2)}, u32[]{:S(2)}) collective-permute-start(bf16[512,128]{1,0:T(8,128)(2,1)S(1)} %shard_map.126.refs_4_.refs_6_), channel_id=1, source_target_pairs={{4,8},{8,4},{12,0},{0,12},{5,9},{9,5},{13,1},{1,13},{6,10},{10,6},... | collective-permute-start | bytes 393224 | tf_op jit(solution)/shard_map/ppermute | solution.py:46
  38.2 8.7 %collective-permute-start.16 = (bf16[512,128]{1,0:T(8,128)(2,1)S(1)}, bf16[512,128]{1,0:T(8,128)(2,1)S(1)}, u32[]{:S(2)}, u32[]{:S(2)}) collective-permute-start(bf16[512,128]{1,0:T(8,128)(2,1)S(1)} %shard_map.132.refs_4_.refs_6_), channel_id=1, source_target_pairs={{0,4},{4,0},{8,12},{12,8},{1,5},{5,1},{9,13},{13,9},{2,6},{6,2},{1... | collective-permute-start | bytes 393224 | tf_op jit(solution)/shard_map/ppermute | solution.py:45
  38.2 11.4 %collective-permute-start.17 = (bf16[512,128]{1,0:T(8,128)(2,1)S(1)}, bf16[512,128]{1,0:T(8,128)(2,1)S(1)}, u32[]{:S(2)}, u32[]{:S(2)}) collective-permute-start(bf16[512,128]{1,0:T(8,128)(2,1)S(1)} %shard_map.132.refs_4_.refs_6_), channel_id=1, source_target_pairs={{4,8},{8,4},{12,0},{0,12},{5,9},{9,5},{13,1},{1,13},{6,10},{10,6},... | collective-permute-start | bytes 393224 | tf_op jit(solution)/shard_map/ppermute | solution.py:46
  41.6 22.9 %collective-permute-start.13 = (bf16[640,256]{1,0:T(8,128)(2,1)S(1)}, bf16[640,256]{1,0:T(8,128)(2,1)S(1)}, u32[]{:S(2)}, u32[]{:S(2)}) collective-permute-start(bf16[640,256]{1,0:T(8,128)(2,1)S(1)} %get-tuple-element.60), channel_id=1, source_target_pairs={{2,0},{0,2},{3,1},{1,3},{6,4},{4,6},{7,5},{5,7},{10,8},{8,10},{11,... | collective-permute-start | bytes 983048 | tf_op jit(solution)/shard_map/ppermute | solution.py:31
  44.0 8.5 %collective-permute-start.8 = (bf16[512,128]{1,0:T(8,128)(2,1)S(1)}, bf16[512,128]{1,0:T(8,128)(2,1)S(1)}, u32[]{:S(2)}, u32[]{:S(2)}) collective-permute-start(bf16[512,128]{1,0:T(8,128)(2,1)S(1)} %get-tuple-element.54.refs_3_.refs_8_), channel_id=1, source_target_pairs={{0,4},{4,0},{8,12},{12,8},{1,5},{5,1},{9,13},{13,9},{2,6},{6,2},{1... | collective-permute-start | bytes 393224 | tf_op jit(solution)/shard_map/ppermute | solution.py:45
  45.3 17.7 %collective-permute-start.12 = (f32[256,256]{1,0:T(8,128)S(1)}, f32[256,256]{1,0:T(8,128)S(1)}, u32[]{:S(2)}, u32[]{:S(2)}) collective-permute-start(f32[256,256]{1,0:T(8,128)S(1)} %get-tuple-element.58.refs_11_), channel_id=1, source_target_pairs={{2,0},{0,2},{3,1},{1,3},{6,4},{4,6},{7,5},{5,7},{10,8},{8,10},{11,... | collective-permute-start | bytes 786440 | tf_op jit(solution)/shard_map/ppermute | solution.py:31
  46.8 8.4 %collective-permute-start.9 = (bf16[512,128]{1,0:T(8,128)(2,1)S(1)}, bf16[512,128]{1,0:T(8,128)(2,1)S(1)}, u32[]{:S(2)}, u32[]{:S(2)}) collective-permute-start(bf16[512,128]{1,0:T(8,128)(2,1)S(1)} %get-tuple-element.54.refs_3_.refs_8_), channel_id=1, source_target_pairs={{4,8},{8,4},{12,0},{0,12},{5,9},{9,5},{13,1},{1,13},{6,10},{10,6},... | collective-permute-start | bytes 393224 | tf_op jit(solution)/shard_map/ppermute | solution.py:46
  50.2 8.6 %collective-permute-start.18 = (bf16[512,128]{1,0:T(8,128)(2,1)S(1)}, bf16[512,128]{1,0:T(8,128)(2,1)S(1)}, u32[]{:S(2)}, u32[]{:S(2)}) collective-permute-start(bf16[512,128]{1,0:T(8,128)(2,1)S(1)} %get-tuple-element.63.refs_3_.refs_7_), channel_id=1, source_target_pairs={{0,4},{4,0},{8,12},{12,8},{1,5},{5,1},{9,13},{13,9},{2,6},{6,2},{1... | collective-permute-start | bytes 393224 | tf_op jit(solution)/shard_map/ppermute | solution.py:45
  52.5 8.3 %collective-permute-start.19 = (bf16[512,128]{1,0:T(8,128)(2,1)S(1)}, bf16[512,128]{1,0:T(8,128)(2,1)S(1)}, u32[]{:S(2)}, u32[]{:S(2)}) collective-permute-start(bf16[512,128]{1,0:T(8,128)(2,1)S(1)} %get-tuple-element.63.refs_3_.refs_7_), channel_id=1, source_target_pairs={{4,8},{8,4},{12,0},{0,12},{5,9},{9,5},{13,1},{1,13},{6,10},{10,6},... | collective-permute-start | bytes 393224 | tf_op jit(solution)/shard_map/ppermute | solution.py:46
  55.8 10.7 %collective-permute-start.10 = (bf16[512,128]{1,0:T(8,128)(2,1)S(1)}, bf16[512,128]{1,0:T(8,128)(2,1)S(1)}, u32[]{:S(2)}, u32[]{:S(2)}) collective-permute-start(bf16[512,128]{1,0:T(8,128)(2,1)S(1)} %shard_map.128.refs_5_.refs_7_.refs_4_.refs_0_), channel_id=1, source_target_pairs={{0,4},{4,0},{8,12},{12,8},{1,5},{5,1},{9,13},{13,9},{2,6},{6,2},{1... | collective-permute-start | bytes 393224 | tf_op jit(solution)/shard_map/ppermute | solution.py:45
  58.8 8.2 %collective-permute-start.11 = (bf16[512,128]{1,0:T(8,128)(2,1)S(1)}, bf16[512,128]{1,0:T(8,128)(2,1)S(1)}, u32[]{:S(2)}, u32[]{:S(2)}) collective-permute-start(bf16[512,128]{1,0:T(8,128)(2,1)S(1)} %shard_map.128.refs_5_.refs_7_.refs_4_.refs_0_), channel_id=1, source_target_pairs={{4,8},{8,4},{12,0},{0,12},{5,9},{9,5},{13,1},{1,13},{6,10},{10,6},... | collective-permute-start | bytes 393224 | tf_op jit(solution)/shard_map/ppermute | solution.py:46
  60.9 23.6 %collective-permute-start.25 = (f32[256,256]{1,0:T(8,128)S(1)}, f32[256,256]{1,0:T(8,128)S(1)}, u32[]{:S(2)}, u32[]{:S(2)}) collective-permute-start(f32[256,256]{1,0:T(8,128)S(1)} %get-tuple-element.66.refs_9_), channel_id=1, source_target_pairs={{2,0},{0,2},{3,1},{1,3},{6,4},{4,6},{7,5},{5,7},{10,8},{8,10},{11,... | collective-permute-start | bytes 786440 | tf_op jit(solution)/shard_map/ppermute | solution.py:31
  63.0 7.7 %collective-permute-start.20 = (bf16[512,128]{1,0:T(8,128)(2,1)S(1)}, bf16[512,128]{1,0:T(8,128)(2,1)S(1)}, u32[]{:S(2)}, u32[]{:S(2)}) collective-permute-start(bf16[512,128]{1,0:T(8,128)(2,1)S(1)} %get-tuple-element.64.refs_4_.refs_5_.refs_1_), channel_id=1, source_target_pairs={{0,4},{4,0},{8,12},{12,8},{1,5},{5,1},{9,13},{13,9},{2,6},{6,2},{1... | collective-permute-start | bytes 393224 | tf_op jit(solution)/shard_map/ppermute | solution.py:45
  69.2 14.0 %collective-permute-start.24 = (bf16[256,256]{1,0:T(8,128)(2,1)S(1)}, bf16[256,256]{1,0:T(8,128)(2,1)S(1)}, u32[]{:S(2)}, u32[]{:S(2)}) collective-permute-start(bf16[256,256]{1,0:T(8,128)(2,1)S(1)} %get-tuple-element.71), channel_id=1, source_target_pairs={{2,0},{0,2},{3,1},{1,3},{6,4},{4,6},{7,5},{5,7},{10,8},{8,10},{11,... | collective-permute-start | bytes 393224 | tf_op jit(solution)/shard_map/ppermute | solution.py:31
  72.9 9.3 %collective-permute-start.27 = (bf16[144,128]{1,0:T(8,128)(2,1)S(1)}, bf16[144,128]{1,0:T(8,128)(2,1)S(1)}, u32[]{:S(2)}, u32[]{:S(2)}) collective-permute-start(bf16[144,128]{1,0:T(8,128)(2,1)S(1)} %get-tuple-element.79), channel_id=1, source_target_pairs={{0,8},{4,12},{8,0},{12,4},{1,9},{5,13},{9,1},{13,5},{2,10},{6,14},... | collective-permute-start | bytes 110600 | tf_op jit(solution)/shard_map/ppermute | solution.py:51
  77.6 6.8 %collective-permute-start.23 = (bf16[256,128]{1,0:T(8,128)(2,1)S(1)}, bf16[256,128]{1,0:T(8,128)(2,1)S(1)}, u32[]{:S(2)}, u32[]{:S(2)}) collective-permute-start(bf16[256,128]{1,0:T(8,128)(2,1)S(1)} %get-tuple-element.70), channel_id=1, source_target_pairs={{2,0},{0,2},{3,1},{1,3},{6,4},{4,6},{7,5},{5,7},{10,8},{8,10},{11,... | collective-permute-start | bytes 196616 | tf_op jit(solution)/shard_map/ppermute | solution.py:31
  (16 other events, 105.9 us)
